TPU v7x, 256 devices: a whole 4x4x8 slice. The times are simulated.
256 devices in a mesh: row: 64 (over y, z, core), col: 4 (over x).
Axes of the slice: x: 4, y: 4, z: 8, core: 2. Of those that a mesh axis runs over, the one named last changes fastest.
Arguments:
- leaf_grad: bfloat16 [256, 32, 1024], P('row', None, 'col'), may hold values from -6 to 6
- leaf_inv: bfloat16 [256, 1024, 1024], P('row', 'col'), as said below
- leaf_cpl: bfloat16 [256, 1024, 512], P('row', 'col'), may hold values from -0.046875 to 0.046875
- leaf_size: int32 [256], P('row'), may hold values from 256 to 1024, as said below
- leaf_parent: int32 [256], P('row'), may hold values from 0 to 3
- leaf_map: int32 [256, 512], P('row'), may hold values from 0 to 2047
- mid_grad: bfloat16 [32, 4, 2048], P(None, 'col', 'row'), may hold values from -6 to 6
- mid_inv: bfloat16 [4, 2048, 2048], P('col', 'row'), as said below
- mid_cpl: bfloat16 [4, 2048, 512], P('col', 'row'), may hold values from -0.125 to 0.125
- mid_map: int32 [4, 512], replicated, may hold values from 0 to 2047
- root_grad: bfloat16 [32, 2048], P(None, 'row'), may hold values from -6 to 6
- root_inv: bfloat16 [2048, 2048], P('row'), as said below
Outputs:
- leaf_x: float32 [256, 32, 1024], P('row', None, 'col')
- mid_x: float32 [32, 4, 2048], P(None, 'col', 'row')
- root_x: float32 [32, 2048], P(None, 'row')
Inputs may be any that keep to these rules, and one draw needn't show every extreme that they name: `leaf_size`: some leaf in every draw has 1024 live pivot columns. `leaf_map`: columns may repeat. `mid_map`: columns may repeat. `leaf_inv`: upper triangular; diagonal entries between 1 and 1.25, entries above the diagonal of scale 1024 ** -0.5. `mid_inv`: each front's block is upper triangular; diagonal entries between 1 and 1.25, entries above the diagonal of scale 2048 ** -0.5. `root_inv`: upper triangular; diagonal entries between 1 and 1.25, entries above the diagonal of scale 2048 ** -0.5.
All inputs are finite; a program needn't handle non-finite values.
Results may differ from a plain program's by a relative error of at most 0.012.
Values may be sent and summed in bfloat16 or wider, within the bound.
No kernel may reach another device: no remote copies, remote signals or barrier semaphores. Data moves between devices by JAX's collectives and lax.ppermute only.
A program may use at most 64 MiB of HBM per device.

v0:
```python
import jax
import jax.numpy as jnp
from jax import lax
from jax.sharding import PartitionSpec as P


def body(
    leaf_grad,
    leaf_inv,
    leaf_cpl,
    leaf_size,
    leaf_parent,
    leaf_map,
    mid_grad,
    mid_inv,
    mid_cpl,
    mid_map,
    root_grad,
    root_inv,
):
    ncolumns = lax.axis_size("col")
    row_id = lax.axis_index("row")
    col_id = lax.axis_index("col")
    nleaves = leaf_inv.shape[0]
    share_rows = leaf_inv.shape[1]
    nrhs = leaf_grad.shape[1]
    front = mid_inv.shape[2]
    mid_rows = mid_inv.shape[1]
    nmiddle = mid_map.shape[0]
    root_order = root_inv.shape[1]
    root_rows = root_inv.shape[0]
    inv_block = mid_inv[0]
    cpl_block = mid_cpl[0]
    first_cols = col_id * share_rows + lax.iota(jnp.int32, share_rows)
    live = (first_cols[None, :] < leaf_size[:, None])[:, None, :]
    partial_value = jnp.einsum(
        "lkp,lpq->lkq", leaf_grad, leaf_inv, preferred_element_type=jnp.float32
    )
    leaf_y = jnp.where(
        live, lax.psum_scatter(partial_value, "col", scatter_dimension=2, tiled=True), 0.0
    )
    leaf_yb = leaf_y.astype(jnp.bfloat16)
    shares = jnp.einsum("lkp,lpc->klc", leaf_yb, leaf_cpl, preferred_element_type=jnp.float32)
    placed_cols = (
        leaf_map // mid_rows * ncolumns + leaf_parent[:, None]
    ) * mid_rows + leaf_map % mid_rows
    targets = placed_cols.reshape(-1)
    spread = (
        jnp.zeros((nrhs, nmiddle * front), jnp.float32).at[:, targets].add(shares.reshape(nrhs, -1))
    )
    arrived = lax.psum_scatter(spread, ("row", "col"), scatter_dimension=1, tiled=True)
    mid_hb = (mid_grad[:, 0, :].astype(jnp.float32) - arrived).astype(jnp.bfloat16)
    mid_part = jnp.dot(mid_hb, inv_block, preferred_element_type=jnp.float32)
    mid_y = lax.psum_scatter(mid_part, "row", scatter_dimension=1, tiled=True)
    mid_yb = mid_y.astype(jnp.bfloat16)
    mid_share = jnp.dot(mid_yb, cpl_block, preferred_element_type=jnp.float32)
    root_cols = lax.dynamic_index_in_dim(mid_map, col_id, 0, keepdims=False)
    root_term = jnp.zeros((nrhs, root_order), jnp.float32).at[:, root_cols].add(mid_share)
    root_total = lax.psum(root_term, ("row", "col"))
    root_slice = lax.dynamic_slice_in_dim(root_total, row_id * root_rows, root_rows, 1)
    root_hb = (root_grad.astype(jnp.float32) - root_slice).astype(jnp.bfloat16)
    root_y = lax.psum(jnp.dot(root_hb, root_inv, preferred_element_type=jnp.float32), "row")
    root_yb = root_y.astype(jnp.bfloat16)
    root_x = jnp.einsum("kq,pq->kp", root_yb, root_inv, preferred_element_type=jnp.float32)
    root_all = lax.all_gather(root_x.astype(jnp.bfloat16), "row", axis=1, tiled=True)
    coupled = root_all[:, root_cols]
    mid_wb = (
        mid_y - jnp.einsum("kc,bc->kb", coupled, cpl_block, preferred_element_type=jnp.float32)
    ).astype(jnp.bfloat16)
    full_w = lax.all_gather(mid_wb, "row", axis=1, tiled=True)
    mid_x = jnp.einsum("kq,bq->kb", full_w, inv_block, preferred_element_type=jnp.float32)
    all_mid = lax.all_gather(mid_x.astype(jnp.bfloat16), ("row", "col"), axis=1, tiled=True)
    picked = all_mid[:, targets].reshape(nrhs, nleaves, -1)
    leaf_w = leaf_y - jnp.einsum(
        "klc,lpc->lkp", picked, leaf_cpl, preferred_element_type=jnp.float32
    )
    leaf_wb = jnp.where(live, leaf_w, 0.0).astype(jnp.bfloat16)
    leaf_x = jnp.einsum(
        "lkq,lpq->lkp",
        lax.all_gather(leaf_wb, "col", axis=2, tiled=True),
        leaf_inv,
        preferred_element_type=jnp.float32,
    )
    return (leaf_x, mid_x[:, None, :], root_x)


def solution(mesh):
    placed = (
        P("row", None, "col"),
        P("row", "col", None),
        P("row", "col", None),
        P("row"),
        P("row"),
        P("row", None),
        P(None, "col", "row"),
        P("col", "row", None),
        P("col", "row", None),
        P(),
        P(None, "row"),
        P("row", None),
    )
    return jax.shard_map(
        body,
        mesh=mesh,
        in_specs=placed,
        out_specs=(P("row", None, "col"), P(None, "col", "row"), P(None, "row")),
        check_vma=False,
    )
```

profile of v0, /device:TPU:1, one launch (start us, length us, event | category | flops | bytes accessed | tf_op | source)
XLA Modules:
  0.0 2241.0 jit_solution(18431036264109343897)
XLA Ops:
  7.3 1.5 copy-done
  8.8 2.1 fusion.32
  11.2 25.9 %reduce-scatter.6.cloned.1.call-done = f32[4,32,256]{2,1,0:T(8,128)} async-done(((f32[4,32,1024]{2,1,0:T(8,128)}), f32[4,32,256]{2,1,0:T(8,128)}) %reduce-scatter.6.cloned.1.call-update) | async-done | bytes 131088 | tf_op jit(solution)/shard_map/reduce_scatter | solution.py:40
  37.1 1.2 convolution_bitcast_fusion.1
  38.3 1.3 copy.29
  39.6 14.0 scatter_custom_fusion
  54.4 1267.6 %reduce-scatter.8.cloned.1.call-done = f32[32,32]{0,1:T(8,128)} async-done(((f32[32,8192]{0,1:T(8,128)}), f32[32,32]{0,1:T(8,128)}) %reduce-scatter.8.cloned.1.call-update) | async-done | bytes 4112 | tf_op jit(solution)/shard_map/reduce_scatter | solution.py:51
  1322.0 2.0 convolution_bitcast_fusion
  1324.9 135.5 %reduce-scatter.10.cloned.1.call-done = f32[32,32]{1,0:T(8,128)} async-done(((f32[2048,32]{1,0:T(8,128)}), f32[32,32]{1,0:T(8,128)}) %reduce-scatter.10.cloned.1.call-update) | async-done | bytes 4112
  1462.2 3.6 scatter_custom_fusion.1
  1467.7 257.2 %all-reduce.3.cloned.1.call-done = f32[32,2048]{0,1:T(8,128)} async-done(((f32[32,2048]{0,1:T(8,128)}), f32[32,2048]{0,1:T(8,128)}) %all-reduce.3.cloned.1.call-update) | async-done | bytes 262160 | tf_op jit(solution)/shard_map/psum | solution.py:59
  1724.9 0.9 fusion.22
  1725.8 246.2 %all-reduce.4 = bf16[32,2048]{1,0:T(8,128)(2,1)S(1)} all-reduce(f32[32,2048]{1,0:T(8,128)S(1)} %fusion.22), channel_id=1, replica_groups=mesh['row'=64,'col'=4] {'row'}, use_global_device_ids=true, to_apply=%region_6.7 | all-reduce | flops 65536 | bytes 393216 | tf_op jit(solution)/shard_map/psum | solution.py:62
  1972.0 1.7 fusion.30
  1973.8 57.5 %all_gather.12 = bf16[32,2048]{0,1:T(8,128)(2,1)} all-gather(bf16[32,32]{0,1:T(8,128)(2,1)S(1)} %copy.32), channel_id=1, replica_groups=mesh['row'=64,'col'=4] {'row'}, dimensions={1}, use_global_device_ids=true | all-gather | bytes 133120 | tf_op jit(solution)/shard_map/all_gather | solution.py:65
  2031.3 2.3 gather_fusion
  2033.6 0.9 fusion.4
  2034.6 49.7 %all_gather.13 = bf16[32,2048]{0,1:T(8,128)(2,1)S(1)} all-gather(bf16[32,32]{0,1:T(8,128)(2,1)S(1)} %copy.33), channel_id=1, replica_groups=mesh['row'=64,'col'=4] {'row'}, dimensions={1}, use_global_device_ids=true | all-gather | bytes 133120 | tf_op jit(solution)/shard_map/all_gather | solution.py:70
  2084.3 1.8 fusion.31
  2086.2 125.9 %all_gather.14 = bf16[32,8192]{0,1:T(8,128)(2,1)} all-gather(bf16[32,32]{0,1:T(8,128)(2,1)S(1)} %copy.34), channel_id=1, replica_groups=mesh['row'=64,'col'=4] {'row','col'}, dimensions={1}, use_global_device_ids=true | all-gather | bytes 526336 | tf_op jit(solution)/shard_map/all_gather | solution.py:72
  2212.2 9.5 gather_fusion.1
  2221.7 1.5 fusion.3
  2223.2 9.9 all_gather.15
  2233.1 1.4 fusion.33
  (56 shorter events, 5.8 us)
Async XLA Ops:
  7.2 1.6 copy-start
  7.2 3.8 copy-start.11
  7.2 3.8 copy-start.14
  7.2 3.9 copy-start.15
  7.2 29.9 %copy-start.1 = (bf16[4,256,512]{2,1,0:T(8,128)(2,1)S(1)}, bf16[4,256,512]{2,1,0:T(8,128)(2,1)}, u32[]{:S(2)}) copy-start(bf16[4,256,512]{2,1,0:T(8,128)(2,1)} %param.14) | copy-start | bytes 3145732
  7.2 29.9 %reduce-scatter.6.cloned.1.call-start = ((), (), s32[]{:S(2)}) async-start(), calls=%async_computation.3 | async-start | bytes 655360 | tf_op jit(solution)/shard_map/reduce_scatter | solution.py:40
  10.9 1311.1 %reduce-scatter.8.cloned.1.call-start = ((), (), s32[]{:S(2)}) async-start(), calls=%async_computation.4 | async-start | bytes 4210688 | tf_op jit(solution)/shard_map/reduce_scatter | solution.py:51
  11.2 26.0 %copy-start.9 = (pred[4,256]{1,0:T(4,128)(4,1)}, pred[4,256]{1,0:T(4,128)(4,1)S(1)}, u32[]{:S(2)}) copy-start(pred[4,256]{1,0:T(4,128)(4,1)S(1)} %broadcast_compare_fusion) | copy-start | bytes 3076
  11.2 42.5 %copy-start.7 = (s32[2048,1]{0,1:T(1,128)}, s32[2048,1]{0,1:T(1,128)S(1)}, u32[]{:S(2)}) copy-start(s32[2048,1]{0,1:T(1,128)S(1)} %compare_select_fusion) | copy-start | bytes 24580
  53.6 0.7 copy-start.12
  53.6 1268.4 %copy-start.4 = (bf16[1,32,2048]{2,1,0:T(8,128)(2,1)S(1)}, bf16[1,32,2048]{2,1,0:T(8,128)(2,1)}, u32[]{:S(2)}) copy-start(bf16[1,32,2048]{2,1,0:T(8,128)(2,1)} %param.19) | copy-start | bytes 393220
  53.7 1407.5 %copy-start.5 = (bf16[1,32,512]{2,1,0:T(8,128)(2,1)S(1)}, bf16[1,32,512]{2,1,0:T(8,128)(2,1)}, u32[]{:S(2)}) copy-start(bf16[1,32,512]{2,1,0:T(8,128)(2,1)} %param.20) | copy-start | bytes 98308
  53.7 1406.7 %reduce-scatter.10.cloned.1.call-start = ((), (), s32[]{:S(2)}) async-start(), calls=%async_computation.6 | async-start | bytes 1064960
  1324.0 141.8 %copy-start.8 = (s32[2048,1]{0,1:T(1,128)S(1)}, s32[2048,1]{0,1:T(1,128)}, u32[]{:S(2)}) copy-start(s32[2048,1]{0,1:T(1,128)} %copy-done.7) | copy-start | bytes 24580
  1324.0 142.4 %copy-start.13 = (bf16[32,32]{1,0:T(8,128)(2,1)S(1)}, bf16[32,32]{1,0:T(8,128)(2,1)}, u32[]{:S(2)}) copy-start(bf16[32,32]{1,0:T(8,128)(2,1)} %param.22) | copy-start | bytes 6148
  1324.0 400.8 %copy-start.3 = (bf16[32,2048]{1,0:T(8,128)(2,1)S(1)}, bf16[32,2048]{1,0:T(8,128)(2,1)}, u32[]{:S(2)}) copy-start(bf16[32,2048]{1,0:T(8,128)(2,1)} %param.23) | copy-start | bytes 393220
  1324.1 400.8 %all-reduce.3.cloned.1.call-start = ((), (), s32[]{:S(2)}) async-start(), calls=%async_computation.5 | async-start | bytes 2097152 | tf_op jit(solution)/shard_map/psum | solution.py:59
  1973.8 238.4 %copy-start.6 = (s32[2048]{0:T(1024)S(1)}, s32[2048]{0:T(1024)}, u32[]{:S(2)}) copy-start(s32[2048]{0:T(1024)} %broadcast_clamp_fusion) | copy-start | bytes 24580
  2084.3 137.4 %copy-start.2 = (f32[4,32,256]{2,1,0:T(8,128)S(1)}, f32[4,32,256]{2,1,0:T(8,128)}, u32[]{:S(2)}) copy-start(f32[4,32,256]{2,1,0:T(8,128)} %reduce-scatter.6.cloned.1.call-done) | copy-start | bytes 393220
  2084.3 137.4 %copy-start.10 = (pred[4,256]{1,0:T(4,128)(4,1)S(1)}, pred[4,256]{1,0:T(4,128)(4,1)}, u32[]{:S(2)}) copy-start(pred[4,256]{1,0:T(4,128)(4,1)} %copy-done.9) | copy-start | bytes 3076
Sparse Core Ops, SparseCore 0:
  11.0 26.0 reduce-scatter.5
  53.8 1268.1 reduce-scatter.7
  1326.5 133.8 reduce-scatter.9
  1466.6 258.2 all-reduce.2
where the time goes:
time: 2240 us
  waiting for transfers between devices  1690 us (75%)
  blocking collectives  489 us (22%)
    reduce_scatter x1, waiting for transfers between devices, body(): lax.psum_scatter(spread, ('row', 'col'), scatter_dimension=1, tiled=True)  1270 us
    psum x1, waiting for transfers between devices, body(): root_total = lax.psum(root_term, ('row', 'col'))  257 us
    psum x1, blocking collectives, body(): lax.psum(jnp.dot(root_hb, root_inv, preferred_element_type=jnp.float32),...  246 us
    unnamed x5, waiting for transfers between devices  136 us
    all_gather x1, blocking collectives, body(): lax.all_gather(mid_x.astype(jnp.bfloat16), ('row', 'col'), axis=1, tiled=...  126 us
    all_gather x1, blocking collectives, body(): lax.all_gather(root_x.astype(jnp.bfloat16), 'row', axis=1, tiled=True)  57.5 us
    all_gather x1, blocking collectives, body(): full_w = lax.all_gather(mid_wb, 'row', axis=1, tiled=True)  49.7 us
  transfers between devices with their start and end apart: 4, of which 4 were waited for; matrix products, arithmetic and copies ran while one was open for 0% of the time, Pallas kernels for 0%

commit v1 on v0

v1 whole, which is shorter than its diff:
```python
import jax
import jax.numpy as jnp
from jax import lax
from jax.sharding import Mesh, PartitionSpec as P

BF = jnp.bfloat16
F32 = jnp.float32


def mm(a, b):
    return jnp.dot(a, b, preferred_element_type=F32)


def mm_t(a, b):
    return lax.dot_general(a, b, (((1,), (1,)), ((), ())), preferred_element_type=F32)


def a2a(v, axes):
    return lax.all_to_all(v, axes, 0, 0, tiled=True)


def spread(v, axes):
    n = lax.axis_size(axes)
    return lax.all_to_all(
        jnp.broadcast_to(v[None], (n,) + v.shape), axes, 0, 0, tiled=True
    )


def swap(v):
    return lax.ppermute(v, "c", [(0, 1), (1, 0)])


def half_sum(v, core):
    k = v.shape[-2] // 2
    lo, hi = v[..., :k, :], v[..., k:, :]
    mine = jnp.where(core == 0, lo, hi)
    theirs = jnp.where(core == 0, hi, lo).astype(BF)
    return mine + swap(theirs).astype(F32)


def both_halves(v, core):
    other = swap(v)
    lo = jnp.where(core == 0, v, other)
    hi = jnp.where(core == 0, other, v)
    return jnp.concatenate([lo, hi], axis=-2)


def to_tiles(v):
    k, n = v.shape
    return v.reshape(k // 8, 8, n // 128, 128).transpose(0, 2, 1, 3).reshape(-1, 8, 128)


def from_tiles(v, k, n):
    return v.reshape(k // 8, n // 128, 8, 128).transpose(0, 2, 1, 3).reshape(k, n)


def body(
    leaf_grad,
    leaf_inv,
    leaf_cpl,
    leaf_size,
    leaf_parent,
    leaf_map,
    mid_grad,
    mid_inv,
    mid_cpl,
    mid_map,
    root_grad,
    root_inv,
):
    ny, nz, nc, nx = (lax.axis_size(a) for a in ("y", "z", "c", "x"))
    iy, iz, ic, ix = (lax.axis_index(a) for a in ("y", "z", "c", "x"))
    nl, share, order = leaf_inv.shape
    nk = leaf_grad.shape[1]
    rows, front = mid_inv.shape[1:]
    ncpl = leaf_cpl.shape[2]
    nmid = mid_map.shape[0]
    parts = ny * nc
    width = front // parts

    def renumber(m):
        i = m % rows
        c = m // rows % nc
        z = m // (rows * nc) % nz
        y = m // (rows * nc * nz)
        return ((z * ny + y) * nc + c) * rows + i

    own = ((iz * ny + iy) * nc + ic) * rows

    with jax.named_scope("gather_inverses"):
        pm = mm(mid_grad[:, 0, :], mid_inv[0]).astype(BF)
        pr = mm(root_grad, root_inv).astype(BF)
        both = jnp.stack(
            [
                jnp.concatenate([mid_inv[0], pm], 0),
                jnp.concatenate([root_inv, pr], 0),
            ]
        )
        both = both.reshape(2, rows + nk, ny, nz, nc, rows)
        both = both.transpose(2, 4, 1, 0, 3, 5).reshape(parts, rows + nk, 2 * width)
        got = a2a(both, ("y", "c"))
        psum = jnp.sum(got[:, rows:].astype(F32), 0).astype(BF)
        mine = jnp.concatenate(
            [got[:, :rows].reshape(parts * rows, 2 * width), psum, mid_cpl[0]], 0
        )
        wide = lax.all_gather(mine, "z", axis=0)
        nr = parts * rows
        cols = wide[:, :nr].reshape(front, 2 * width)
        minv, rinv = cols[:, :width], cols[:, width:]
        pres = jnp.sum(wide[:, nr : nr + nk].astype(F32), 0)
        pre_m, pre_r = pres[:, :width], pres[:, width:]
        mcpl = wide[:, nr + nk :].reshape(width, ncpl)

    with jax.named_scope("leaf_forward"):
        live = (ix * share + lax.iota(jnp.int32, share))[None, :] < leaf_size[:, None]
        live = live[:, None, :]
        part = jnp.einsum(
            "lkp,lpxq->xlkq",
            leaf_grad,
            leaf_inv.reshape(nl, share, nx, share),
            preferred_element_type=F32,
        ).astype(BF)
        leaf_y = jnp.where(live, jnp.sum(a2a(part, "x").astype(F32), 0), 0.0)
        leaf_u = jnp.einsum(
            "lkp,lpc->klc", leaf_y.astype(BF), leaf_cpl, preferred_element_type=F32
        ).astype(BF)
    with jax.named_scope("leaf_spread"):
        target = renumber(leaf_map)
        hot = (target.reshape(-1)[:, None] == lax.iota(jnp.int32, front)[None, :]).astype(BF)
        parent_of = jnp.arange(nmid)[:, None] == leaf_parent[None, :]
        lhs = jnp.where(parent_of[:, None, :, None], leaf_u[None], 0).reshape(
            nmid * nk, nl * ncpl
        )
        placed = mm(lhs, hot).reshape(nmid, nk, front)
    with jax.named_scope("contrib_sum"):
        s = half_sum(placed, ic).astype(BF)
        s = jnp.sum(a2a(s, "x").astype(F32), 0).astype(BF)
        s = jnp.sum(a2a(to_tiles(s), ("y", "z")).reshape(ny * nz, 8, 128).astype(F32), 0)
        s = spread(s.astype(BF), ("y", "z"))
        contrib = both_halves(from_tiles(s.reshape(-1, 8, 128), nk // 2, front), ic)
    with jax.named_scope("mid_forward"):
        mid_y = pre_m - mm(contrib, minv)
        mid_u = half_sum(mm(mid_y.astype(BF), mcpl), ic).astype(BF)
        u = spread(mid_u, ("y", "x")).reshape(ny, nx, nk // 2, ncpl)
        u = both_halves(jnp.sum(u.astype(F32), 0).astype(BF), ic)
    with jax.named_scope("root"):
        rmap = renumber(mid_map)
        rhot = (rmap.reshape(-1)[:, None] == lax.iota(jnp.int32, front)[None, :]).astype(BF)
        total = mm(u.transpose(1, 0, 2).reshape(nk, nmid * ncpl), rhot).astype(BF)
        root_y = (pre_r - mm(total, rinv)).astype(BF)
        rx = half_sum(mm_t(root_y, rinv), ic).astype(BF)
        rx = jnp.sum(spread(rx, "y").reshape(ny, nk // 2, front).astype(F32), 0).astype(BF)
        root_x = both_halves(rx, ic)
    with jax.named_scope("mid_backward"):
        mymap = lax.dynamic_index_in_dim(rmap, ix, 0, keepdims=False)
        myhot = (mymap[:, None] == lax.iota(jnp.int32, front)[None, :]).astype(BF)
        coupled = mm_t(root_x, myhot).astype(BF)
        mid_w = (mid_y - mm_t(coupled, mcpl)).astype(BF)
        mx = half_sum(mm_t(mid_w, minv), ic).astype(BF)
        mx = spread(mx, ("y", "x")).reshape(ny, nx, nk // 2, front)
        mid_x = both_halves(jnp.sum(mx.astype(F32), 0).astype(BF), ic)
    with jax.named_scope("leaf_backward"):
        hot3 = hot.reshape(nl, ncpl, front)
        picked = jnp.einsum(
            "lkn,lcn->lkc", mid_x[leaf_parent], hot3, preferred_element_type=F32
        ).astype(BF)
        leaf_w = leaf_y - jnp.einsum(
            "lkc,lpc->lkp", picked, leaf_cpl, preferred_element_type=F32
        )
        leaf_w = jnp.where(live, leaf_w, 0.0).astype(BF)
        full = spread(leaf_w, "x").reshape(nx, nl, nk, share)
        leaf_x = jnp.einsum(
            "xlkq,lpxq->lkp",
            full,
            leaf_inv.reshape(nl, share, nx, share),
            preferred_element_type=F32,
        )
    out_m = lax.dynamic_slice(
        lax.dynamic_index_in_dim(mid_x, ix, 0, keepdims=False), (0, own), (nk, rows)
    )
    out_r = lax.dynamic_slice(root_x, (0, own), (nk, rows))
    return leaf_x, out_m.astype(F32)[:, None, :], out_r.astype(F32)


def solution(mesh):
    grid = Mesh(mesh.devices.reshape(4, 8, 2, 4), ("y", "z", "c", "x"))
    row = ("y", "z", "c")
    placed = (
        P(row, None, "x"),
        P(row, "x", None),
        P(row, "x", None),
        P(row),
        P(row),
        P(row, None),
        P(None, "x", row),
        P("x", row, None),
        P("x", row, None),
        P(),
        P(None, row),
        P(row, None),
    )
    return jax.shard_map(
        body,
        mesh=grid,
        in_specs=placed,
        out_specs=(P(row, None, "x"), P(None, "x", row), P(None, row)),
        check_vma=False,
    )
```

time: 2240 us -> 208 us (0.09)
  waiting for transfers between devices: 1690 us -> 37.3 us
  blocking collectives: 489 us -> 66.3 us
  starting transfers between devices: 0.16 us -> 27.1 us
    reduce_scatter x2 -> x0, waiting for transfers between devices: 1290 us -> none  [the longest x1 1270 us: body(): lax.psum_scatter(spread, ('row', 'col'), scatter_dimension=1, tiled=True)]
    psum x1 -> x0, waiting for transfers between devices: 257 us -> none  [body(): root_total = lax.psum(root_term, ('row', 'col'))]
    psum x1 -> x0, blocking collectives: 246 us -> none  [body(): lax.psum(jnp.dot(root_hb, root_inv, preferred_element_type=jnp.float32),...]
    all_gather x4 -> x0, blocking collectives: 243 us -> none  [the longest x1 126 us: body(): lax.all_gather(mid_x.astype(jnp.bfloat16), ('row', 'col'), axis=1, tiled=...]
    unnamed x5 -> x1, waiting for transfers between devices: 136 us -> 0.02 us
    all_to_all x0 -> x5, blocking collectives: none -> 66.3 us  [the longest x3 43.1 us: a2a(): return lax.all_to_all(v, axes, 0, 0, tiled=True)]
    all_to_all x0 -> x4, waiting for transfers between devices: none -> 30.1 us  [the longest x3 26 us: spread(): lax.all_to_all(jnp.broadcast_to(v[None], (n,) + v.shape), axes, 0, 0, til...]
  transfers between devices with their start and end apart: 4 -> 13, of which waited for: 4 -> 12; matrix products, arithmetic and copies ran while one was open for 0% -> 7% of each run, Pallas kernels for 0% -> 0%
where the time goes in v1:
time: 208 us; the launch traced here: 207 us
  blocking collectives  66.3 us (32%)
  waiting for transfers between devices  37.3 us (18%)
  starting transfers between devices  27.1 us (13%)
  matrix products  25.7 us (12%)
  other arithmetic  18.1 us (9%)
  local copies, waits for them, and re-layouts  17.8 us (9%)
  between operations  14.5 us (7%)
    all_to_all x3, blocking collectives, a2a(): return lax.all_to_all(v, axes, 0, 0, tiled=True)  43.1 us
    all_to_all x3, waiting for transfers between devices, spread(): lax.all_to_all(jnp.broadcast_to(v[None], (n,) + v.shape), axes, 0, 0, til...  26 us
    all_to_all x2, blocking collectives, spread(): lax.all_to_all(jnp.broadcast_to(v[None], (n,) + v.shape), axes, 0, 0, til...  23.2 us
    ppermute x8, starting transfers between devices, swap(): return lax.ppermute(v, 'c', [(0, 1), (1, 0)])  11.9 us
    all_to_all x3, starting transfers between devices, spread(): lax.all_to_all(jnp.broadcast_to(v[None], (n,) + v.shape), axes, 0, 0, til...  11.8 us
    dot_general x6, matrix products, mm(): return jnp.dot(a, b, preferred_element_type=F32)  11.3 us
    ppermute x8, waiting for transfers between devices, swap(): return lax.ppermute(v, 'c', [(0, 1), (1, 0)])  7.14 us
    dot_general x3, matrix products, mm_t(): lax.dot_general(a, b, (((1,), (1,)), ((), ())), preferred_element_type=F32)  5.35 us
  transfers between devices with their start and end apart: 13, of which 12 were waited for; matrix products, arithmetic and copies ran while one was open for 7% of the time, Pallas kernels for 0%

profile of v1, /device:TPU:1, one launch (start us, length us, event | category | flops | bytes accessed | tf_op | source)
XLA Modules:
  0.0 206.7 jit_solution(6767824319285872340)
XLA Ops:
  14.6 2.5 %copy.54 = bf16[8,64,512]{2,1,0:T(8,128)(2,1)} copy(bf16[8,64,512]{1,2,0:T(8,128)(2,1)} %bitcast.94) | data formatting | bytes 1048576 | tf_op jit(solution)/shard_map/gather_inverses/reshape | solution.py:100
  17.1 16.0 %all_to_all.45 = bf16[8,64,512]{2,1,0:T(8,128)(2,1)S(1)} all-to-all(bf16[8,64,512]{2,1,0:T(8,128)(2,1)} %copy.54), channel_id=1, replica_groups=mesh['y'=4,'z'=8,'c'=2,'x'=4] {'y','c'}, dimensions={0} | all-to-all | bytes 1048576 | tf_op jit(solution)/shard_map/gather_inverses/all_to_all | solution.py:19
  35.2 3.4 %all-to-all-start = ((bf16[4,4,32,256]{3,2,1,0:T(8,128)(2,1)}), bf16[4,4,32,256]{3,2,1,0:T(8,128)(2,1)S(1)}, u32[]{:S(2)}, u32[]{:S(2)}) async-start(bf16[4,4,32,256]{3,2,1,0:T(8,128)(2,1)} %copy.49), calls=%async_computation | async-start | bytes 524288 | tf_op jit(solution)/shard_map/leaf_forward/all_to_all | solution.py:19
  40.0 4.1 %all-to-all-done = bf16[4,4,32,256]{3,2,1,0:T(8,128)(2,1)S(1)} async-done(((bf16[4,4,32,256]{3,2,1,0:T(8,128)(2,1)}), bf16[4,4,32,256]{3,2,1,0:T(8,128)(2,1)S(1)}, u32[]{:S(2)}, u32[]{:S(2)}) %all-to-all-start) | async-done | bytes 262176 | tf_op jit(solution)/shard_map/leaf_forward/all_to_all | solution.py:19
  45.1 4.4 %fusion.3 = f32[4,32,2048]{2,1,0:T(8,128)S(1)} fusion(s32[2048]{0:T(1024)} %bitcast.113, pred[4,2048]{1,0:T(4,128)(4,1)S(1)} %bitcast.112, bf16[32,2048]{1,0:T(8,128)(2,1)S(1)} %bitcast.108), kind=kOutput, calls=%fused_computation.7 | convolution fusion | flops 1078198272 | bytes 1196032 | tf_op jit(solution)/shard_map/leaf_spread/dot_general | solution.py:11
  49.6 2.5 %collective-permute-start = (bf16[4,16,2048]{2,1,0:T(8,128)(2,1)S(1)}, bf16[4,16,2048]{2,1,0:T(8,128)(2,1)S(1)}, u32[]{:S(2)}, u32[]{:S(2)}) collective-permute-start(bf16[4,16,2048]{2,1,0:T(8,128)(2,1)S(1)} %select_convert_fusion), channel_id=1, source_target_pairs={{0,4},{4,0},{1,5},{5,1},{2,6},{6,2},{3,7},{7,3},{8,12},{12,8},{9,1... | collective-permute-start | bytes 786440 | tf_op jit(solution)/shard_map/contrib_sum/ppermute | solution.py:30
  53.4 8.8 %all_to_all.46 = bf16[4,16,2048]{2,1,0:T(8,128)(2,1)S(1)} all-to-all(bf16[4,16,2048]{2,1,0:T(8,128)(2,1)S(1)} %add_convert_fusion), channel_id=1, replica_groups=mesh['y'=4,'z'=8,'c'=2,'x'=4] {'x'}, dimensions={0} | all-to-all | bytes 524288 | tf_op jit(solution)/shard_map/contrib_sum/all_to_all | solution.py:19
  62.8 18.3 %all_to_all.47 = bf16[32,8,128]{2,1,0:T(8,128)(2,1)S(1)} all-to-all(bf16[32,8,128]{2,1,0:T(8,128)(2,1)} %bitcast.105), channel_id=1, replica_groups=mesh['y'=4,'z'=8,'c'=2,'x'=4] {'y','z'}, dimensions={0} | all-to-all | bytes 131072 | tf_op jit(solution)/shard_map/contrib_sum/all_to_all | solution.py:19
  81.2 12.1 %all_to_all.48 = bf16[32,8,128]{2,1,0:T(8,128)(2,1)S(1)} all-to-all(bf16[32,8,128]{2,1,0:T(8,128)(2,1)S(1)} %broadcast_in_dim.95), channel_id=1, replica_groups=mesh['y'=4,'z'=8,'c'=2,'x'=4] {'y','z'}, dimensions={0} | all-to-all | bytes 131072 | tf_op jit(solution)/shard_map/contrib_sum/all_to_all | solution.py:24
  93.3 3.4 %collective-permute-start.1 = (bf16[16,2048]{1,0:T(8,128)(2,1)S(1)}, bf16[16,2048]{1,0:T(8,128)(2,1)S(1)}, u32[]{:S(2)}, u32[]{:S(2)}) collective-permute-start(bf16[16,2048]{1,0:T(8,128)(2,1)S(1)} %bitcast.106), channel_id=1, source_target_pairs={{0,4},{4,0},{1,5},{5,1},{2,6},{6,2},{3,7},{7,3},{8,12},{12,8},{9,1... | collective-permute-start | bytes 196616 | tf_op jit(solution)/shard_map/contrib_sum/ppermute | solution.py:30
  97.7 1.8 slice.76
  103.5 11.1 %all_to_all.49 = bf16[16,16,512]{2,1,0:T(8,128)(2,1)S(1)} all-to-all(bf16[16,16,512]{2,1,0:T(8,128)(2,1)S(1)} %broadcast_in_dim.96), channel_id=1, replica_groups=mesh['y'=4,'z'=8,'c'=2,'x'=4] {'y','x'}, dimensions={0} | all-to-all | bytes 524288 | tf_op jit(solution)/shard_map/mid_forward/all_to_all | solution.py:24
  118.8 5.2 %fusion.34 = bf16[32,256]{1,0:T(8,128)(2,1)} fusion(bf16[32,2048]{1,0:T(8,128)(2,1)S(1)} %bitcast.109, s32[2048]{0:T(1024)S(1)} %bitcast.114, bf16[2048,512]{1,0:T(8,128)(2,1)} %bitcast.91, f32[32,512]{1,0:T(8,128)} %copy-done.10), kind=kOutput, calls=%fused_computation.38 | convolution fusion | flops 306266112 | bytes 1236992 | tf_op jit(solution)/shard_map/root/dot_general | solution.py:11
  129.4 3.4 %all-to-all-start.6 = ((bf16[4,16,2048]{2,1,0:T(8,128)(2,1)}), bf16[4,16,2048]{2,1,0:T(8,128)(2,1)S(1)}, u32[]{:S(2)}, u32[]{:S(2)}) async-start(bf16[4,16,2048]{2,1,0:T(8,128)(2,1)} %broadcast_in_dim.97), calls=%async_computation.6 | async-start | bytes 524288 | tf_op jit(solution)/shard_map/root/all_to_all | solution.py:24
  133.5 5.5 %all-to-all-done.6 = bf16[4,16,2048]{2,1,0:T(8,128)(2,1)S(1)} async-done(((bf16[4,16,2048]{2,1,0:T(8,128)(2,1)}), bf16[4,16,2048]{2,1,0:T(8,128)(2,1)S(1)}, u32[]{:S(2)}, u32[]{:S(2)}) %all-to-all-start.6) | async-done | bytes 262176 | tf_op jit(solution)/shard_map/root/all_to_all | solution.py:24
  143.1 2.1 fusion.33
  149.3 4.3 %all-to-all-start.7 = ((bf16[16,16,2048]{2,1,0:T(8,128)(2,1)}), bf16[16,16,2048]{2,1,0:T(8,128)(2,1)}, u32[]{:S(2)}, u32[]{:S(2)}) async-start(bf16[16,16,2048]{2,1,0:T(8,128)(2,1)} %broadcast_in_dim.98), calls=%async_computation.7 | async-start | bytes 2097152 | tf_op jit(solution)/shard_map/mid_backward/all_to_all | solution.py:24
  153.7 17.2 %all-to-all-done.7 = bf16[16,16,2048]{2,1,0:T(8,128)(2,1)} async-done(((bf16[16,16,2048]{2,1,0:T(8,128)(2,1)}), bf16[16,16,2048]{2,1,0:T(8,128)(2,1)}, u32[]{:S(2)}, u32[]{:S(2)}) %all-to-all-start.7) | async-done | bytes 1048608 | tf_op jit(solution)/shard_map/mid_backward/all_to_all | solution.py:24
  172.3 1.7 collective-permute-start.7
  177.9 2.5 %gather_fusion = bf16[4,32,2048]{2,1,0:T(8,128)(2,1)} fusion(bf16[4,32,2048]{2,1,0:T(8,128)(2,1)} %pad_maximum_fusion, s32[1024]{0:T(1024)} %pad_clamp_fusion), kind=kCustom, calls=%fused_computation | custom fusion | bytes 1048592 | tf_op jit(solution)/shard_map/leaf_backward/gather | solution.py:165
  180.5 5.3 %fusion.29 = bf16[4,32,256]{2,1,0:T(8,128)(2,1)} fusion(bf16[4,256,512]{2,1,0:T(8,128)(2,1)S(1)} %copy-done, bf16[4,32,2048]{2,1,0:T(8,128)(2,1)} %gather_fusion, s32[4,512]{1,0:T(4,128)S(1)} %fusion.63, f32[4,32,256]{2,1,0:T(8,128)S(1)} %convert_reduce_fusion.1, pred[4,256]{1,0:T(4,128)(4,1)} %broadcast_compare_fusion), kind=kOutput, calls=%fused_computation.31 | convolution fusion | flops 306380800 | bytes 1778688 | tf_op jit(solution)/shard_map/leaf_backward/lkc,lpc->lkp/dot_general | solution.py:167
  187.3 4.0 %all-to-all-start.8 = ((bf16[4,4,32,256]{3,2,1,0:T(8,128)(2,1)}), bf16[4,4,32,256]{3,2,1,0:T(8,128)(2,1)}, u32[]{:S(2)}, u32[]{:S(2)}) async-start(bf16[4,4,32,256]{3,2,1,0:T(8,128)(2,1)} %broadcast_in_dim.100), calls=%async_computation.8 | async-start | bytes 524288 | tf_op jit(solution)/shard_map/leaf_backward/all_to_all | solution.py:24
  194.1 3.4 %all-to-all-done.8 = bf16[4,4,32,256]{3,2,1,0:T(8,128)(2,1)} async-done(((bf16[4,4,32,256]{3,2,1,0:T(8,128)(2,1)}), bf16[4,4,32,256]{3,2,1,0:T(8,128)(2,1)}, u32[]{:S(2)}, u32[]{:S(2)}) %all-to-all-start.8) | async-done | bytes 262176 | tf_op jit(solution)/shard_map/leaf_backward/all_to_all | solution.py:24
  197.5 2.3 %fusion.25 = f32[4,32,256]{2,1,0:T(8,128)} fusion(bf16[4,4,32,256]{3,2,1,0:T(8,128)(2,1)} %all-to-all-done.8, bf16[4,32,4,8,256]{4,3,2,1,0:T(8,128)(2,1)S(1)} %bitcast.89), kind=kOutput, calls=%fused_computation.28 | convolution fusion | flops 67108864 | bytes 2490368 | tf_op jit(solution)/shard_map/leaf_backward/xlkq,lpxq->lkp/dot_general | solution.py:172
  (116 shorter events, 46.9 us)
Async XLA Ops:
  7.2 37.0 %copy-start = (bf16[4,256,512]{2,1,0:T(8,128)(2,1)S(1)}, bf16[4,256,512]{2,1,0:T(8,128)(2,1)}, u32[]{:S(2)}) copy-start(bf16[4,256,512]{2,1,0:T(8,128)(2,1)} %param.14) | copy-start | bytes 3145732
  7.2 90.4 %all-gather.3.cloned.1.call-start = ((), (), s32[]{:S(2)}) async-start(), calls=%async_computation.9 | async-start | bytes 2949120 | tf_op jit(solution)/shard_map/gather_inverses/all_gather | solution.py:106
  14.6 18.6 %copy-start.11 = (bf16[1,32,512]{2,1,0:T(8,128)(2,1)S(1)}, bf16[1,32,512]{2,1,0:T(8,128)(2,1)}, u32[]{:S(2)}) copy-start(bf16[1,32,512]{2,1,0:T(8,128)(2,1)} %param.20) | copy-start | bytes 98308
  14.6 19.4 %copy-start.1 = (bf16[4,256,1024]{2,1,0:T(8,128)(2,1)S(1)}, bf16[4,256,1024]{2,1,0:T(8,128)(2,1)}, u32[]{:S(2)}) copy-start(bf16[4,256,1024]{2,1,0:T(8,128)(2,1)} %param.13) | copy-start | bytes 6291460
  14.6 19.4 %copy-start.9 = (bf16[4,32,256]{2,1,0:T(8,128)(2,1)S(1)}, bf16[4,32,256]{2,1,0:T(8,128)(2,1)}, u32[]{:S(2)}) copy-start(bf16[4,32,256]{2,1,0:T(8,128)(2,1)} %param.12) | copy-start | bytes 196612
  33.2 5.5 %copy-start.13 = (s32[4,512]{1,0:T(4,128)S(1)}, s32[4,512]{1,0:T(4,128)}, u32[]{:S(2)}) copy-start(s32[4,512]{1,0:T(4,128)} %param.17) | copy-start | bytes 24580
  33.9 5.4 %copy-start.16 = (s32[4]{0:T(128)S(1)}, s32[4]{0:T(128)}, u32[]{:S(2)}) copy-start(s32[4]{0:T(128)} %param.15) | copy-start | bytes 52
  35.2 8.9 %all-to-all-start = ((bf16[4,4,32,256]{3,2,1,0:T(8,128)(2,1)}), bf16[4,4,32,256]{3,2,1,0:T(8,128)(2,1)S(1)}, u32[]{:S(2)}, u32[]{:S(2)}) async-start(bf16[4,4,32,256]{3,2,1,0:T(8,128)(2,1)} %copy.49), calls=%async_computation | async-start | bytes 524288 | tf_op jit(solution)/shard_map/leaf_forward/all_to_all | solution.py:19
  49.6 3.7 %collective-permute-start = (bf16[4,16,2048]{2,1,0:T(8,128)(2,1)S(1)}, bf16[4,16,2048]{2,1,0:T(8,128)(2,1)S(1)}, u32[]{:S(2)}, u32[]{:S(2)}) collective-permute-start(bf16[4,16,2048]{2,1,0:T(8,128)(2,1)S(1)} %select_convert_fusion), channel_id=1, source_target_pairs={{0,4},{4,0},{1,5},{5,1},{2,6},{6,2},{3,7},{7,3},{8,12},{12,8},{9,1... | collective-permute-start | bytes 786440 | tf_op jit(solution)/shard_map/contrib_sum/ppermute | solution.py:30
  93.3 4.3 %collective-permute-start.1 = (bf16[16,2048]{1,0:T(8,128)(2,1)S(1)}, bf16[16,2048]{1,0:T(8,128)(2,1)S(1)}, u32[]{:S(2)}, u32[]{:S(2)}) collective-permute-start(bf16[16,2048]{1,0:T(8,128)(2,1)S(1)} %bitcast.106), channel_id=1, source_target_pairs={{0,4},{4,0},{1,5},{5,1},{2,6},{6,2},{3,7},{7,3},{8,12},{12,8},{9,1... | collective-permute-start | bytes 196616 | tf_op jit(solution)/shard_map/contrib_sum/ppermute | solution.py:30
  99.5 17.3 %copy-start.12 = (s32[4,512]{1,0:T(4,128)S(1)}, s32[4,512]{1,0:T(4,128)}, u32[]{:S(2)}) copy-start(s32[4,512]{1,0:T(4,128)} %param.21) | copy-start | bytes 24580
  100.7 13.9 %copy-start.10 = (f32[32,512]{1,0:T(8,128)}, f32[32,512]{1,0:T(8,128)S(1)}, u32[]{:S(2)}) copy-start(f32[32,512]{1,0:T(8,128)S(1)} %convert_reduce_fusion) | copy-start | bytes 196612
  102.2 1.3 collective-permute-start.2
  115.3 2.6 %collective-permute-start.3 = (bf16[4,16,512]{2,1,0:T(8,128)(2,1)}, bf16[4,16,512]{2,1,0:T(8,128)(2,1)S(1)}, u32[]{:S(2)}, u32[]{:S(2)}) collective-permute-start(bf16[4,16,512]{2,1,0:T(8,128)(2,1)} %reduce_sum.95), channel_id=1, source_target_pairs={{0,4},{4,0},{1,5},{5,1},{2,6},{6,2},{3,7},{7,3},{8,12},{12,8},{9,1... | collective-permute-start | bytes 196616 | tf_op jit(solution)/shard_map/mid_forward/ppermute | solution.py:30
  126.3 1.6 collective-permute-start.4
  129.4 9.5 %all-to-all-start.6 = ((bf16[4,16,2048]{2,1,0:T(8,128)(2,1)}), bf16[4,16,2048]{2,1,0:T(8,128)(2,1)S(1)}, u32[]{:S(2)}, u32[]{:S(2)}) async-start(bf16[4,16,2048]{2,1,0:T(8,128)(2,1)} %broadcast_in_dim.97), calls=%async_computation.6 | async-start | bytes 524288 | tf_op jit(solution)/shard_map/root/all_to_all | solution.py:24
  139.6 2.6 %collective-permute-start.5 = (bf16[16,2048]{1,0:T(8,128)(2,1)}, bf16[16,2048]{1,0:T(8,128)(2,1)S(1)}, u32[]{:S(2)}, u32[]{:S(2)}) collective-permute-start(bf16[16,2048]{1,0:T(8,128)(2,1)} %reduce_sum.96), channel_id=1, source_target_pairs={{0,4},{4,0},{1,5},{5,1},{2,6},{6,2},{3,7},{7,3},{8,12},{12,8},{9,1... | collective-permute-start | bytes 196616 | tf_op jit(solution)/shard_map/root/ppermute | solution.py:30
  143.1 6.2 %copy-start.7 = (bf16[16,2048]{1,0:T(8,128)(2,1)}, bf16[16,2048]{1,0:T(8,128)(2,1)S(1)}, u32[]{:S(2)}) copy-start(bf16[16,2048]{1,0:T(8,128)(2,1)S(1)} %get-tuple-element.22) | copy-start | bytes 196612
  143.1 6.2 %copy-start.8 = (bf16[16,2048]{1,0:T(8,128)(2,1)}, bf16[16,2048]{1,0:T(8,128)(2,1)S(1)}, u32[]{:S(2)}) copy-start(bf16[16,2048]{1,0:T(8,128)(2,1)S(1)} %get-tuple-element.23) | copy-start | bytes 196612
  146.8 6.9 %copy-start.18 = (s32[4]{0:T(128)S(1)}, s32[4]{0:T(128)}, u32[]{:S(2)}) copy-start(s32[4]{0:T(128)} %param.16) | copy-start | bytes 52
  146.9 1.3 collective-permute-start.6
  149.3 21.5 %all-to-all-start.7 = ((bf16[16,16,2048]{2,1,0:T(8,128)(2,1)}), bf16[16,16,2048]{2,1,0:T(8,128)(2,1)}, u32[]{:S(2)}, u32[]{:S(2)}) async-start(bf16[16,16,2048]{2,1,0:T(8,128)(2,1)} %broadcast_in_dim.98), calls=%async_computation.7 | async-start | bytes 2097152 | tf_op jit(solution)/shard_map/mid_backward/all_to_all | solution.py:24
  172.3 3.0 %collective-permute-start.7 = (bf16[4,16,2048]{2,1,0:T(8,128)(2,1)S(1)}, bf16[4,16,2048]{2,1,0:T(8,128)(2,1)}, u32[]{:S(2)}, u32[]{:S(2)}) collective-permute-start(bf16[4,16,2048]{2,1,0:T(8,128)(2,1)S(1)} %reduce_sum.97), channel_id=1, source_target_pairs={{0,4},{4,0},{1,5},{5,1},{2,6},{6,2},{3,7},{7,3},{8,12},{12,8},{9,1... | collective-permute-start | bytes 786440 | tf_op jit(solution)/shard_map/mid_backward/ppermute | solution.py:30
  187.3 10.2 %all-to-all-start.8 = ((bf16[4,4,32,256]{3,2,1,0:T(8,128)(2,1)}), bf16[4,4,32,256]{3,2,1,0:T(8,128)(2,1)}, u32[]{:S(2)}, u32[]{:S(2)}) async-start(bf16[4,4,32,256]{3,2,1,0:T(8,128)(2,1)} %broadcast_in_dim.100), calls=%async_computation.8 | async-start | bytes 524288 | tf_op jit(solution)/shard_map/leaf_backward/all_to_all | solution.py:24
  (8 other events, 22.8 us)
Sparse Core Ops, SparseCore 0:
  34.1 40.3 all-gather.2

commit v2 on v1

v2 whole, which is shorter than its diff:
```python
import functools

import jax
import jax.numpy as jnp
from jax import lax
from jax.experimental import pallas as pl
from jax.experimental.pallas import tpu as pltpu
from jax.sharding import Mesh, PartitionSpec as P

BF = jnp.bfloat16
F32 = jnp.float32
VM = pl.BlockSpec(memory_space=pltpu.VMEM)
SM = pl.BlockSpec(memory_space=pltpu.SMEM)
PARAMS = pltpu.CompilerParams(vmem_limit_bytes=56 * 2**20)


def mm(a, b):
    return jnp.dot(a, b, preferred_element_type=F32)


def mm_t(a, b):
    return lax.dot_general(a, b, (((1,), (1,)), ((), ())), preferred_element_type=F32)


def a2a(v, axes):
    return lax.all_to_all(v, axes, 0, 0, tiled=True)


def spread(v, axes):
    n = lax.axis_size(axes)
    return a2a(jnp.broadcast_to(v[None], (n,) + v.shape), axes)


def swap(v):
    return lax.ppermute(v, "c", [(0, 1), (1, 0)])


def ahead(v, axis):
    n = lax.axis_size(axis)
    return [v] + [
        lax.ppermute(v, axis, [((i + k) % n, i) for i in range(n)]) for k in range(1, n)
    ]


def flip(v):
    n = v.shape[-1] // 2
    return jnp.concatenate([v[..., n:], v[..., :n]], -1)


def after(v, *first):
    return lax.optimization_barrier((v,) + first)[0]


def by_core(core, first, second):
    return jnp.where(core == 0, first, second), jnp.where(core == 0, second, first)


def root_pack_kernel(at, inv_ref, grad_ref, cpl_ref, out_ref, keep_ref):
    rows, nk = inv_ref.shape[0], grad_ref.shape[0]
    keep_ref[...] = inv_ref[...]
    out_ref[:rows, :] = inv_ref[...]
    out_ref[rows : rows + nk, :] = mm(grad_ref[...], inv_ref[...]).astype(BF)
    out_ref[rows + nk :, :] = cpl_ref[...]


def pack_kernel(nk, iy, inv_ref, g0, g1, g2, g3, out_ref):
    rows, front = inv_ref.shape
    got = (g0, g1, g2, g3)
    n = g0.shape[1]
    lane = lax.broadcasted_iota(jnp.int32, (rows, 128), 1) // 32
    for pair in range(front // 256):
        a = inv_ref[:, pair * 256 : pair * 256 + 128].astype(F32)
        b = inv_ref[:, pair * 256 + 128 : pair * 256 + 256].astype(F32)
        for c in range(2):
            if c == 0:
                parts = [a, pltpu.roll(a, 96, 1), pltpu.roll(b, 64, 1), pltpu.roll(b, 32, 1)]
            else:
                parts = [pltpu.roll(a, 96, 1), pltpu.roll(a, 64, 1), pltpu.roll(b, 32, 1), b]
            v = jnp.where(
                lane == 0,
                parts[0],
                jnp.where(lane == 1, parts[1], jnp.where(lane == 2, parts[2], parts[3])),
            )
            at = c * (front // 2) + pair * 128
            out_ref[:rows, at : at + 128] = v.astype(BF)
    for i, ref in enumerate(got):
        out_ref[2 * rows : 3 * rows, i * n : (i + 1) * n] = ref[:rows, :]
        s = lax.rem(iy[0] + i, len(got))
        for j in range(len(got)):

            @pl.when(s == j)
            def _():
                out_ref[rows : 2 * rows, j * n : (j + 1) * n] = ref[rows + nk :, :]

    pre = sum(ref[rows : rows + nk, :].astype(F32) for ref in got).astype(BF)
    step = nk // len(got)
    for i in range(len(got)):
        out_ref[3 * rows :, i * n : (i + 1) * n] = pre[i * step : (i + 1) * step, :]


def mid_kernel(core, h_ref, m0_ref, m1_ref, c0_ref, c1_ref, y_ref, u_ref):
    nz, rows, front = m0_ref.shape
    zi, ncpl = nz * rows, u_ref.shape[-1]
    m0 = m0_ref[...].reshape(zi, front)
    m1 = m1_ref[...].reshape(zi, front)
    y = -(mm(h_ref[:, :zi], m0) + mm(h_ref[:, zi:], m1))
    y = y.astype(BF)
    y_ref[...] = y
    mine, other = by_core(core[0], y[:, : front // 2], y[:, front // 2 :])
    u = jnp.zeros(u_ref.shape[1:], F32)
    for half, ref in ((mine, c0_ref), (other, c1_ref)):
        for i in range(front // ncpl):
            block = ref[:, :, i * ncpl : (i + 1) * ncpl].reshape(zi, ncpl)
            u += mm(half[:, i * zi : (i + 1) * zi], block)
    u_ref[...] = jnp.broadcast_to(u.astype(BF)[None], u_ref.shape)


def select_kernel(at_ref, w_ref, out_ref):
    nz, rows, front = w_ref.shape
    zi, tile = nz * rows, out_ref.shape[0]
    ncol = out_ref.shape[1]
    at = at_ref[...]
    lane = lax.broadcasted_iota(jnp.int32, (tile, zi), 1)
    acc = jnp.zeros(out_ref.shape, F32)
    for i in range(front // ncol):
        hot = jnp.where(at - i * zi == lane, 1.0, 0.0).astype(BF)
        acc += mm(hot, w_ref[:, :, i * ncol : (i + 1) * ncol].reshape(zi, ncol))
    out_ref[...] = acc.astype(BF)


def root_kernel(nx, u_ref, r0_ref, r1_ref, pre_ref, y_ref, cpl_ref):
    n = u_ref.shape[-1]
    acc = pre_ref[...]
    sel = []
    for x in range(nx):
        u = sum(u_ref[j].astype(F32) for j in range(x, u_ref.shape[0], nx))
        sel.append(r0_ref[x * n : (x + 1) * n, :] + r1_ref[x * n : (x + 1) * n, :])
        acc -= mm(u.astype(BF), sel[x])
    y = acc.astype(BF)
    y_ref[...] = y
    for x in range(nx):
        cpl_ref[x] = mm_t(y, sel[x]).astype(BF)


def back_kernel(core, cp_ref, y0, y1, y2, y3, m0_ref, m1_ref, c0_ref, c1_ref, out_ref):
    nz, rows, front = m0_ref.shape
    zi, ncpl = nz * rows, cp_ref.shape[-1]
    cp = sum(cp_ref[j].astype(F32) for j in range(cp_ref.shape[0])).astype(BF)
    halves = []
    for ref in (c0_ref, c1_ref):
        parts = [
            mm_t(cp, ref[:, :, i * ncpl : (i + 1) * ncpl].reshape(zi, ncpl))
            for i in range(front // ncpl)
        ]
        halves.append(jnp.concatenate(parts, 1))
    full = jnp.concatenate(by_core(core[0], halves[0], halves[1]), 1)
    y = sum(r[...].astype(F32) for r in (y0, y1, y2, y3))
    w = (y - full).astype(BF)
    x0 = mm_t(w, m0_ref[...].reshape(zi, front))
    x1 = mm_t(w, m1_ref[...].reshape(zi, front))
    x = jnp.concatenate([x0, x1], 1).astype(BF)
    out_ref[...] = jnp.broadcast_to(x[None], out_ref.shape)


def leaf_kernel(parent, size, first, core, x0_ref, x1_ref, cw_ref, y_ref, out_ref):
    leaf = pl.program_id(0)
    half = x0_ref.shape[2] // 2
    x0 = x0_ref[0]
    x1 = jnp.concatenate([x1_ref[0, :, half:], x1_ref[0, :, :half]], 1)
    x = jnp.concatenate(by_core(core[0], x0, x1), 0)
    w = y_ref[0] - mm(x, cw_ref[0])
    lane = first[0] + lax.broadcasted_iota(jnp.int32, w.shape, 1)
    w = jnp.where(lane < size[leaf], w, 0.0).astype(BF)
    out_ref[...] = jnp.broadcast_to(w[None, None], out_ref.shape)


def body(
    leaf_grad,
    leaf_inv,
    leaf_cpl,
    leaf_size,
    leaf_parent,
    leaf_map,
    mid_grad,
    mid_inv,
    mid_cpl,
    mid_map,
    root_grad,
    root_inv,
):
    ny, nz, nc, nx = (lax.axis_size(a) for a in ("y", "z", "c", "x"))
    iy, iz, ic, ix = (lax.axis_index(a) for a in ("y", "z", "c", "x"))
    nl, share, order = leaf_inv.shape
    nk = leaf_grad.shape[1]
    hk = nk // nc
    rows, front = mid_inv.shape[1:]
    ncpl = leaf_cpl.shape[2]
    nmid = mid_map.shape[0]
    zi = nz * rows
    half = front // nc
    width = front // ny
    blk = front // nx
    core = ic.astype(jnp.int32).reshape(1)

    def pick(first, second):
        return jnp.where(ic == 0, first, second)

    def place(m, y0):
        c = (m // rows % nc) ^ ic
        z = m // (rows * nc) % nz
        y = (m // (rows * nc * nz) - y0) % ny
        return (c * ny + y) * zi + z * rows + m % rows

    def half_sum(v, turn=lambda t: t):
        lo, hi = v[..., :hk, :], v[..., hk:, :]
        return pick(lo, hi) + swap(turn(pick(hi, lo).astype(BF))).astype(F32)

    own = iy * zi + iz * rows

    with jax.named_scope("leaf_forward"):
        live = (ix * share + lax.iota(jnp.int32, share))[None, :] < leaf_size[:, None]
        live = live[:, None, :]
        inv4 = leaf_inv.reshape(nl, share, nx, share)
        part = jnp.einsum(
            "lkp,lpxq->xlkq", leaf_grad, inv4, preferred_element_type=F32
        ).astype(BF)
        leaf_y = jnp.where(live, jnp.sum(a2a(part, "x").astype(F32), 0), 0.0)
        leaf_yb = leaf_y.astype(BF)

    with jax.named_scope("gather"):
        place_x = ix.astype(jnp.int32).reshape(1)
        mine, rinv_x = pl.pallas_call(
            root_pack_kernel,
            grid_spec=pltpu.PrefetchScalarGridSpec(
                num_scalar_prefetch=1,
                grid=(1,),
                in_specs=[
                    pl.BlockSpec((rows, blk), lambda i, at: (0, at[0])),
                    pl.BlockSpec((nk, rows), lambda i, at: (0, 0)),
                    pl.BlockSpec((rows, ncpl), lambda i, at: (0, 0)),
                ],
                out_specs=[
                    pl.BlockSpec((2 * rows + nk, blk), lambda i, at: (0, 0)),
                    pl.BlockSpec((rows, blk), lambda i, at: (0, 0)),
                ],
            ),
            out_shape=[
                jax.ShapeDtypeStruct((2 * rows + nk, blk), BF),
                jax.ShapeDtypeStruct((rows, blk), BF),
            ],
            compiler_params=PARAMS,
            name="root_pack",
        )(place_x, root_inv, root_grad, mid_cpl[0])
        got = ahead(mine, "y")
        g = front // blk
        payload = pl.pallas_call(
            functools.partial(pack_kernel, nk),
            in_specs=[SM] + [VM] * 5,
            out_specs=VM,
            out_shape=jax.ShapeDtypeStruct((3 * rows + nk // g, front), BF),
            compiler_params=PARAMS,
            name="pack",
        )(iy.astype(jnp.int32).reshape(1), after(mid_inv[0], part), *got)
        wide = lax.all_gather(payload, "z", axis=0)

    with jax.named_scope("leaf_spread"):
        target = place(leaf_map, 0)
        hot = (target[:, :, None] == lax.iota(jnp.int32, front)).astype(BF)
        cpl_wide = jnp.einsum(
            "lcn,lpc->lnp", hot, leaf_cpl, preferred_element_type=F32
        ).astype(BF)
        parent_of = jnp.arange(nmid)[:, None] == leaf_parent[None, :]
        lhs = jnp.where(parent_of[:, None, :, None], leaf_yb.transpose(1, 0, 2)[None], 0)
        placed = jnp.einsum(
            "mlp,lnp->mn",
            lhs.reshape(nmid * nk, nl, share),
            cpl_wide,
            preferred_element_type=F32,
        ).reshape(nmid, nk, front)
        here = own + lax.iota(jnp.int32, rows)
        hot_here = (here[:, None] == lax.iota(jnp.int32, front)[None, :]).astype(BF)
        grad = mm(mid_grad[:, 0, :], hot_here)
        placed = placed - jnp.where(jnp.arange(nmid)[:, None, None] == ix, grad[None], 0.0)

    with jax.named_scope("contrib_sum"):
        s = half_sum(placed, flip).astype(BF)
        s = s.reshape(nx, hk, nc, ny, zi).transpose(3, 0, 1, 2, 4).reshape(ny * nx, hk, width)
        s_own = jnp.sum(a2a(s, ("y", "x")).astype(F32), 0).astype(BF)
        s = jnp.sum(spread(s_own, "z").astype(F32), 0)
        contrib = s.astype(BF)

    with jax.named_scope("gather"):
        w0 = after(wide, contrib)
        w1 = swap(w0)
        pre = jnp.sum(w0[:, 3 * rows :].astype(F32), 0)
        pre = half_sum(jnp.concatenate(jnp.split(pre, g, 1), 0))

        def part_of(i):
            return pl.BlockSpec((nz, rows, front), lambda *_: (0, i, 0))

        at = place(mid_map, iy).reshape(-1, 1)
        tile = 256

        rsel0 = pl.pallas_call(
            select_kernel,
            grid=(nmid * ncpl // tile,),
            in_specs=[pl.BlockSpec((tile, 1), lambda i: (i, 0)), part_of(2)],
            out_specs=pl.BlockSpec((tile, blk), lambda i: (i, 0)),
            out_shape=jax.ShapeDtypeStruct((nmid * ncpl, blk), BF),
            compiler_params=PARAMS,
            name="root_select",
        )(at, w0)
        contrib = after(contrib, rsel0)
        rsel1 = swap(rsel0)

    def whole(shape):
        return pl.BlockSpec(shape, lambda *_: (0,) * len(shape))

    with jax.named_scope("mid_forward"):
        part_y, u = pl.pallas_call(
            mid_kernel,
            grid=(1,),
            in_specs=[SM, whole((hk, width)), part_of(0), part_of(0), part_of(1), part_of(1)],
            out_specs=[whole((hk, front)), whole((ny * nx, hk, ncpl))],
            out_shape=[
                jax.ShapeDtypeStruct((hk, front), BF),
                jax.ShapeDtypeStruct((ny * nx, hk, ncpl), BF),
            ],
            compiler_params=PARAMS,
            name="mid_forward",
        )(core, contrib, w0, w1, w0, w1)
        u = a2a(u, ("y", "x"))

    with jax.named_scope("root"):
        root_y, coupled = pl.pallas_call(
            functools.partial(root_kernel, nx),
            in_specs=[VM] * 4,
            out_specs=[VM] * 2,
            out_shape=[
                jax.ShapeDtypeStruct((hk, blk), BF),
                jax.ShapeDtypeStruct((nx, hk, ncpl), BF),
            ],
            compiler_params=PARAMS,
            name="root",
        )(u, rsel0, rsel1, pre)
        ys = ahead(after(part_y, root_y), "y")
        coupled = a2a(coupled, "x")

    with jax.named_scope("mid_backward"):
        mx = pl.pallas_call(
            back_kernel,
            grid=(1,),
            in_specs=[SM, whole((nx, hk, ncpl))]
            + [whole((hk, front))] * ny
            + [part_of(0), part_of(0), part_of(1), part_of(1)],
            out_specs=whole((ny * nx, hk, width)),
            out_shape=jax.ShapeDtypeStruct((ny * nx, hk, width), BF),
            compiler_params=PARAMS,
            name="mid_backward",
        )(core, coupled, *ys, w0, w1, w0, w1)
        both = jnp.concatenate([rinv_x, swap(rinv_x)], 0)
        rx = sum(ahead(mm_t(root_y, both), "x"))
        mx = after(a2a(mx, ("y", "x")), rx).reshape(ny, nx, hk, nc, zi)
        mx = mx.transpose(1, 2, 3, 0, 4).reshape(nx, hk, front)
        mo = swap(mx)

    with jax.named_scope("leaf_backward"):
        w = pl.pallas_call(
            leaf_kernel,
            grid_spec=pltpu.PrefetchScalarGridSpec(
                num_scalar_prefetch=4,
                grid=(nl,),
                in_specs=[
                    pl.BlockSpec((1, hk, front), lambda i, parent, *_: (parent[i], 0, 0)),
                    pl.BlockSpec((1, hk, front), lambda i, parent, *_: (parent[i], 0, 0)),
                    pl.BlockSpec((1, front, share), lambda i, *_: (i, 0, 0)),
                    pl.BlockSpec((1, nk, share), lambda i, *_: (i, 0, 0)),
                ],
                out_specs=pl.BlockSpec((nx, 1, nk, share), lambda i, *_: (0, i, 0, 0)),
            ),
            out_shape=jax.ShapeDtypeStruct((nx, nl, nk, share), BF),
            compiler_params=PARAMS,
            name="leaf_backward",
        )(leaf_parent, leaf_size, (ix * share).astype(jnp.int32).reshape(1), core, mx, mo, cpl_wide, leaf_y)

    with jax.named_scope("outputs"):

        def mine_of(v, at):
            v = lax.dynamic_index_in_dim(v, ix, 0, keepdims=False)
            return lax.dynamic_slice(v, (0, at), (hk, rows))

        om = mine_of(mx, own), mine_of(mo, half + own)
        out_m = jnp.concatenate([pick(*om), pick(om[1], om[0])], 0)
        rx = after(rx, w)
        ro = swap(rx[:, rows:])
        out_r = jnp.concatenate(
            [pick(rx[:, :rows], ro), pick(ro, rx[:, :rows])], 0
        )

    with jax.named_scope("leaf_result"):
        w = a2a(w, "x")
        w, out_r = lax.optimization_barrier((w, out_r))
        leaf_x = jnp.einsum("xlkq,lpxq->lkp", w, inv4, preferred_element_type=F32)
    return leaf_x, out_m.astype(F32)[:, None, :], out_r


def solution(mesh):
    grid = Mesh(mesh.devices.reshape(4, 8, 2, 4), ("y", "z", "c", "x"))
    row = ("y", "z", "c")
    placed = (
        P(row, None, "x"),
        P(row, "x", None),
        P(row, "x", None),
        P(row),
        P(row),
        P(row, None),
        P(None, "x", row),
        P("x", row, None),
        P("x", row, None),
        P(),
        P(None, row),
        P(row, None),
    )
    return jax.shard_map(
        body,
        mesh=grid,
        in_specs=placed,
        out_specs=(P(row, None, "x"), P(None, "x", row), P(None, row)),
        check_vma=False,
    )
```

time: 208 us -> 169 us (0.81)
  blocking collectives: 66.3 us -> 29.5 us
  Pallas kernels: 0 us -> 28.4 us
  starting transfers between devices: 27.1 us -> 45.5 us
  matrix products: 25.7 us -> 12.8 us
  waiting for transfers between devices: 37.3 us -> 24.4 us
  other arithmetic: 18.1 us -> 5.37 us
  local copies, waits for them, and re-layouts: 17.8 us -> 7.74 us
    pallas_call x0 -> x7, Pallas kernels: none -> 28.4 us  [the longest x1 7.64 us: body(): pl.pallas_call(select_kernel, grid=(nmid * ncpl // tile,), in_specs=[pl.B...]
    all_to_all x3 -> x0, waiting for transfers between devices: 26 us -> none  [spread(): lax.all_to_all(jnp.broadcast_to(v[None], (n,) + v.shape), axes, 0, 0, til...]
    all_to_all x2 -> x0, blocking collectives: 23.2 us -> none  [spread(): lax.all_to_all(jnp.broadcast_to(v[None], (n,) + v.shape), axes, 0, 0, til...]
    all_to_all x1 -> x5, starting transfers between devices: 3.4 us -> 23.2 us  [a2a(): return lax.all_to_all(v, axes, 0, 0, tiled=True)]
    all_to_all x3 -> x2, blocking collectives: 43.1 us -> 29.5 us  [a2a(): return lax.all_to_all(v, axes, 0, 0, tiled=True)]
    all_to_all x3 -> x0, starting transfers between devices: 11.8 us -> none  [spread(): lax.all_to_all(jnp.broadcast_to(v[None], (n,) + v.shape), axes, 0, 0, til...]
    dot_general x6 -> x1, matrix products: 11.3 us -> 0.24 us  [mm(): return jnp.dot(a, b, preferred_element_type=F32)]
    ppermute x0 -> x9, starting transfers between devices: none -> 9.81 us  [ahead(): lax.ppermute(v, axis, [((i + k) % n, i) for i in range(n)])]
  transfers between devices with their start and end apart: 13 -> 22, of which waited for: 12 -> 13; matrix products, arithmetic and copies ran while one was open for 7% -> 12% of each run, Pallas kernels for 0% -> 9%
where the time goes in v2:
time: 169 us; the launch traced here: 168 us
  starting transfers between devices  45.5 us (27%)
  blocking collectives  29.5 us (17%)
  Pallas kernels  28.4 us (17%)
  waiting for transfers between devices  24.4 us (14%)
  between operations  14.4 us (9%)
  matrix products  12.8 us (8%)
  local copies, waits for them, and re-layouts  7.74 us (5%)
  other arithmetic  5.37 us (3%)
    all_to_all x2, blocking collectives, a2a(): return lax.all_to_all(v, axes, 0, 0, tiled=True)  29.5 us
    all_to_all x5, starting transfers between devices, a2a(): return lax.all_to_all(v, axes, 0, 0, tiled=True)  23.2 us
    ppermute x7, starting transfers between devices, swap(): return lax.ppermute(v, 'c', [(0, 1), (1, 0)])  12.5 us
    all_to_all x5, waiting for transfers between devices, a2a(): return lax.all_to_all(v, axes, 0, 0, tiled=True)  11.4 us
    ppermute x9, starting transfers between devices, ahead(): lax.ppermute(v, axis, [((i + k) % n, i) for i in range(n)])  9.81 us
    ppermute x9, waiting for transfers between devices, ahead(): lax.ppermute(v, axis, [((i + k) % n, i) for i in range(n)])  7.99 us
    pallas_call x1, Pallas kernels, body(): pl.pallas_call(select_kernel, grid=(nmid * ncpl // tile,), in_specs=[pl.B...  7.64 us
    pallas_call x1, Pallas kernels, body(): pl.pallas_call(leaf_kernel, grid_spec=pltpu.PrefetchScalarGridSpec(num_sc...  5.18 us
  transfers between devices with their start and end apart: 22, of which 13 were waited for; matrix products, arithmetic and copies ran while one was open for 12% of the time, Pallas kernels for 9%

profile of v2, /device:TPU:1, one launch (start us, length us, event | category | flops | bytes accessed | tf_op | source)
XLA Modules:
  0.0 168.1 jit_solution(8608424551638851397)
XLA Ops:
  8.9 3.6 %collective-permute-start.1 = (bf16[96,512]{1,0:T(8,128)(2,1)}, bf16[96,512]{1,0:T(8,128)(2,1)S(1)}, u32[]{:S(2)}, u32[]{:S(2)}) collective-permute-start(bf16[96,512]{1,0:T(8,128)(2,1)} %get-tuple-element.18.g0), channel_id=1, source_target_pairs={{64,0},{128,64},{192,128},{0,192},{65,1},{129,65},{193,129},{1,193... | collective-permute-start | bytes 294920 | tf_op jit(solution)/shard_map/gather/ppermute | solution.py:41
  17.8 2.7 %collective-permute-done.3.g3 = bf16[96,512]{1,0:T(8,128)(2,1)S(1)} collective-permute-done((bf16[96,512]{1,0:T(8,128)(2,1)}, bf16[96,512]{1,0:T(8,128)(2,1)S(1)}, u32[]{:S(2)}, u32[]{:S(2)}) %collective-permute-start.3) | collective-permute-done | bytes 98336 | tf_op jit(solution)/shard_map/gather/ppermute | solution.py:41
  21.1 2.1 %pack.1 = bf16[104,2048]{1,0:T(8,128)(2,1)} custom-call(s32[1]{0:T(128)} %bitcast.12.iy, bf16[32,2048]{1,0:T(8,128)(2,1)} %bitcast.80, bf16[96,512]{1,0:T(8,128)(2,1)} %get-tuple-element.18.g0, bf16[96,512]{1,0:T(8,128)(2,1)} %copy-done.6, bf16[96,512]{1,0:T(8,128)(2,1)} %copy-done.7, bf16[96,512]{1,0:T(8,128)(2,1)} %copy-done.8), custom_call_target="tpu_custom_call" | custom-call | tf_op jit(solution)/shard_map/gather/pack/pallas_call | solution.py:256
  24.0 4.0 %all-to-all-start = ((bf16[4,4,32,256]{3,2,1,0:T(8,128)(2,1)}), bf16[4,4,32,256]{3,2,1,0:T(8,128)(2,1)S(1)}, u32[]{:S(2)}, u32[]{:S(2)}) async-start(bf16[4,4,32,256]{3,2,1,0:T(8,128)(2,1)} %copy.35), calls=%async_computation | async-start | bytes 524288 | tf_op jit(solution)/shard_map/leaf_forward/all_to_all | solution.py:26
  28.5 5.1 %fusion.4.cw_ref = bf16[4,2048,256]{2,1,0:T(8,128)(2,1)} fusion(bf16[4,256,512]{2,1,0:T(8,128)(2,1)S(1)} %copy-done, s32[4,512]{1,0:T(4,128)S(1)} %fusion.42), kind=kOutput, calls=%fused_computation.5 | convolution fusion | flops 2153775104 | bytes 5251072 | tf_op jit(solution)/shard_map/leaf_spread/lcn,lpc->lnp/dot_general | solution.py:269
  34.3 3.8 %fusion.8 = f32[4,32,2048]{2,1,0:T(8,128)S(1)} fusion(bf16[4,2048,256]{2,1,0:T(8,128)(2,1)} %fusion.4.cw_ref, f32[32,2048]{1,0:T(8,128)S(1)} %convolution_bitcast_fusion, pred[4]{0:T(512)(128)(4,1)S(1)} %iota_compare_fusion.7, pred[4,4]{1,0:T(4,128)(4,1)S(1)} %iota_compare_fusion.6, bf16[32,4,256]{2,0,1:T(8,128)(2,1)S(1)} %get-tuple-element.43), kind=kOutput, calls=%fused_computation.7 | convolution fusion | flops 537526272 | bytes 5570580 | tf_op jit(solution)/shard_map/leaf_spread/mlp,lnp->mn/dot_general | solution.py:274
  38.2 2.4 %collective-permute-start = (bf16[4,16,2048]{2,1,0:T(8,128)(2,1)S(1)}, bf16[4,16,2048]{2,1,0:T(8,128)(2,1)S(1)}, u32[]{:S(2)}, u32[]{:S(2)}) collective-permute-start(bf16[4,16,2048]{2,1,0:T(8,128)(2,1)S(1)} %pad_maximum_fusion), channel_id=1, source_target_pairs={{0,4},{4,0},{1,5},{5,1},{2,6},{6,2},{3,7},{7,3},{8,12},{12,8},{9,1... | collective-permute-start | bytes 786440 | tf_op jit(solution)/shard_map/contrib_sum/ppermute | solution.py:35
  42.5 11.5 %all_to_all.35 = bf16[16,16,512]{2,1,0:T(8,128)(2,1)S(1)} all-to-all(bf16[16,16,512]{2,1,0:T(8,128)(2,1)S(1)} %reshape.154), channel_id=1, replica_groups=mesh['y'=4,'z'=8,'c'=2,'x'=4] {'y','x'}, dimensions={0} | all-to-all | bytes 524288 | tf_op jit(solution)/shard_map/contrib_sum/all_to_all | solution.py:26
  54.1 17.9 %all_to_all.36 = bf16[8,16,512]{2,1,0:T(8,128)(2,1)S(1)} all-to-all(bf16[8,16,512]{2,1,0:T(8,128)(2,1)S(1)} %broadcast_in_dim.80), channel_id=1, replica_groups=mesh['y'=4,'z'=8,'c'=2,'x'=4] {'z'}, dimensions={0} | all-to-all | bytes 262144 | tf_op jit(solution)/shard_map/contrib_sum/all_to_all | solution.py:26
  76.8 7.6 %root_select.1.r0_ref = bf16[2048,512]{1,0:T(8,128)(2,1)} custom-call(s32[2048,1]{1,0:T(8,128)} %bitcast.77, bf16[8,104,2048]{2,1,0:T(8,128)(2,1)} %bitcast.69), custom_call_target="tpu_custom_call" | custom-call | tf_op jit(solution)/shard_map/gather/root_select/pallas_call | solution.py:304
  85.5 3.6 %mid_forward.1 = (bf16[16,2048]{1,0:T(8,128)(2,1)}, bf16[16,16,512]{2,1,0:T(8,128)(2,1)}) custom-call(s32[1]{0:T(128)} %bitcast.1.core, bf16[16,512]{1,0:T(8,128)(2,1)} %reduce_sum.44.h_ref, bf16[8,104,2048]{2,1,0:T(8,128)(2,1)} %bitcast.71, bf16[8,104,2048]{2,1,0:T(8,128)(2,1)} %collective-permute-done.4.m1_ref.c1_ref, bf16[8,104,2048]{2,1,0:T(8,128)(2,1)} %bitcast.72, ...), custom_call_target="tpu_custom_call" | custom-call | tf_op jit(solution)/shard_map/mid_forward/mid_forward/pallas_call | solution.py:320
  89.1 6.5 %all-to-all-start.3 = ((bf16[16,16,512]{2,1,0:T(8,128)(2,1)}), bf16[16,16,512]{2,1,0:T(8,128)(2,1)S(1)}, u32[]{:S(2)}, u32[]{:S(2)}) async-start(bf16[16,16,512]{2,1,0:T(8,128)(2,1)} %get-tuple-element.21), calls=%async_computation.3 | async-start | bytes 524288 | tf_op jit(solution)/shard_map/mid_forward/all_to_all | solution.py:26
  98.1 5.4 %all-to-all-done.3.u_ref = bf16[16,16,512]{2,1,0:T(8,128)(2,1)S(1)} async-done(((bf16[16,16,512]{2,1,0:T(8,128)(2,1)}), bf16[16,16,512]{2,1,0:T(8,128)(2,1)S(1)}, u32[]{:S(2)}, u32[]{:S(2)}) %all-to-all-start.3) | async-done | bytes 262176 | tf_op jit(solution)/shard_map/mid_forward/all_to_all | solution.py:26
  104.3 3.9 %root.1 = (bf16[16,512]{1,0:T(8,128)(2,1)}, bf16[4,16,512]{2,1,0:T(8,128)(2,1)}) custom-call(bf16[16,16,512]{2,1,0:T(8,128)(2,1)} %copy-done.4, bf16[2048,512]{1,0:T(8,128)(2,1)} %root_select.1.r0_ref, bf16[2048,512]{1,0:T(8,128)(2,1)} %copy-done.2, f32[16,512]{1,0:T(8,128)} %convert_add_fusion.pre_ref), custom_call_target="tpu_custom_call" | custom-call | tf_op jit(solution)/shard_map/root/root/pallas_call | solution.py:335
  109.6 3.3 %all-to-all-start.4 = ((bf16[4,16,512]{2,1,0:T(8,128)(2,1)}), bf16[4,16,512]{2,1,0:T(8,128)(2,1)S(1)}, u32[]{:S(2)}, u32[]{:S(2)}) async-start(bf16[4,16,512]{2,1,0:T(8,128)(2,1)} %get-tuple-element.22), calls=%async_computation.4 | async-start | bytes 131072 | tf_op jit(solution)/shard_map/root/all_to_all | solution.py:26
  113.0 2.6 %collective-permute-start.10 = (bf16[32,512]{1,0:T(8,128)(2,1)S(1)}, bf16[32,512]{1,0:T(8,128)(2,1)S(1)}, u32[]{:S(2)}, u32[]{:S(2)}) collective-permute-start(bf16[32,512]{1,0:T(8,128)(2,1)S(1)} %copy-done.18), channel_id=1, source_target_pairs={{0,4},{4,0},{1,5},{5,1},{2,6},{6,2},{3,7},{7,3},{8,12},{12,8},{9,1... | collective-permute-start | bytes 98312 | tf_op jit(solution)/shard_map/mid_backward/ppermute | solution.py:35
  118.7 4.3 %mid_backward.1 = bf16[16,16,512]{2,1,0:T(8,128)(2,1)} custom-call(s32[1]{0:T(128)} %bitcast.1.core, bf16[4,16,512]{2,1,0:T(8,128)(2,1)} %copy-done.5, bf16[16,2048]{1,0:T(8,128)(2,1)} %get-tuple-element.25.y0, bf16[16,2048]{1,0:T(8,128)(2,1)} %copy-done.10, bf16[16,2048]{1,0:T(8,128)(2,1)} %copy-done.11, bf16[16,2048]{1,0:T(8,128)(2,1)} %copy-done.12, ...), custom_call_target="tpu_custom_call" | custom-call | tf_op jit(solution)/shard_map/mid_backward/mid_backward/pallas_call | solution.py:350
  122.9 6.0 %all-to-all-start.5 = ((bf16[16,16,512]{2,1,0:T(8,128)(2,1)}), bf16[16,16,512]{2,1,0:T(8,128)(2,1)S(1)}, u32[]{:S(2)}, u32[]{:S(2)}) async-start(bf16[16,16,512]{2,1,0:T(8,128)(2,1)} %mid_backward.1), calls=%async_computation.5 | async-start | bytes 524288 | tf_op jit(solution)/shard_map/mid_backward/all_to_all | solution.py:26
  129.1 2.6 %collective-permute-start.11 = (f32[16,64]{1,0:T(8,128)S(1)}, f32[16,64]{1,0:T(8,128)S(1)}, u32[]{:S(2)}, u32[]{:S(2)}) collective-permute-start(f32[16,64]{1,0:T(8,128)S(1)} %fusion.31), channel_id=1, source_target_pairs={{1,0},{2,1},{3,2},{0,3},{5,4},{6,5},{7,6},{4,7},{9,8},{10,9},{11,1... | collective-permute-start | bytes 12296 | tf_op jit(solution)/shard_map/mid_backward/ppermute | solution.py:41
  132.9 2.7 %collective-permute-done.12 = f32[16,64]{1,0:T(8,128)S(1)} collective-permute-done((f32[16,64]{1,0:T(8,128)S(1)}, f32[16,64]{1,0:T(8,128)S(1)}, u32[]{:S(2)}, u32[]{:S(2)}) %collective-permute-start.12) | collective-permute-done | bytes 4128 | tf_op jit(solution)/shard_map/mid_backward/ppermute | solution.py:41
  138.7 5.1 %collective-permute-start.14 = (bf16[4,16,2048]{2,1,0:T(8,128)(2,1)S(1)}, bf16[4,16,2048]{2,1,0:T(8,128)(2,1)}, u32[]{:S(2)}, u32[]{:S(2)}) collective-permute-start(bf16[4,16,2048]{2,1,0:T(8,128)(2,1)S(1)} %reshape.159.x0_ref), channel_id=1, source_target_pairs={{0,4},{4,0},{1,5},{5,1},{2,6},{6,2},{3,7},{7,3},{8,12},{12,8},{9,1... | collective-permute-start | bytes 786440 | tf_op jit(solution)/shard_map/mid_backward/ppermute | solution.py:35
  145.1 5.2 %leaf_backward.1 = bf16[4,4,32,256]{3,2,1,0:T(8,128)(2,1)} custom-call(s32[4]{0:T(128)} %parent.1, s32[4]{0:T(128)} %size.1, s32[1]{0:T(128)} %bitcast.first, s32[1]{0:T(128)} %bitcast.1.core, bf16[4,16,2048]{2,1,0:T(8,128)(2,1)} %copy-done.3, bf16[4,16,2048]{2,1,0:T(8,128)(2,1)} %collective-permute-done.14.x1_ref, bf16[4,2048,256]{2,1,0:T(8,128)(2,1)} %fusion.4.cw_ref, ...), custom_call_target="tpu_custom_call" | custom-call | tf_op jit(solution)/shard_map/leaf_backward/leaf_backward/pallas_call | solution.py:368
  150.3 3.4 %all-to-all-start.6 = ((bf16[4,4,32,256]{3,2,1,0:T(8,128)(2,1)}), bf16[4,4,32,256]{3,2,1,0:T(8,128)(2,1)S(1)}, u32[]{:S(2)}, u32[]{:S(2)}) async-start(bf16[4,4,32,256]{3,2,1,0:T(8,128)(2,1)} %leaf_backward.1), calls=%async_computation.6 | async-start | bytes 524288 | tf_op jit(solution)/shard_map/leaf_result/all_to_all | solution.py:26
  156.2 3.6 %all-to-all-done.6 = bf16[4,4,32,256]{3,2,1,0:T(8,128)(2,1)S(1)} async-done(((bf16[4,4,32,256]{3,2,1,0:T(8,128)(2,1)}), bf16[4,4,32,256]{3,2,1,0:T(8,128)(2,1)S(1)}, u32[]{:S(2)}, u32[]{:S(2)}) %all-to-all-start.6) | async-done | bytes 262176 | tf_op jit(solution)/shard_map/leaf_result/all_to_all | solution.py:26
  (111 shorter events, 34.7 us)
Async XLA Ops:
  7.2 67.1 %all-gather.3.cloned.1.call-start = ((), (), s32[]{:S(2)}) async-start(), calls=%async_computation.7 | async-start | bytes 3833856 | tf_op jit(solution)/shard_map/gather/all_gather | solution.py:264
  8.9 6.7 %collective-permute-start.1 = (bf16[96,512]{1,0:T(8,128)(2,1)}, bf16[96,512]{1,0:T(8,128)(2,1)S(1)}, u32[]{:S(2)}, u32[]{:S(2)}) collective-permute-start(bf16[96,512]{1,0:T(8,128)(2,1)} %get-tuple-element.18.g0), channel_id=1, source_target_pairs={{64,0},{128,64},{192,128},{0,192},{65,1},{129,65},{193,129},{1,193... | collective-permute-start | bytes 294920 | tf_op jit(solution)/shard_map/gather/ppermute | solution.py:41
  12.5 5.3 %collective-permute-start.2 = (bf16[96,512]{1,0:T(8,128)(2,1)}, bf16[96,512]{1,0:T(8,128)(2,1)S(1)}, u32[]{:S(2)}, u32[]{:S(2)}) collective-permute-start(bf16[96,512]{1,0:T(8,128)(2,1)} %get-tuple-element.18.g0), channel_id=1, source_target_pairs={{128,0},{192,64},{0,128},{64,192},{129,1},{193,65},{1,129},{65,193... | collective-permute-start | bytes 294920 | tf_op jit(solution)/shard_map/gather/ppermute | solution.py:41
  12.8 7.7 %collective-permute-start.3 = (bf16[96,512]{1,0:T(8,128)(2,1)}, bf16[96,512]{1,0:T(8,128)(2,1)S(1)}, u32[]{:S(2)}, u32[]{:S(2)}) collective-permute-start(bf16[96,512]{1,0:T(8,128)(2,1)} %get-tuple-element.18.g0), channel_id=1, source_target_pairs={{192,0},{0,64},{64,128},{128,192},{193,1},{1,65},{65,129},{129,193... | collective-permute-start | bytes 294920 | tf_op jit(solution)/shard_map/gather/ppermute | solution.py:41
  24.0 9.5 %all-to-all-start = ((bf16[4,4,32,256]{3,2,1,0:T(8,128)(2,1)}), bf16[4,4,32,256]{3,2,1,0:T(8,128)(2,1)S(1)}, u32[]{:S(2)}, u32[]{:S(2)}) async-start(bf16[4,4,32,256]{3,2,1,0:T(8,128)(2,1)} %copy.35), calls=%async_computation | async-start | bytes 524288 | tf_op jit(solution)/shard_map/leaf_forward/all_to_all | solution.py:26
  38.1 37.2 %copy-start.15 = (s32[4,512]{1,0:T(4,128)S(1)}, s32[4,512]{1,0:T(4,128)}, u32[]{:S(2)}) copy-start(s32[4,512]{1,0:T(4,128)} %param.21) | copy-start | bytes 24580
  38.2 3.5 %collective-permute-start = (bf16[4,16,2048]{2,1,0:T(8,128)(2,1)S(1)}, bf16[4,16,2048]{2,1,0:T(8,128)(2,1)S(1)}, u32[]{:S(2)}, u32[]{:S(2)}) collective-permute-start(bf16[4,16,2048]{2,1,0:T(8,128)(2,1)S(1)} %pad_maximum_fusion), channel_id=1, source_target_pairs={{0,4},{4,0},{1,5},{5,1},{2,6},{6,2},{3,7},{7,3},{8,12},{12,8},{9,1... | collective-permute-start | bytes 786440 | tf_op jit(solution)/shard_map/contrib_sum/ppermute | solution.py:35
  74.4 11.1 %collective-permute-start.4 = (bf16[8,104,2048]{2,1,0:T(8,128)(2,1)}, bf16[8,104,2048]{2,1,0:T(8,128)(2,1)}, u32[]{:S(2)}, u32[]{:S(2)}) collective-permute-start(bf16[8,104,2048]{2,1,0:T(8,128)(2,1)} %bitcast.68), channel_id=1, source_target_pairs={{0,4},{4,0},{1,5},{5,1},{2,6},{6,2},{3,7},{7,3},{8,12},{12,8},{9,1... | collective-permute-start | bytes 10223624 | tf_op jit(solution)/shard_map/gather/ppermute | solution.py:35
  84.4 13.7 %collective-permute-start.5 = (bf16[2048,512]{1,0:T(8,128)(2,1)}, bf16[2048,512]{1,0:T(8,128)(2,1)S(1)}, u32[]{:S(2)}, u32[]{:S(2)}) collective-permute-start(bf16[2048,512]{1,0:T(8,128)(2,1)} %root_select.1.r0_ref), channel_id=1, source_target_pairs={{0,4},{4,0},{1,5},{5,1},{2,6},{6,2},{3,7},{7,3},{8,12},{12,8},{9,1... | collective-permute-start | bytes 6291464 | tf_op jit(solution)/shard_map/gather/ppermute | solution.py:35
  89.1 14.5 %all-to-all-start.3 = ((bf16[16,16,512]{2,1,0:T(8,128)(2,1)}), bf16[16,16,512]{2,1,0:T(8,128)(2,1)S(1)}, u32[]{:S(2)}, u32[]{:S(2)}) async-start(bf16[16,16,512]{2,1,0:T(8,128)(2,1)} %get-tuple-element.21), calls=%async_computation.3 | async-start | bytes 524288 | tf_op jit(solution)/shard_map/mid_forward/all_to_all | solution.py:26
  95.6 1.9 %collective-permute-start.6 = (bf16[16,512]{1,0:T(8,128)(2,1)S(1)}, bf16[16,512]{1,0:T(8,128)(2,1)S(1)}, u32[]{:S(2)}, u32[]{:S(2)}) collective-permute-start(bf16[16,512]{1,0:T(8,128)(2,1)S(1)} %select_convert_fusion.1), channel_id=1, source_target_pairs={{0,4},{4,0},{1,5},{5,1},{2,6},{6,2},{3,7},{7,3},{8,12},{12,8},{9,1... | collective-permute-start | bytes 49160 | tf_op jit(solution)/shard_map/gather/ppermute | solution.py:35
  108.2 9.2 %collective-permute-start.7 = (bf16[16,2048]{1,0:T(8,128)(2,1)S(1)}, bf16[16,2048]{1,0:T(8,128)(2,1)S(1)}, u32[]{:S(2)}, u32[]{:S(2)}) collective-permute-start(bf16[16,2048]{1,0:T(8,128)(2,1)S(1)} %copy-done.9), channel_id=1, source_target_pairs={{64,0},{128,64},{192,128},{0,192},{65,1},{129,65},{193,129},{1,193... | collective-permute-start | bytes 196616 | tf_op jit(solution)/shard_map/root/ppermute | solution.py:41
  108.7 8.6 %collective-permute-start.8 = (bf16[16,2048]{1,0:T(8,128)(2,1)S(1)}, bf16[16,2048]{1,0:T(8,128)(2,1)S(1)}, u32[]{:S(2)}, u32[]{:S(2)}) collective-permute-start(bf16[16,2048]{1,0:T(8,128)(2,1)S(1)} %copy-done.9), channel_id=1, source_target_pairs={{128,0},{192,64},{0,128},{64,192},{129,1},{193,65},{1,129},{65,193... | collective-permute-start | bytes 196616 | tf_op jit(solution)/shard_map/root/ppermute | solution.py:41
  109.1 8.3 %collective-permute-start.9 = (bf16[16,2048]{1,0:T(8,128)(2,1)S(1)}, bf16[16,2048]{1,0:T(8,128)(2,1)S(1)}, u32[]{:S(2)}, u32[]{:S(2)}) collective-permute-start(bf16[16,2048]{1,0:T(8,128)(2,1)S(1)} %copy-done.9), channel_id=1, source_target_pairs={{192,0},{0,64},{64,128},{128,192},{193,1},{1,65},{65,129},{129,193... | collective-permute-start | bytes 196616 | tf_op jit(solution)/shard_map/root/ppermute | solution.py:41
  109.6 7.7 %all-to-all-start.4 = ((bf16[4,16,512]{2,1,0:T(8,128)(2,1)}), bf16[4,16,512]{2,1,0:T(8,128)(2,1)S(1)}, u32[]{:S(2)}, u32[]{:S(2)}) async-start(bf16[4,16,512]{2,1,0:T(8,128)(2,1)} %get-tuple-element.22), calls=%async_computation.4 | async-start | bytes 131072 | tf_op jit(solution)/shard_map/root/all_to_all | solution.py:26
  113.0 16.0 %collective-permute-start.10 = (bf16[32,512]{1,0:T(8,128)(2,1)S(1)}, bf16[32,512]{1,0:T(8,128)(2,1)S(1)}, u32[]{:S(2)}, u32[]{:S(2)}) collective-permute-start(bf16[32,512]{1,0:T(8,128)(2,1)S(1)} %copy-done.18), channel_id=1, source_target_pairs={{0,4},{4,0},{1,5},{5,1},{2,6},{6,2},{3,7},{7,3},{8,12},{12,8},{9,1... | collective-permute-start | bytes 98312 | tf_op jit(solution)/shard_map/mid_backward/ppermute | solution.py:35
  122.9 13.5 %all-to-all-start.5 = ((bf16[16,16,512]{2,1,0:T(8,128)(2,1)}), bf16[16,16,512]{2,1,0:T(8,128)(2,1)S(1)}, u32[]{:S(2)}, u32[]{:S(2)}) async-start(bf16[16,16,512]{2,1,0:T(8,128)(2,1)} %mid_backward.1), calls=%async_computation.5 | async-start | bytes 524288 | tf_op jit(solution)/shard_map/mid_backward/all_to_all | solution.py:26
  129.1 3.9 %collective-permute-start.11 = (f32[16,64]{1,0:T(8,128)S(1)}, f32[16,64]{1,0:T(8,128)S(1)}, u32[]{:S(2)}, u32[]{:S(2)}) collective-permute-start(f32[16,64]{1,0:T(8,128)S(1)} %fusion.31), channel_id=1, source_target_pairs={{1,0},{2,1},{3,2},{0,3},{5,4},{6,5},{7,6},{4,7},{9,8},{10,9},{11,1... | collective-permute-start | bytes 12296 | tf_op jit(solution)/shard_map/mid_backward/ppermute | solution.py:41
  131.6 4.0 %collective-permute-start.12 = (f32[16,64]{1,0:T(8,128)S(1)}, f32[16,64]{1,0:T(8,128)S(1)}, u32[]{:S(2)}, u32[]{:S(2)}) collective-permute-start(f32[16,64]{1,0:T(8,128)S(1)} %fusion.31), channel_id=1, source_target_pairs={{2,0},{3,1},{0,2},{1,3},{6,4},{7,5},{4,6},{5,7},{10,8},{11,9},{8,1... | collective-permute-start | bytes 12296 | tf_op jit(solution)/shard_map/mid_backward/ppermute | solution.py:41
  132.2 3.7 %collective-permute-start.13 = (f32[16,64]{1,0:T(8,128)S(1)}, f32[16,64]{1,0:T(8,128)S(1)}, u32[]{:S(2)}, u32[]{:S(2)}) collective-permute-start(f32[16,64]{1,0:T(8,128)S(1)} %fusion.31), channel_id=1, source_target_pairs={{3,0},{0,1},{1,2},{2,3},{7,4},{4,5},{5,6},{6,7},{11,8},{8,9},{9,10... | collective-permute-start | bytes 12296 | tf_op jit(solution)/shard_map/mid_backward/ppermute | solution.py:41
  136.5 23.3 %copy-start.1 = (bf16[4,256,1024]{2,1,0:T(8,128)(2,1)S(1)}, bf16[4,256,1024]{2,1,0:T(8,128)(2,1)}, u32[]{:S(2)}) copy-start(bf16[4,256,1024]{2,1,0:T(8,128)(2,1)} %param.13) | copy-start | bytes 6291460
  138.7 6.4 %collective-permute-start.14 = (bf16[4,16,2048]{2,1,0:T(8,128)(2,1)S(1)}, bf16[4,16,2048]{2,1,0:T(8,128)(2,1)}, u32[]{:S(2)}, u32[]{:S(2)}) collective-permute-start(bf16[4,16,2048]{2,1,0:T(8,128)(2,1)S(1)} %reshape.159.x0_ref), channel_id=1, source_target_pairs={{0,4},{4,0},{1,5},{5,1},{2,6},{6,2},{3,7},{7,3},{8,12},{12,8},{9,1... | collective-permute-start | bytes 786440 | tf_op jit(solution)/shard_map/mid_backward/ppermute | solution.py:35
  150.3 9.5 %all-to-all-start.6 = ((bf16[4,4,32,256]{3,2,1,0:T(8,128)(2,1)}), bf16[4,4,32,256]{3,2,1,0:T(8,128)(2,1)S(1)}, u32[]{:S(2)}, u32[]{:S(2)}) async-start(bf16[4,4,32,256]{3,2,1,0:T(8,128)(2,1)} %leaf_backward.1), calls=%async_computation.6 | async-start | bytes 524288 | tf_op jit(solution)/shard_map/leaf_result/all_to_all | solution.py:26
  153.8 1.8 %collective-permute-start.15 = (f32[16,32]{1,0:T(8,128)S(1)}, f32[16,32]{1,0:T(8,128)S(1)}, u32[]{:S(2)}, u32[]{:S(2)}) collective-permute-start(f32[16,32]{1,0:T(8,128)S(1)} %slice.32), channel_id=1, source_target_pairs={{0,4},{4,0},{1,5},{5,1},{2,6},{6,2},{3,7},{7,3},{8,12},{12,8},{9,1... | collective-permute-start | bytes 6152 | tf_op jit(solution)/shard_map/outputs/ppermute | solution.py:35
  (18 other events, 162.5 us)
Sparse Core Ops, SparseCore 0:
  23.4 50.9 all-gather.2

commit v3 on v2

--- a/solution.py
+++ b/solution.py
@@ -11,7 +11,7 @@
 F32 = jnp.float32
 VM = pl.BlockSpec(memory_space=pltpu.VMEM)
 SM = pl.BlockSpec(memory_space=pltpu.SMEM)
-PARAMS = pltpu.CompilerParams(vmem_limit_bytes=56 * 2**20)
+PARAMS = pltpu.CompilerParams(vmem_limit_bytes=60 * 2**20)
 
 
 def mm(a, b):
@@ -119,7 +119,7 @@
     nz, rows, front = w_ref.shape
     zi, tile = nz * rows, out_ref.shape[0]
     ncol = out_ref.shape[1]
-    at = at_ref[...]
+    at = jnp.broadcast_to(at_ref[0], (zi, tile)).T
     lane = lax.broadcasted_iota(jnp.int32, (tile, zi), 1)
     acc = jnp.zeros(out_ref.shape, F32)
     for i in range(front // ncol):
@@ -128,7 +128,7 @@
     out_ref[...] = acc.astype(BF)
 
 
-def root_kernel(nx, u_ref, r0_ref, r1_ref, pre_ref, y_ref, cpl_ref):
+def root_kernel(nx, u_ref, r0_ref, r1_ref, pre_ref, w0_ref, w1_ref, ly_ref, y_ref, cpl_ref):
     n = u_ref.shape[-1]
     acc = pre_ref[...]
     sel = []
@@ -138,14 +138,25 @@
         acc -= mm(u.astype(BF), sel[x])
     y = acc.astype(BF)
     y_ref[...] = y
+    both = jnp.concatenate([w0_ref[...], w1_ref[...]], 0)
+    both = jnp.concatenate([both, jnp.zeros((128 - both.shape[0], both.shape[1]), BF)], 0)
+    part = mm_t(y, both).astype(BF)
+    hk = y.shape[0]
+    share = ly_ref.shape[2]
     for x in range(nx):
-        cpl_ref[x] = mm_t(y, sel[x]).astype(BF)
+        cpl_ref[x, :hk, :n] = mm_t(y, sel[x]).astype(BF)
+        cpl_ref[x, :hk, n:] = part
+        for i in range(ly_ref.shape[0]):
+            for h in range(2):
+                cpl_ref[x, (i + 1) * hk : (i + 2) * hk, h * share : (h + 1) * share] = ly_ref[
+                    i, h * hk : (h + 1) * hk, :
+                ]
 
 
 def back_kernel(core, cp_ref, y0, y1, y2, y3, m0_ref, m1_ref, c0_ref, c1_ref, out_ref):
     nz, rows, front = m0_ref.shape
-    zi, ncpl = nz * rows, cp_ref.shape[-1]
-    cp = sum(cp_ref[j].astype(F32) for j in range(cp_ref.shape[0])).astype(BF)
+    zi, ncpl = nz * rows, cp_ref.shape[-1] - 128
+    cp = sum(cp_ref[j, :, :ncpl].astype(F32) for j in range(cp_ref.shape[0])).astype(BF)
     halves = []
     for ref in (c0_ref, c1_ref):
         parts = [
@@ -162,16 +173,18 @@
     out_ref[...] = jnp.broadcast_to(x[None], out_ref.shape)
 
 
-def leaf_kernel(parent, size, first, core, x0_ref, x1_ref, cw_ref, y_ref, out_ref):
-    leaf = pl.program_id(0)
+def leaf_kernel(parent, core, x0_ref, x1_ref, at_ref, n_ref, base_ref, out_ref):
     half = x0_ref.shape[2] // 2
-    x0 = x0_ref[0]
+    ncpl, chunk = at_ref.shape[2], 256
     x1 = jnp.concatenate([x1_ref[0, :, half:], x1_ref[0, :, :half]], 1)
-    x = jnp.concatenate(by_core(core[0], x0, x1), 0)
-    w = y_ref[0] - mm(x, cw_ref[0])
-    lane = first[0] + lax.broadcasted_iota(jnp.int32, w.shape, 1)
-    w = jnp.where(lane < size[leaf], w, 0.0).astype(BF)
-    out_ref[...] = jnp.broadcast_to(w[None, None], out_ref.shape)
+    x = jnp.concatenate(by_core(core[0], x0_ref[0], x1), 0)
+    at = at_ref[0]
+    place = lax.broadcasted_iota(jnp.int32, (chunk, ncpl), 0)
+    acc = jnp.zeros((x.shape[0], ncpl), F32)
+    for i in range(x.shape[1] // chunk):
+        hot = jnp.where(at - i * chunk == place, 1.0, 0.0).astype(BF)
+        acc += mm(x[:, i * chunk : (i + 1) * chunk], hot)
+    out_ref[0] = base_ref[0] - mm_t(acc.astype(BF), n_ref[0])
 
 
 def body(
@@ -251,6 +264,7 @@
             compiler_params=PARAMS,
             name="root_pack",
         )(place_x, root_inv, root_grad, mid_cpl[0])
+        rinv_o = swap(rinv_x)
         got = ahead(mine, "y")
         g = front // blk
         payload = pl.pallas_call(
@@ -288,23 +302,21 @@
         s_own = jnp.sum(a2a(s, ("y", "x")).astype(F32), 0).astype(BF)
         s = jnp.sum(spread(s_own, "z").astype(F32), 0)
         contrib = s.astype(BF)
+        cpl_all = lax.all_gather(after(leaf_cpl, s_own), "x", axis=0)
 
     with jax.named_scope("gather"):
         w0 = after(wide, contrib)
         w1 = swap(w0)
-        pre = jnp.sum(w0[:, 3 * rows :].astype(F32), 0)
-        pre = half_sum(jnp.concatenate(jnp.split(pre, g, 1), 0))
-
         def part_of(i):
             return pl.BlockSpec((nz, rows, front), lambda *_: (0, i, 0))
 
-        at = place(mid_map, iy).reshape(-1, 1)
         tile = 256
+        at = place(mid_map, iy).reshape(-1, 1, tile)
 
         rsel0 = pl.pallas_call(
             select_kernel,
             grid=(nmid * ncpl // tile,),
-            in_specs=[pl.BlockSpec((tile, 1), lambda i: (i, 0)), part_of(2)],
+            in_specs=[pl.BlockSpec((1, 1, tile), lambda i: (i, 0, 0)), part_of(2)],
             out_specs=pl.BlockSpec((tile, blk), lambda i: (i, 0)),
             out_shape=jax.ShapeDtypeStruct((nmid * ncpl, blk), BF),
             compiler_params=PARAMS,
@@ -329,20 +341,22 @@
             compiler_params=PARAMS,
             name="mid_forward",
         )(core, contrib, w0, w1, w0, w1)
+        pre = jnp.sum(after(w0, part_y)[:, 3 * rows :].astype(F32), 0)
+        pre = half_sum(jnp.concatenate(jnp.split(pre, g, 1), 0))
         u = a2a(u, ("y", "x"))
 
     with jax.named_scope("root"):
         root_y, coupled = pl.pallas_call(
             functools.partial(root_kernel, nx),
-            in_specs=[VM] * 4,
+            in_specs=[VM] * 7,
             out_specs=[VM] * 2,
             out_shape=[
                 jax.ShapeDtypeStruct((hk, blk), BF),
-                jax.ShapeDtypeStruct((nx, hk, ncpl), BF),
+                jax.ShapeDtypeStruct((nx, hk * (1 + nl), ncpl + 128), BF),
             ],
             compiler_params=PARAMS,
             name="root",
-        )(u, rsel0, rsel1, pre)
+        )(u, rsel0, rsel1, pre, rinv_x, rinv_o, leaf_yb)
         ys = ahead(after(part_y, root_y), "y")
         coupled = a2a(coupled, "x")
 
@@ -350,7 +364,7 @@
         mx = pl.pallas_call(
             back_kernel,
             grid=(1,),
-            in_specs=[SM, whole((nx, hk, ncpl))]
+            in_specs=[SM, whole((nx, hk, ncpl + 128))]
             + [whole((hk, front))] * ny
             + [part_of(0), part_of(0), part_of(1), part_of(1)],
             out_specs=whole((ny * nx, hk, width)),
@@ -358,30 +372,41 @@
             compiler_params=PARAMS,
             name="mid_backward",
         )(core, coupled, *ys, w0, w1, w0, w1)
-        both = jnp.concatenate([rinv_x, swap(rinv_x)], 0)
-        rx = sum(ahead(mm_t(root_y, both), "x"))
-        mx = after(a2a(mx, ("y", "x")), rx).reshape(ny, nx, hk, nc, zi)
+        rx = jnp.sum(coupled[:, :hk, ncpl : ncpl + nc * rows].astype(F32), 0)
+        alive = lax.iota(jnp.int32, order)[None, :] < leaf_size[:, None]
+        inv_m = jnp.where(alive[:, None, :], after(leaf_inv, root_y), 0)
+        nmat = jnp.einsum(
+            "lpxq,xlqc->lpc",
+            inv_m.reshape(nl, share, nx, share),
+            after(cpl_all, mx),
+            preferred_element_type=F32,
+        ).astype(BF)
+        y_all = coupled[:, hk:, :ncpl].reshape(nx, nl, hk, 2, share)
+        y_all = y_all.transpose(0, 1, 3, 2, 4).reshape(nx, nl, nk, share)
+        base = jnp.einsum("xlkq,lpxq->lkp", y_all, inv4, preferred_element_type=F32)
+        mx = after(a2a(mx, ("y", "x")), nmat, base).reshape(ny, nx, hk, nc, zi)
         mx = mx.transpose(1, 2, 3, 0, 4).reshape(nx, hk, front)
         mo = swap(mx)
 
     with jax.named_scope("leaf_backward"):
-        w = pl.pallas_call(
+        leaf_x = pl.pallas_call(
             leaf_kernel,
             grid_spec=pltpu.PrefetchScalarGridSpec(
-                num_scalar_prefetch=4,
+                num_scalar_prefetch=2,
                 grid=(nl,),
                 in_specs=[
                     pl.BlockSpec((1, hk, front), lambda i, parent, *_: (parent[i], 0, 0)),
                     pl.BlockSpec((1, hk, front), lambda i, parent, *_: (parent[i], 0, 0)),
-                    pl.BlockSpec((1, front, share), lambda i, *_: (i, 0, 0)),
+                    pl.BlockSpec((1, 1, ncpl), lambda i, *_: (i, 0, 0)),
+                    pl.BlockSpec((1, share, ncpl), lambda i, *_: (i, 0, 0)),
                     pl.BlockSpec((1, nk, share), lambda i, *_: (i, 0, 0)),
                 ],
-                out_specs=pl.BlockSpec((nx, 1, nk, share), lambda i, *_: (0, i, 0, 0)),
+                out_specs=pl.BlockSpec((1, nk, share), lambda i, *_: (i, 0, 0)),
             ),
-            out_shape=jax.ShapeDtypeStruct((nx, nl, nk, share), BF),
+            out_shape=jax.ShapeDtypeStruct((nl, nk, share), F32),
             compiler_params=PARAMS,
             name="leaf_backward",
-        )(leaf_parent, leaf_size, (ix * share).astype(jnp.int32).reshape(1), core, mx, mo, cpl_wide, leaf_y)
+        )(leaf_parent, core, mx, mo, target[:, None, :], nmat, base)
 
     with jax.named_scope("outputs"):
 
@@ -391,16 +416,10 @@
 
         om = mine_of(mx, own), mine_of(mo, half + own)
         out_m = jnp.concatenate([pick(*om), pick(om[1], om[0])], 0)
-        rx = after(rx, w)
         ro = swap(rx[:, rows:])
         out_r = jnp.concatenate(
             [pick(rx[:, :rows], ro), pick(ro, rx[:, :rows])], 0
         )
-
-    with jax.named_scope("leaf_result"):
-        w = a2a(w, "x")
-        w, out_r = lax.optimization_barrier((w, out_r))
-        leaf_x = jnp.einsum("xlkq,lpxq->lkp", w, inv4, preferred_element_type=F32)
     return leaf_x, out_m.astype(F32)[:, None, :], out_r
 
 

time: 169 us -> 170 us (level)
  starting transfers between devices: 45.5 us -> 33.3 us
  waiting for transfers between devices: 24.4 us -> 30.7 us
  matrix products: 12.8 us -> 17.7 us
    all_to_all x5 -> x4, waiting for transfers between devices: 11.4 us -> 21.6 us  [a2a(): return lax.all_to_all(v, axes, 0, 0, tiled=True)]
    ppermute x7, starting transfers between devices: 12.5 us -> 6.63 us  [swap(): return lax.ppermute(v, 'c', [(0, 1), (1, 0)])]
    dot_general x2, matrix products: 1.52 us -> 6.53 us  [the longest x1 5.13 us: body(): jnp.einsum('lpxq,xlqc->lpc', inv_m.reshape(nl, share, nx, share), after(c...]
    all_to_all x5 -> x4, starting transfers between devices: 23.2 us -> 19.4 us  [a2a(): return lax.all_to_all(v, axes, 0, 0, tiled=True)]
    ppermute x9 -> x6, waiting for transfers between devices: 7.99 us -> 4.79 us  [ahead(): lax.ppermute(v, axis, [((i + k) % n, i) for i in range(n)])]
    ppermute x9 -> x6, starting transfers between devices: 9.81 us -> 7.28 us  [ahead(): lax.ppermute(v, axis, [((i + k) % n, i) for i in range(n)])]
    unnamed x42 -> x46, local copies, waits for them, and re-layouts: 4.06 us -> 4.46 us
  transfers between devices with their start and end apart: 22 -> 19, of which waited for: 13 -> 8; matrix products, arithmetic and copies ran while one was open for 12% -> 16% of each run, Pallas kernels for 9% -> 11%
where the time goes in v3:
time: 170 us; the launch traced here: 169 us
  starting transfers between devices  33.3 us (20%)
  waiting for transfers between devices  30.7 us (18%)
  blocking collectives  29.4 us (17%)
  Pallas kernels  28.2 us (17%)
  matrix products  17.7 us (10%)
  between operations  14.4 us (8%)
  local copies, waits for them, and re-layouts  7.82 us (5%)
  other arithmetic  7.03 us (4%)
    all_to_all x2, blocking collectives, a2a(): return lax.all_to_all(v, axes, 0, 0, tiled=True)  29.4 us
    all_to_all x4, waiting for transfers between devices, a2a(): return lax.all_to_all(v, axes, 0, 0, tiled=True)  21.6 us
    all_to_all x4, starting transfers between devices, a2a(): return lax.all_to_all(v, axes, 0, 0, tiled=True)  19.4 us
    ppermute x6, starting transfers between devices, ahead(): lax.ppermute(v, axis, [((i + k) % n, i) for i in range(n)])  7.28 us
    pallas_call x1, Pallas kernels, body(): pl.pallas_call(select_kernel, grid=(nmid * ncpl // tile,), in_specs=[pl.B...  6.87 us
    ppermute x7, starting transfers between devices, swap(): return lax.ppermute(v, 'c', [(0, 1), (1, 0)])  6.63 us
    pallas_call x1, Pallas kernels, body(): pl.pallas_call(leaf_kernel, grid_spec=pltpu.PrefetchScalarGridSpec(num_sc...  5.14 us
    dot_general x1, matrix products, body(): jnp.einsum('lpxq,xlqc->lpc', inv_m.reshape(nl, share, nx, share), after(c...  5.13 us
  transfers between devices with their start and end apart: 19, of which 8 were waited for; matrix products, arithmetic and copies ran while one was open for 16% of the time, Pallas kernels for 11%

profile of v3, /device:TPU:1, one launch (start us, length us, event | category | flops | bytes accessed | tf_op | source)
XLA Modules:
  0.0 168.6 jit_solution(4190550921256968545)
XLA Ops:
  8.8 3.6 %collective-permute-start.1 = (bf16[96,512]{1,0:T(8,128)(2,1)}, bf16[96,512]{1,0:T(8,128)(2,1)S(1)}, u32[]{:S(2)}, u32[]{:S(2)}) collective-permute-start(bf16[96,512]{1,0:T(8,128)(2,1)} %get-tuple-element.19.g0), channel_id=1, source_target_pairs={{64,0},{128,64},{192,128},{0,192},{65,1},{129,65},{193,129},{1,193... | collective-permute-start | bytes 294920 | tf_op jit(solution)/shard_map/gather/ppermute | solution.py:41
  13.4 2.1 %fusion.28 = bf16[4,4,32,256]{3,2,0,1:T(8,128)(2,1)S(1)} fusion(bf16[4,32,4,8,256]{4,3,2,1,0:T(8,128)(2,1)} %bitcast.79, bf16[4,32,256]{2,1,0:T(8,128)(2,1)S(1)} %copy-done), kind=kOutput, calls=%fused_computation.22 | convolution fusion | flops 67239936 | bytes 2424832 | tf_op jit(solution)/shard_map/leaf_forward/lkp,lpxq->xlkq/dot_general | solution.py:237
  15.6 2.1 %collective-permute-done.2.g2 = bf16[96,512]{1,0:T(8,128)(2,1)S(1)} collective-permute-done((bf16[96,512]{1,0:T(8,128)(2,1)}, bf16[96,512]{1,0:T(8,128)(2,1)S(1)}, u32[]{:S(2)}, u32[]{:S(2)}) %collective-permute-start.2) | collective-permute-done | bytes 98336 | tf_op jit(solution)/shard_map/gather/ppermute | solution.py:41
  17.6 2.7 %collective-permute-done.3.g3 = bf16[96,512]{1,0:T(8,128)(2,1)S(1)} collective-permute-done((bf16[96,512]{1,0:T(8,128)(2,1)}, bf16[96,512]{1,0:T(8,128)(2,1)S(1)}, u32[]{:S(2)}, u32[]{:S(2)}) %collective-permute-start.3) | collective-permute-done | bytes 98336 | tf_op jit(solution)/shard_map/gather/ppermute | solution.py:41
  21.0 2.1 %pack.1 = bf16[104,2048]{1,0:T(8,128)(2,1)} custom-call(s32[1]{0:T(128)} %bitcast.11.iy, bf16[32,2048]{1,0:T(8,128)(2,1)} %bitcast.86, bf16[96,512]{1,0:T(8,128)(2,1)} %get-tuple-element.19.g0, bf16[96,512]{1,0:T(8,128)(2,1)} %copy-done.9, bf16[96,512]{1,0:T(8,128)(2,1)} %copy-done.10, bf16[96,512]{1,0:T(8,128)(2,1)} %copy-done.11), custom_call_target="tpu_custom_call" | custom-call | tf_op jit(solution)/shard_map/gather/pack/pallas_call | solution.py:270
  23.9 4.0 %all-to-all-start = ((bf16[4,4,32,256]{3,2,1,0:T(8,128)(2,1)}), bf16[4,4,32,256]{3,2,1,0:T(8,128)(2,1)S(1)}, u32[]{:S(2)}, u32[]{:S(2)}) async-start(bf16[4,4,32,256]{3,2,1,0:T(8,128)(2,1)} %copy.43), calls=%async_computation | async-start | bytes 524288 | tf_op jit(solution)/shard_map/leaf_forward/all_to_all | solution.py:26
  28.4 5.1 %fusion = bf16[4,2048,256]{2,1,0:T(8,128)(2,1)} fusion(bf16[4,256,512]{2,1,0:T(8,128)(2,1)S(1)} %copy-done.7, s32[4,512]{1,0:T(4,128)S(1)} %fusion.46), kind=kOutput, calls=%fused_computation.1 | convolution fusion | flops 2151677952 | bytes 5251072 | tf_op jit(solution)/shard_map/leaf_spread/lcn,lpc->lnp/dot_general | solution.py:283
  33.6 3.7 %fusion.10 = f32[4,32,2048]{2,1,0:T(8,128)S(1)} fusion(bf16[4,2048,256]{2,1,0:T(8,128)(2,1)} %fusion, f32[32,2048]{1,0:T(8,128)S(1)} %convolution_bitcast_fusion, pred[4]{0:T(512)(128)(4,1)S(1)} %iota_compare_fusion.6, pred[4,4]{1,0:T(4,128)(4,1)S(1)} %iota_compare_fusion.5, bf16[32,4,256]{2,0,1:T(8,128)(2,1)S(1)} %fusion.71), kind=kOutput, calls=%fused_computation.9 | convolution fusion | flops 537526272 | bytes 5570580 | tf_op jit(solution)/shard_map/leaf_spread/mlp,lnp->mn/dot_general | solution.py:288
  37.4 2.5 %collective-permute-start = (bf16[4,16,2048]{2,1,0:T(8,128)(2,1)S(1)}, bf16[4,16,2048]{2,1,0:T(8,128)(2,1)S(1)}, u32[]{:S(2)}, u32[]{:S(2)}) collective-permute-start(bf16[4,16,2048]{2,1,0:T(8,128)(2,1)S(1)} %pad_maximum_fusion), channel_id=1, source_target_pairs={{0,4},{4,0},{1,5},{5,1},{2,6},{6,2},{3,7},{7,3},{8,12},{12,8},{9,1... | collective-permute-start | bytes 786440 | tf_op jit(solution)/shard_map/contrib_sum/ppermute | solution.py:35
  41.8 11.5 %all_to_all.30 = bf16[16,16,512]{2,1,0:T(8,128)(2,1)S(1)} all-to-all(bf16[16,16,512]{2,1,0:T(8,128)(2,1)S(1)} %reshape.174), channel_id=1, replica_groups=mesh['y'=4,'z'=8,'c'=2,'x'=4] {'y','x'}, dimensions={0} | all-to-all | bytes 524288 | tf_op jit(solution)/shard_map/contrib_sum/all_to_all | solution.py:26
  53.4 17.9 %all_to_all.31 = bf16[8,16,512]{2,1,0:T(8,128)(2,1)S(1)} all-to-all(bf16[8,16,512]{2,1,0:T(8,128)(2,1)S(1)} %broadcast_in_dim.98), channel_id=1, replica_groups=mesh['y'=4,'z'=8,'c'=2,'x'=4] {'z'}, dimensions={0} | all-to-all | bytes 262144 | tf_op jit(solution)/shard_map/contrib_sum/all_to_all | solution.py:26
  71.9 2.5 %all-gather.5.cloned.1.call-done = bf16[832,2048]{1,0:T(8,128)(2,1)} async-done(((bf16[104,2048]{1,0:T(8,128)(2,1)}), bf16[832,2048]{1,0:T(8,128)(2,1)}) %all-gather.5.cloned.1.call-update) | async-done | bytes 3407888 | tf_op jit(solution)/shard_map/gather/all_gather | solution.py:278
  76.4 6.9 %root_select.1.r0_ref = bf16[2048,512]{1,0:T(8,128)(2,1)} custom-call(s32[8,1,256]{2,1,0:T(1,128)} %reshape.190.at_ref, bf16[8,104,2048]{2,1,0:T(8,128)(2,1)} %bitcast.73), custom_call_target="tpu_custom_call" | custom-call | tf_op jit(solution)/shard_map/gather/root_select/pallas_call | solution.py:316
  86.3 4.1 %mid_forward.1 = (bf16[16,2048]{1,0:T(8,128)(2,1)}, bf16[16,16,512]{2,1,0:T(8,128)(2,1)}) custom-call(s32[1]{0:T(128)} %bitcast.core, bf16[16,512]{1,0:T(8,128)(2,1)} %reduce_sum.53.h_ref, bf16[8,104,2048]{2,1,0:T(8,128)(2,1)} %bitcast.74, bf16[8,104,2048]{2,1,0:T(8,128)(2,1)} %copy-done.1, bf16[8,104,2048]{2,1,0:T(8,128)(2,1)} %bitcast.75, ...), custom_call_target="tpu_custom_call" | custom-call | tf_op jit(solution)/shard_map/mid_forward/mid_forward/pallas_call | solution.py:332
  91.7 6.6 %all-to-all-start.3 = ((bf16[16,16,512]{2,1,0:T(8,128)(2,1)}), bf16[16,16,512]{2,1,0:T(8,128)(2,1)S(1)}, u32[]{:S(2)}, u32[]{:S(2)}) async-start(bf16[16,16,512]{2,1,0:T(8,128)(2,1)} %get-tuple-element.22), calls=%async_computation.3 | async-start | bytes 524288 | tf_op jit(solution)/shard_map/mid_forward/all_to_all | solution.py:26
  99.6 10.1 %all-to-all-done.3.u_ref = bf16[16,16,512]{2,1,0:T(8,128)(2,1)S(1)} async-done(((bf16[16,16,512]{2,1,0:T(8,128)(2,1)}), bf16[16,16,512]{2,1,0:T(8,128)(2,1)S(1)}, u32[]{:S(2)}, u32[]{:S(2)}) %all-to-all-start.3) | async-done | bytes 262176 | tf_op jit(solution)/shard_map/mid_forward/all_to_all | solution.py:26
  110.3 4.2 %root.1 = (bf16[16,512]{1,0:T(8,128)(2,1)}, bf16[4,80,640]{2,1,0:T(8,128)(2,1)}) custom-call(bf16[16,16,512]{2,1,0:T(8,128)(2,1)} %copy-done.6, bf16[2048,512]{1,0:T(8,128)(2,1)} %root_select.1.r0_ref, bf16[2048,512]{1,0:T(8,128)(2,1)} %collective-permute-done.5.r1_ref, f32[16,512]{1,0:T(8,128)} %convert_add_fusion.pre_ref, ...), custom_call_target="tpu_custom_call" | custom-call | tf_op jit(solution)/shard_map/root/root/pallas_call | solution.py:349
  114.5 2.7 %collective-permute-start.8 = (bf16[16,2048]{1,0:T(8,128)(2,1)S(1)}, bf16[16,2048]{1,0:T(8,128)(2,1)S(1)}, u32[]{:S(2)}, u32[]{:S(2)}) collective-permute-start(bf16[16,2048]{1,0:T(8,128)(2,1)S(1)} %copy-done.12), channel_id=1, source_target_pairs={{64,0},{128,64},{192,128},{0,192},{65,1},{129,65},{193,129},{1,193... | collective-permute-start | bytes 196616 | tf_op jit(solution)/shard_map/root/ppermute | solution.py:41
  117.1 3.5 %all-to-all-start.4 = ((bf16[4,80,640]{2,1,0:T(8,128)(2,1)}), bf16[4,80,640]{2,1,0:T(8,128)(2,1)S(1)}, u32[]{:S(2)}, u32[]{:S(2)}) async-start(bf16[4,80,640]{2,1,0:T(8,128)(2,1)} %get-tuple-element.26), calls=%async_computation.4 | async-start | bytes 819200 | tf_op jit(solution)/shard_map/root/all_to_all | solution.py:26
  122.2 9.8 %all-to-all-done.4.cp_ref = bf16[4,80,640]{2,1,0:T(8,128)(2,1)S(1)} async-done(((bf16[4,80,640]{2,1,0:T(8,128)(2,1)}), bf16[4,80,640]{2,1,0:T(8,128)(2,1)S(1)}, u32[]{:S(2)}, u32[]{:S(2)}) %all-to-all-start.4) | async-done | bytes 409632 | tf_op jit(solution)/shard_map/root/all_to_all | solution.py:26
  134.8 4.3 %mid_backward.1 = bf16[16,16,512]{2,1,0:T(8,128)(2,1)} custom-call(s32[1]{0:T(128)} %bitcast.core, bf16[4,80,640]{2,1,0:T(8,128)(2,1)} %copy-done.3, bf16[16,2048]{1,0:T(8,128)(2,1)} %get-tuple-element.28.y0, bf16[16,2048]{1,0:T(8,128)(2,1)} %copy-done.14, bf16[16,2048]{1,0:T(8,128)(2,1)} %copy-done.15, bf16[16,2048]{1,0:T(8,128)(2,1)} %copy-done.13, ...), custom_call_target="tpu_custom_call" | custom-call | tf_op jit(solution)/shard_map/mid_backward/mid_backward/pallas_call | solution.py:364
  139.1 5.3 %all-to-all-start.5 = ((bf16[16,16,512]{2,1,0:T(8,128)(2,1)}), bf16[16,16,512]{2,1,0:T(8,128)(2,1)S(1)}, u32[]{:S(2)}, u32[]{:S(2)}) async-start(bf16[16,16,512]{2,1,0:T(8,128)(2,1)} %mid_backward.1), calls=%async_computation.5 | async-start | bytes 524288 | tf_op jit(solution)/shard_map/mid_backward/all_to_all | solution.py:26
  144.5 5.1 %bitcast_convert_fusion.n_ref = bf16[4,256,512]{2,1,0:T(8,128)(2,1)} fusion(bf16[4,4,256,512]{3,2,1,0:T(8,128)(2,1)} %bitcast.89, bf16[4,32,4,8,256]{4,3,2,1,0:T(8,128)(2,1)} %bitcast.81), kind=kOutput, calls=%fused_computation.17 | convolution fusion | flops 1074266112 | bytes 7340032 | tf_op jit(solution)/shard_map/mid_backward/lpxq,xlqc->lpc/dot_general | solution.py:378
  156.6 5.1 %leaf_backward.1 = f32[4,32,256]{2,1,0:T(8,128)} custom-call(s32[4]{0:T(128)} %parent.1, s32[1]{0:T(128)} %bitcast.core, bf16[4,16,2048]{2,1,0:T(8,128)(2,1)} %copy-done.5, bf16[4,16,2048]{2,1,0:T(8,128)(2,1)} %copy-done.8, s32[4,1,512]{2,1,0:T(1,128)} %broadcast_in_dim.101.at_ref, bf16[4,256,512]{2,1,0:T(8,128)(2,1)} %bitcast_convert_fusion.n_ref, ...), custom_call_target="tpu_custom_call" | custom-call | tf_op jit(solution)/shard_map/leaf_backward/leaf_backward/pallas_call | solution.py:392
  (118 shorter events, 26.8 us)
Async XLA Ops:
  7.2 67.2 %all-gather.5.cloned.1.call-start = ((), (), s32[]{:S(2)}) async-start(), calls=%async_computation.6 | async-start | bytes 3833856 | tf_op jit(solution)/shard_map/gather/all_gather | solution.py:278
  8.8 6.8 %collective-permute-start.1 = (bf16[96,512]{1,0:T(8,128)(2,1)}, bf16[96,512]{1,0:T(8,128)(2,1)S(1)}, u32[]{:S(2)}, u32[]{:S(2)}) collective-permute-start(bf16[96,512]{1,0:T(8,128)(2,1)} %get-tuple-element.19.g0), channel_id=1, source_target_pairs={{64,0},{128,64},{192,128},{0,192},{65,1},{129,65},{193,129},{1,193... | collective-permute-start | bytes 294920 | tf_op jit(solution)/shard_map/gather/ppermute | solution.py:41
  12.4 5.3 %collective-permute-start.2 = (bf16[96,512]{1,0:T(8,128)(2,1)}, bf16[96,512]{1,0:T(8,128)(2,1)S(1)}, u32[]{:S(2)}, u32[]{:S(2)}) collective-permute-start(bf16[96,512]{1,0:T(8,128)(2,1)} %get-tuple-element.19.g0), channel_id=1, source_target_pairs={{128,0},{192,64},{0,128},{64,192},{129,1},{193,65},{1,129},{65,193... | collective-permute-start | bytes 294920 | tf_op jit(solution)/shard_map/gather/ppermute | solution.py:41
  12.7 7.7 %collective-permute-start.3 = (bf16[96,512]{1,0:T(8,128)(2,1)}, bf16[96,512]{1,0:T(8,128)(2,1)S(1)}, u32[]{:S(2)}, u32[]{:S(2)}) collective-permute-start(bf16[96,512]{1,0:T(8,128)(2,1)} %get-tuple-element.19.g0), channel_id=1, source_target_pairs={{192,0},{0,64},{64,128},{128,192},{193,1},{1,65},{65,129},{129,193... | collective-permute-start | bytes 294920 | tf_op jit(solution)/shard_map/gather/ppermute | solution.py:41
  13.4 14.6 %copy-start.19 = (s32[4,512]{1,0:T(4,128)S(1)}, s32[4,512]{1,0:T(4,128)}, u32[]{:S(2)}) copy-start(s32[4,512]{1,0:T(4,128)} %param.17) | copy-start | bytes 24580
  13.4 14.7 %copy-start.18 = (bf16[32,1,32]{2,0,1:T(8,128)(2,1)S(1)}, bf16[32,1,32]{2,0,1:T(8,128)(2,1)}, u32[]{:S(2)}) copy-start(bf16[32,1,32]{2,0,1:T(8,128)(2,1)} %param.18) | copy-start | bytes 6148
  13.4 14.9 %copy-start.7 = (bf16[4,256,512]{2,1,0:T(8,128)(2,1)S(1)}, bf16[4,256,512]{2,1,0:T(8,128)(2,1)}, u32[]{:S(2)}) copy-start(bf16[4,256,512]{2,1,0:T(8,128)(2,1)} %param.14) | copy-start | bytes 3145732
  23.9 9.6 %all-to-all-start = ((bf16[4,4,32,256]{3,2,1,0:T(8,128)(2,1)}), bf16[4,4,32,256]{3,2,1,0:T(8,128)(2,1)S(1)}, u32[]{:S(2)}, u32[]{:S(2)}) async-start(bf16[4,4,32,256]{3,2,1,0:T(8,128)(2,1)} %copy.43), calls=%async_computation | async-start | bytes 524288 | tf_op jit(solution)/shard_map/leaf_forward/all_to_all | solution.py:26
  27.9 116.5 %all-gather.7.cloned.1.call-start = ((), (), s32[]{:S(2)}) async-start(), calls=%async_computation.7 | async-start | bytes 5242880 | tf_op jit(solution)/shard_map/contrib_sum/all_gather | solution.py:305
  37.4 3.7 %collective-permute-start = (bf16[4,16,2048]{2,1,0:T(8,128)(2,1)S(1)}, bf16[4,16,2048]{2,1,0:T(8,128)(2,1)S(1)}, u32[]{:S(2)}, u32[]{:S(2)}) collective-permute-start(bf16[4,16,2048]{2,1,0:T(8,128)(2,1)S(1)} %pad_maximum_fusion), channel_id=1, source_target_pairs={{0,4},{4,0},{1,5},{5,1},{2,6},{6,2},{3,7},{7,3},{8,12},{12,8},{9,1... | collective-permute-start | bytes 786440 | tf_op jit(solution)/shard_map/contrib_sum/ppermute | solution.py:35
  74.4 10.1 %collective-permute-start.4 = (bf16[8,104,2048]{2,1,0:T(8,128)(2,1)}, bf16[8,104,2048]{2,1,0:T(8,128)(2,1)S(1)}, u32[]{:S(2)}, u32[]{:S(2)}) collective-permute-start(bf16[8,104,2048]{2,1,0:T(8,128)(2,1)} %bitcast.72), channel_id=1, source_target_pairs={{0,4},{4,0},{1,5},{5,1},{2,6},{6,2},{3,7},{7,3},{8,12},{12,8},{9,1... | collective-permute-start | bytes 10223624 | tf_op jit(solution)/shard_map/gather/ppermute | solution.py:35
  83.3 16.2 %collective-permute-start.5 = (bf16[2048,512]{1,0:T(8,128)(2,1)}, bf16[2048,512]{1,0:T(8,128)(2,1)}, u32[]{:S(2)}, u32[]{:S(2)}) collective-permute-start(bf16[2048,512]{1,0:T(8,128)(2,1)} %root_select.1.r0_ref), channel_id=1, source_target_pairs={{0,4},{4,0},{1,5},{5,1},{2,6},{6,2},{3,7},{7,3},{8,12},{12,8},{9,1... | collective-permute-start | bytes 6291464 | tf_op jit(solution)/shard_map/gather/ppermute | solution.py:35
  83.3 16.2 %collective-permute-start.7 = (bf16[32,512]{1,0:T(8,128)(2,1)}, bf16[32,512]{1,0:T(8,128)(2,1)}, u32[]{:S(2)}, u32[]{:S(2)}) collective-permute-start(bf16[32,512]{1,0:T(8,128)(2,1)} %get-tuple-element.25.w0_ref), channel_id=1, source_target_pairs={{0,4},{4,0},{1,5},{5,1},{2,6},{6,2},{3,7},{7,3},{8,12},{12,8},{9,1... | collective-permute-start | bytes 98312 | tf_op jit(solution)/shard_map/gather/ppermute | solution.py:35
  91.4 7.5 %collective-permute-start.6 = (bf16[16,512]{1,0:T(8,128)(2,1)S(1)}, bf16[16,512]{1,0:T(8,128)(2,1)S(1)}, u32[]{:S(2)}, u32[]{:S(2)}) collective-permute-start(bf16[16,512]{1,0:T(8,128)(2,1)S(1)} %select_convert_fusion.2), channel_id=1, source_target_pairs={{0,4},{4,0},{1,5},{5,1},{2,6},{6,2},{3,7},{7,3},{8,12},{12,8},{9,1... | collective-permute-start | bytes 49160 | tf_op jit(solution)/shard_map/mid_forward/ppermute | solution.py:35
  91.7 17.9 %all-to-all-start.3 = ((bf16[16,16,512]{2,1,0:T(8,128)(2,1)}), bf16[16,16,512]{2,1,0:T(8,128)(2,1)S(1)}, u32[]{:S(2)}, u32[]{:S(2)}) async-start(bf16[16,16,512]{2,1,0:T(8,128)(2,1)} %get-tuple-element.22), calls=%async_computation.3 | async-start | bytes 524288 | tf_op jit(solution)/shard_map/mid_forward/all_to_all | solution.py:26
  99.5 14.9 %copy-start.12 = (bf16[16,2048]{1,0:T(8,128)(2,1)S(1)}, bf16[16,2048]{1,0:T(8,128)(2,1)}, u32[]{:S(2)}) copy-start(bf16[16,2048]{1,0:T(8,128)(2,1)} %get-tuple-element.28.y0) | copy-start | bytes 196612
  99.5 21.1 %copy-start.2 = (bf16[4,256,1024]{2,1,0:T(8,128)(2,1)S(1)}, bf16[4,256,1024]{2,1,0:T(8,128)(2,1)}, u32[]{:S(2)}) copy-start(bf16[4,256,1024]{2,1,0:T(8,128)(2,1)} %param.13) | copy-start | bytes 6291460
  114.5 19.1 %collective-permute-start.10 = (bf16[16,2048]{1,0:T(8,128)(2,1)S(1)}, bf16[16,2048]{1,0:T(8,128)(2,1)S(1)}, u32[]{:S(2)}, u32[]{:S(2)}) collective-permute-start(bf16[16,2048]{1,0:T(8,128)(2,1)S(1)} %copy-done.12), channel_id=1, source_target_pairs={{192,0},{0,64},{64,128},{128,192},{193,1},{1,65},{65,129},{129,193... | collective-permute-start | bytes 196616 | tf_op jit(solution)/shard_map/root/ppermute | solution.py:41
  114.5 19.1 %collective-permute-start.8 = (bf16[16,2048]{1,0:T(8,128)(2,1)S(1)}, bf16[16,2048]{1,0:T(8,128)(2,1)S(1)}, u32[]{:S(2)}, u32[]{:S(2)}) collective-permute-start(bf16[16,2048]{1,0:T(8,128)(2,1)S(1)} %copy-done.12), channel_id=1, source_target_pairs={{64,0},{128,64},{192,128},{0,192},{65,1},{129,65},{193,129},{1,193... | collective-permute-start | bytes 196616 | tf_op jit(solution)/shard_map/root/ppermute | solution.py:41
  117.1 16.4 %collective-permute-start.9 = (bf16[16,2048]{1,0:T(8,128)(2,1)S(1)}, bf16[16,2048]{1,0:T(8,128)(2,1)S(1)}, u32[]{:S(2)}, u32[]{:S(2)}) collective-permute-start(bf16[16,2048]{1,0:T(8,128)(2,1)S(1)} %copy-done.12), channel_id=1, source_target_pairs={{128,0},{192,64},{0,128},{64,192},{129,1},{193,65},{1,129},{65,193... | collective-permute-start | bytes 196616 | tf_op jit(solution)/shard_map/root/ppermute | solution.py:41
  117.1 14.9 %all-to-all-start.4 = ((bf16[4,80,640]{2,1,0:T(8,128)(2,1)}), bf16[4,80,640]{2,1,0:T(8,128)(2,1)S(1)}, u32[]{:S(2)}, u32[]{:S(2)}) async-start(bf16[4,80,640]{2,1,0:T(8,128)(2,1)} %get-tuple-element.26), calls=%async_computation.4 | async-start | bytes 819200 | tf_op jit(solution)/shard_map/root/all_to_all | solution.py:26
  132.1 22.7 %collective-permute-start.12 = (f32[16,32]{1,0:T(8,128)S(1)}, f32[16,32]{1,0:T(8,128)S(1)}, u32[]{:S(2)}, u32[]{:S(2)}) collective-permute-start(f32[16,32]{1,0:T(8,128)S(1)} %slice.48), channel_id=1, source_target_pairs={{0,4},{4,0},{1,5},{5,1},{2,6},{6,2},{3,7},{7,3},{8,12},{12,8},{9,1... | collective-permute-start | bytes 6152 | tf_op jit(solution)/shard_map/outputs/ppermute | solution.py:35
  139.1 13.8 %all-to-all-start.5 = ((bf16[16,16,512]{2,1,0:T(8,128)(2,1)}), bf16[16,16,512]{2,1,0:T(8,128)(2,1)S(1)}, u32[]{:S(2)}, u32[]{:S(2)}) async-start(bf16[16,16,512]{2,1,0:T(8,128)(2,1)} %mid_backward.1), calls=%async_computation.5 | async-start | bytes 524288 | tf_op jit(solution)/shard_map/mid_backward/all_to_all | solution.py:26
  153.5 2.4 %collective-permute-start.11 = (bf16[4,16,2048]{2,1,0:T(8,128)(2,1)S(1)}, bf16[4,16,2048]{2,1,0:T(8,128)(2,1)S(1)}, u32[]{:S(2)}, u32[]{:S(2)}) collective-permute-start(bf16[4,16,2048]{2,1,0:T(8,128)(2,1)S(1)} %reshape.182.x0_ref), channel_id=1, source_target_pairs={{0,4},{4,0},{1,5},{5,1},{2,6},{6,2},{3,7},{7,3},{8,12},{12,8},{9,1... | collective-permute-start | bytes 786440 | tf_op jit(solution)/shard_map/mid_backward/ppermute | solution.py:35
  (18 other events, 74.4 us)
Sparse Core Ops, SparseCore 0:
  23.3 51.0 all-gather.4
  76.2 54.6 all-gather.6

commit v4 on v3

--- a/solution.py
+++ b/solution.py
@@ -128,7 +128,7 @@
     out_ref[...] = acc.astype(BF)
 
 
-def root_kernel(nx, u_ref, r0_ref, r1_ref, pre_ref, w0_ref, w1_ref, ly_ref, y_ref, cpl_ref):
+def root_kernel(nx, u_ref, r0_ref, r1_ref, pre_ref, w0_ref, w1_ref, y_ref, cpl_ref):
     n = u_ref.shape[-1]
     acc = pre_ref[...]
     sel = []
@@ -141,16 +141,9 @@
     both = jnp.concatenate([w0_ref[...], w1_ref[...]], 0)
     both = jnp.concatenate([both, jnp.zeros((128 - both.shape[0], both.shape[1]), BF)], 0)
     part = mm_t(y, both).astype(BF)
-    hk = y.shape[0]
-    share = ly_ref.shape[2]
     for x in range(nx):
-        cpl_ref[x, :hk, :n] = mm_t(y, sel[x]).astype(BF)
-        cpl_ref[x, :hk, n:] = part
-        for i in range(ly_ref.shape[0]):
-            for h in range(2):
-                cpl_ref[x, (i + 1) * hk : (i + 2) * hk, h * share : (h + 1) * share] = ly_ref[
-                    i, h * hk : (h + 1) * hk, :
-                ]
+        cpl_ref[x, :, :n] = mm_t(y, sel[x]).astype(BF)
+        cpl_ref[x, :, n:] = part
 
 
 def back_kernel(core, cp_ref, y0, y1, y2, y3, m0_ref, m1_ref, c0_ref, c1_ref, out_ref):
@@ -299,7 +292,11 @@
     with jax.named_scope("contrib_sum"):
         s = half_sum(placed, flip).astype(BF)
         s = s.reshape(nx, hk, nc, ny, zi).transpose(3, 0, 1, 2, 4).reshape(ny * nx, hk, width)
+        ysx = ahead(leaf_yb, "x")
+        y_all = jnp.stack([lax.select_n((k - ix) % nx, *ysx) for k in range(nx)])
+        at = place(mid_map, iy).reshape(-1, 1, 256)
         s_own = jnp.sum(a2a(s, ("y", "x")).astype(F32), 0).astype(BF)
+        s_own, y_all, at = lax.optimization_barrier((s_own, y_all, at))
         s = jnp.sum(spread(s_own, "z").astype(F32), 0)
         contrib = s.astype(BF)
         cpl_all = lax.all_gather(after(leaf_cpl, s_own), "x", axis=0)
@@ -311,7 +308,6 @@
             return pl.BlockSpec((nz, rows, front), lambda *_: (0, i, 0))
 
         tile = 256
-        at = place(mid_map, iy).reshape(-1, 1, tile)
 
         rsel0 = pl.pallas_call(
             select_kernel,
@@ -338,25 +334,25 @@
                 jax.ShapeDtypeStruct((hk, front), BF),
                 jax.ShapeDtypeStruct((ny * nx, hk, ncpl), BF),
             ],
-            compiler_params=PARAMS,
+            compiler_params=pltpu.CompilerParams(vmem_limit_bytes=40 * 2**20),
             name="mid_forward",
         )(core, contrib, w0, w1, w0, w1)
-        pre = jnp.sum(after(w0, part_y)[:, 3 * rows :].astype(F32), 0)
+        pre = jnp.sum(after(w0, part_y, rsel1)[:, 3 * rows :].astype(F32), 0)
         pre = half_sum(jnp.concatenate(jnp.split(pre, g, 1), 0))
         u = a2a(u, ("y", "x"))
 
     with jax.named_scope("root"):
         root_y, coupled = pl.pallas_call(
             functools.partial(root_kernel, nx),
-            in_specs=[VM] * 7,
+            in_specs=[VM] * 6,
             out_specs=[VM] * 2,
             out_shape=[
                 jax.ShapeDtypeStruct((hk, blk), BF),
-                jax.ShapeDtypeStruct((nx, hk * (1 + nl), ncpl + 128), BF),
+                jax.ShapeDtypeStruct((nx, hk, ncpl + 128), BF),
             ],
             compiler_params=PARAMS,
             name="root",
-        )(u, rsel0, rsel1, pre, rinv_x, rinv_o, leaf_yb)
+        )(u, rsel0, rsel1, pre, rinv_x, rinv_o)
         ys = ahead(after(part_y, root_y), "y")
         coupled = a2a(coupled, "x")
 
@@ -372,7 +368,7 @@
             compiler_params=PARAMS,
             name="mid_backward",
         )(core, coupled, *ys, w0, w1, w0, w1)
-        rx = jnp.sum(coupled[:, :hk, ncpl : ncpl + nc * rows].astype(F32), 0)
+        rx = jnp.sum(coupled[:, :, ncpl : ncpl + nc * rows].astype(F32), 0)
         alive = lax.iota(jnp.int32, order)[None, :] < leaf_size[:, None]
         inv_m = jnp.where(alive[:, None, :], after(leaf_inv, root_y), 0)
         nmat = jnp.einsum(
@@ -381,8 +377,6 @@
             after(cpl_all, mx),
             preferred_element_type=F32,
         ).astype(BF)
-        y_all = coupled[:, hk:, :ncpl].reshape(nx, nl, hk, 2, share)
-        y_all = y_all.transpose(0, 1, 3, 2, 4).reshape(nx, nl, nk, share)
         base = jnp.einsum("xlkq,lpxq->lkp", y_all, inv4, preferred_element_type=F32)
         mx = after(a2a(mx, ("y", "x")), nmat, base).reshape(ny, nx, hk, nc, zi)
         mx = mx.transpose(1, 2, 3, 0, 4).reshape(nx, hk, front)

time: 170 us -> 160 us (0.941)
  blocking collectives: 29.4 us -> 16.8 us
  starting transfers between devices: 33.3 us -> 42.1 us
  waiting for transfers between devices: 30.7 us -> 27.5 us
    all_to_all x2 -> x1, blocking collectives: 29.4 us -> 16.8 us  [a2a(): return lax.all_to_all(v, axes, 0, 0, tiled=True)]
    ppermute x6 -> x9, starting transfers between devices: 7.28 us -> 11 us  [ahead(): lax.ppermute(v, axis, [((i + k) % n, i) for i in range(n)])]
    ppermute x7, starting transfers between devices: 6.63 us -> 10.3 us  [swap(): return lax.ppermute(v, 'c', [(0, 1), (1, 0)])]
    all_gather x1, waiting for transfers between devices: 2.5 us -> 0.02 us  [body(): wide = lax.all_gather(payload, 'z', axis=0)]
    unnamed x46 -> x50, local copies, waits for them, and re-layouts: 4.46 us -> 2.71 us
    dot_general x1, matrix products: 1.39 us -> 3.13 us  [body(): base = jnp.einsum('xlkq,lpxq->lkp', y_all, inv4, preferred_element_type=F32)]
    all_to_all x4 -> x5, starting transfers between devices: 19.4 us -> 20.7 us  [a2a(): return lax.all_to_all(v, axes, 0, 0, tiled=True)]
    all_to_all x4 -> x5, waiting for transfers between devices: 21.6 us -> 22.1 us  [a2a(): return lax.all_to_all(v, axes, 0, 0, tiled=True)]
  transfers between devices with their start and end apart: 19 -> 23, of which waited for: 8 -> 7; matrix products, arithmetic and copies ran while one was open for 16% -> 17% of each run, Pallas kernels for 11% -> 11%
where the time goes in v4:
time: 160 us; the launch traced here: 159 us
  starting transfers between devices  42.1 us (26%)
  waiting for transfers between devices  27.5 us (17%)
  Pallas kernels  26.8 us (17%)
  matrix products  18.7 us (12%)
  blocking collectives  16.8 us (10%)
  between operations  14.6 us (9%)
  local copies, waits for them, and re-layouts  6.68 us (4%)
  other arithmetic  5.6 us (4%)
    all_to_all x5, waiting for transfers between devices, a2a(): return lax.all_to_all(v, axes, 0, 0, tiled=True)  22.1 us
    all_to_all x5, starting transfers between devices, a2a(): return lax.all_to_all(v, axes, 0, 0, tiled=True)  20.7 us
    all_to_all x1, blocking collectives, a2a(): return lax.all_to_all(v, axes, 0, 0, tiled=True)  16.8 us
    ppermute x9, starting transfers between devices, ahead(): lax.ppermute(v, axis, [((i + k) % n, i) for i in range(n)])  11 us
    ppermute x7, starting transfers between devices, swap(): return lax.ppermute(v, 'c', [(0, 1), (1, 0)])  10.3 us
    pallas_call x1, Pallas kernels, body(): pl.pallas_call(select_kernel, grid=(nmid * ncpl // tile,), in_specs=[pl.B...  7.04 us
    pallas_call x1, Pallas kernels, body(): pl.pallas_call(leaf_kernel, grid_spec=pltpu.PrefetchScalarGridSpec(num_sc...  5.12 us
    dot_general x1, matrix products, body(): jnp.einsum('lcn,lpc->lnp', hot, leaf_cpl, preferred_element_type=F32)  5.07 us
  transfers between devices with their start and end apart: 23, of which 7 were waited for; matrix products, arithmetic and copies ran while one was open for 17% of the time, Pallas kernels for 11%

profile of v4, /device:TPU:1, one launch (start us, length us, event | category | flops | bytes accessed | tf_op | source)
XLA Modules:
  0.0 158.9 jit_solution(396508316924383733)
XLA Ops:
  8.8 3.6 %collective-permute-start.4 = (bf16[96,512]{1,0:T(8,128)(2,1)}, bf16[96,512]{1,0:T(8,128)(2,1)S(1)}, u32[]{:S(2)}, u32[]{:S(2)}) collective-permute-start(bf16[96,512]{1,0:T(8,128)(2,1)} %get-tuple-element.24.g0), channel_id=1, source_target_pairs={{64,0},{128,64},{192,128},{0,192},{65,1},{129,65},{193,129},{1,193... | collective-permute-start | bytes 294920 | tf_op jit(solution)/shard_map/gather/ppermute | solution.py:41
  17.6 2.7 %collective-permute-done.6.g3 = bf16[96,512]{1,0:T(8,128)(2,1)S(1)} collective-permute-done((bf16[96,512]{1,0:T(8,128)(2,1)}, bf16[96,512]{1,0:T(8,128)(2,1)S(1)}, u32[]{:S(2)}, u32[]{:S(2)}) %collective-permute-start.6) | collective-permute-done | bytes 98336 | tf_op jit(solution)/shard_map/gather/ppermute | solution.py:41
  24.0 4.0 %all-to-all-start = ((bf16[4,4,32,256]{3,2,1,0:T(8,128)(2,1)}), bf16[4,4,32,256]{3,2,1,0:T(8,128)(2,1)S(1)}, u32[]{:S(2)}, u32[]{:S(2)}) async-start(bf16[4,4,32,256]{3,2,1,0:T(8,128)(2,1)} %copy.49), calls=%async_computation | async-start | bytes 524288 | tf_op jit(solution)/shard_map/leaf_forward/all_to_all | solution.py:26
  28.4 5.1 %fusion = bf16[4,2048,256]{2,1,0:T(8,128)(2,1)} fusion(bf16[4,256,512]{2,1,0:T(8,128)(2,1)S(1)} %copy-done.7, s32[4,512]{1,0:T(4,128)S(1)} %fusion.46), kind=kOutput, calls=%fused_computation.1 | convolution fusion | flops 2151677952 | bytes 5251072 | tf_op jit(solution)/shard_map/leaf_spread/lcn,lpc->lnp/dot_general | solution.py:276
  33.6 3.7 %fusion.10 = f32[4,32,2048]{2,1,0:T(8,128)S(1)} fusion(bf16[4,2048,256]{2,1,0:T(8,128)(2,1)} %fusion, f32[32,2048]{1,0:T(8,128)S(1)} %convolution_bitcast_fusion, pred[4]{0:T(512)(128)(4,1)S(1)} %iota_compare_fusion.6, pred[4,4]{1,0:T(4,128)(4,1)S(1)} %iota_compare_fusion.5, bf16[32,4,256]{2,0,1:T(8,128)(2,1)S(1)} %fusion.71), kind=kOutput, calls=%fused_computation.9 | convolution fusion | flops 537526272 | bytes 5570580 | tf_op jit(solution)/shard_map/leaf_spread/mlp,lnp->mn/dot_general | solution.py:281
  37.4 2.5 %collective-permute-start = (bf16[4,16,2048]{2,1,0:T(8,128)(2,1)S(1)}, bf16[4,16,2048]{2,1,0:T(8,128)(2,1)S(1)}, u32[]{:S(2)}, u32[]{:S(2)}) collective-permute-start(bf16[4,16,2048]{2,1,0:T(8,128)(2,1)S(1)} %pad_maximum_fusion), channel_id=1, source_target_pairs={{0,4},{4,0},{1,5},{5,1},{2,6},{6,2},{3,7},{7,3},{8,12},{12,8},{9,1... | collective-permute-start | bytes 786440 | tf_op jit(solution)/shard_map/contrib_sum/ppermute | solution.py:35
  46.5 3.5 %all-to-all-start.1 = ((bf16[16,16,512]{2,1,0:T(8,128)(2,1)}), bf16[16,16,512]{2,1,0:T(8,128)(2,1)S(1)}, u32[]{:S(2)}, u32[]{:S(2)}) async-start(bf16[16,16,512]{2,1,0:T(8,128)(2,1)} %reshape.168), calls=%async_computation.1 | async-start | bytes 524288 | tf_op jit(solution)/shard_map/contrib_sum/all_to_all | solution.py:26
  51.0 6.9 %all-to-all-done.1 = bf16[16,16,512]{2,1,0:T(8,128)(2,1)S(1)} async-done(((bf16[16,16,512]{2,1,0:T(8,128)(2,1)}), bf16[16,16,512]{2,1,0:T(8,128)(2,1)S(1)}, u32[]{:S(2)}, u32[]{:S(2)}) %all-to-all-start.1) | async-done | bytes 262176 | tf_op jit(solution)/shard_map/contrib_sum/all_to_all | solution.py:26
  58.0 16.8 %all_to_all.30 = bf16[8,16,512]{2,1,0:T(8,128)(2,1)S(1)} all-to-all(bf16[8,16,512]{2,1,0:T(8,128)(2,1)S(1)} %broadcast_in_dim.98), channel_id=1, replica_groups=mesh['y'=4,'z'=8,'c'=2,'x'=4] {'z'}, dimensions={0} | all-to-all | bytes 262144 | tf_op jit(solution)/shard_map/contrib_sum/all_to_all | solution.py:26
  74.9 2.4 %collective-permute-start.7 = (bf16[8,104,2048]{2,1,0:T(8,128)(2,1)}, bf16[8,104,2048]{2,1,0:T(8,128)(2,1)}, u32[]{:S(2)}, u32[]{:S(2)}) collective-permute-start(bf16[8,104,2048]{2,1,0:T(8,128)(2,1)} %bitcast.84), channel_id=1, source_target_pairs={{0,4},{4,0},{1,5},{5,1},{2,6},{6,2},{3,7},{7,3},{8,12},{12,8},{9,1... | collective-permute-start | bytes 10223624 | tf_op jit(solution)/shard_map/gather/ppermute | solution.py:35
  77.9 7.0 %root_select.1.r0_ref = bf16[2048,512]{1,0:T(8,128)(2,1)} custom-call(s32[8,1,256]{2,1,0:T(1,128)} %copy.54.at_ref, bf16[8,104,2048]{2,1,0:T(8,128)(2,1)} %bitcast.85), custom_call_target="tpu_custom_call" | custom-call | tf_op jit(solution)/shard_map/gather/root_select/pallas_call | solution.py:312
  86.7 2.6 %mid_forward.1 = (bf16[16,2048]{1,0:T(8,128)(2,1)S(1)}, bf16[16,16,512]{2,1,0:T(8,128)(2,1)S(1)}) custom-call(s32[1]{0:T(128)} %bitcast.core, bf16[16,512]{1,0:T(8,128)(2,1)S(1)} %reduce_sum.53.h_ref, bf16[8,104,2048]{2,1,0:T(8,128)(2,1)S(1)} %bitcast.88, bf16[8,104,2048]{2,1,0:T(8,128)(2,1)} %collective-permute-done.7.m1_ref.c1_ref, ...), custom_call_target="tpu_custom_call" | custom-call | tf_op jit(solution)/shard_map/mid_forward/mid_forward/pallas_call | solution.py:328
  90.1 4.2 %all-to-all-start.3 = ((bf16[16,16,512]{2,1,0:T(8,128)(2,1)}), bf16[16,16,512]{2,1,0:T(8,128)(2,1)}, u32[]{:S(2)}, u32[]{:S(2)}) async-start(bf16[16,16,512]{2,1,0:T(8,128)(2,1)} %copy-done.2), calls=%async_computation.3 | async-start | bytes 524288 | tf_op jit(solution)/shard_map/mid_forward/all_to_all | solution.py:26
  94.7 3.1 %fusion.31.base_ref = f32[4,32,256]{2,1,0:T(8,128)} fusion(bf16[4,4,32,256]{3,2,0,1:T(8,128)(2,1)} %pad_maximum_fusion.1, bf16[4,32,4,8,256]{4,3,2,1,0:T(8,128)(2,1)} %bitcast.92), kind=kOutput, calls=%fused_computation.23 | convolution fusion | flops 67108864 | bytes 2490368 | tf_op jit(solution)/shard_map/mid_backward/xlkq,lpxq->lkp/dot_general | solution.py:380
  98.5 7.3 %all-to-all-done.3.u_ref = bf16[16,16,512]{2,1,0:T(8,128)(2,1)} async-done(((bf16[16,16,512]{2,1,0:T(8,128)(2,1)}), bf16[16,16,512]{2,1,0:T(8,128)(2,1)}, u32[]{:S(2)}, u32[]{:S(2)}) %all-to-all-start.3) | async-done | bytes 262176 | tf_op jit(solution)/shard_map/mid_forward/all_to_all | solution.py:26
  105.8 4.1 %root.1 = (bf16[16,512]{1,0:T(8,128)(2,1)}, bf16[4,16,640]{2,1,0:T(8,128)(2,1)}) custom-call(bf16[16,16,512]{2,1,0:T(8,128)(2,1)} %all-to-all-done.3.u_ref, bf16[2048,512]{1,0:T(8,128)(2,1)} %root_select.1.r0_ref, bf16[2048,512]{1,0:T(8,128)(2,1)} %collective-permute-done.8.r1_ref, f32[16,512]{1,0:T(8,128)} %convert_add_fusion.pre_ref, ...), custom_call_target="tpu_custom_call" | custom-call | tf_op jit(solution)/shard_map/root/root/pallas_call | solution.py:345
  111.3 3.3 %all-to-all-start.4 = ((bf16[4,16,640]{2,1,0:T(8,128)(2,1)}), bf16[4,16,640]{2,1,0:T(8,128)(2,1)S(1)}, u32[]{:S(2)}, u32[]{:S(2)}) async-start(bf16[4,16,640]{2,1,0:T(8,128)(2,1)} %get-tuple-element.31), calls=%async_computation.4 | async-start | bytes 163840 | tf_op jit(solution)/shard_map/root/all_to_all | solution.py:26
  116.2 3.8 %all-to-all-done.4.cp_ref = bf16[4,16,640]{2,1,0:T(8,128)(2,1)S(1)} async-done(((bf16[4,16,640]{2,1,0:T(8,128)(2,1)}), bf16[4,16,640]{2,1,0:T(8,128)(2,1)S(1)}, u32[]{:S(2)}, u32[]{:S(2)}) %all-to-all-start.4) | async-done | bytes 81952 | tf_op jit(solution)/shard_map/root/all_to_all | solution.py:26
  120.1 3.3 %collective-permute-start.15 = (f32[16,32]{1,0:T(8,128)S(1)}, f32[16,32]{1,0:T(8,128)S(1)}, u32[]{:S(2)}, u32[]{:S(2)}) collective-permute-start(f32[16,32]{1,0:T(8,128)S(1)} %slice.43), channel_id=1, source_target_pairs={{0,4},{4,0},{1,5},{5,1},{2,6},{6,2},{3,7},{7,3},{8,12},{12,8},{9,1... | collective-permute-start | bytes 6152 | tf_op jit(solution)/shard_map/outputs/ppermute | solution.py:35
  124.7 4.3 %mid_backward.1 = bf16[16,16,512]{2,1,0:T(8,128)(2,1)} custom-call(s32[1]{0:T(128)} %bitcast.core, bf16[4,16,640]{2,1,0:T(8,128)(2,1)} %copy-done.8, bf16[16,2048]{1,0:T(8,128)(2,1)} %copy-done.3, bf16[16,2048]{1,0:T(8,128)(2,1)} %copy-done.13, bf16[16,2048]{1,0:T(8,128)(2,1)} %copy-done.14, bf16[16,2048]{1,0:T(8,128)(2,1)} %copy-done.15, ...), custom_call_target="tpu_custom_call" | custom-call | tf_op jit(solution)/shard_map/mid_backward/mid_backward/pallas_call | solution.py:360
  129.0 5.7 %all-to-all-start.5 = ((bf16[16,16,512]{2,1,0:T(8,128)(2,1)}), bf16[16,16,512]{2,1,0:T(8,128)(2,1)S(1)}, u32[]{:S(2)}, u32[]{:S(2)}) async-start(bf16[16,16,512]{2,1,0:T(8,128)(2,1)} %mid_backward.1), calls=%async_computation.5 | async-start | bytes 524288 | tf_op jit(solution)/shard_map/mid_backward/all_to_all | solution.py:26
  134.7 4.4 %bitcast_convert_fusion.n_ref = bf16[4,256,512]{2,1,0:T(8,128)(2,1)} fusion(bf16[4,4,256,512]{3,2,1,0:T(8,128)(2,1)} %bitcast.99, bf16[4,32,4,8,256]{4,3,2,1,0:T(8,128)(2,1)S(1)} %bitcast.93), kind=kOutput, calls=%fused_computation.17 | convolution fusion | flops 1074266112 | bytes 7340032 | tf_op jit(solution)/shard_map/mid_backward/lpxq,xlqc->lpc/dot_general | solution.py:374
  139.2 4.1 %all-to-all-done.5 = bf16[16,16,512]{2,1,0:T(8,128)(2,1)S(1)} async-done(((bf16[16,16,512]{2,1,0:T(8,128)(2,1)}), bf16[16,16,512]{2,1,0:T(8,128)(2,1)S(1)}, u32[]{:S(2)}, u32[]{:S(2)}) %all-to-all-start.5) | async-done | bytes 262176 | tf_op jit(solution)/shard_map/mid_backward/all_to_all | solution.py:26
  146.9 5.1 %leaf_backward.1 = f32[4,32,256]{2,1,0:T(8,128)} custom-call(s32[4]{0:T(128)} %parent.1, s32[1]{0:T(128)} %bitcast.core, bf16[4,16,2048]{2,1,0:T(8,128)(2,1)} %copy-done.6, bf16[4,16,2048]{2,1,0:T(8,128)(2,1)} %copy-done.9, s32[4,1,512]{2,1,0:T(1,128)} %broadcast_in_dim.101.at_ref, bf16[4,256,512]{2,1,0:T(8,128)(2,1)} %bitcast_convert_fusion.n_ref, ...), custom_call_target="tpu_custom_call" | custom-call | tf_op jit(solution)/shard_map/leaf_backward/leaf_backward/pallas_call | solution.py:386
  (129 shorter events, 30.7 us)
Async XLA Ops:
  7.2 67.7 %all-gather.5.cloned.1.call-start = ((), (), s32[]{:S(2)}) async-start(), calls=%async_computation.6 | async-start | bytes 3833856 | tf_op jit(solution)/shard_map/gather/all_gather | solution.py:271
  8.8 6.8 %collective-permute-start.4 = (bf16[96,512]{1,0:T(8,128)(2,1)}, bf16[96,512]{1,0:T(8,128)(2,1)S(1)}, u32[]{:S(2)}, u32[]{:S(2)}) collective-permute-start(bf16[96,512]{1,0:T(8,128)(2,1)} %get-tuple-element.24.g0), channel_id=1, source_target_pairs={{64,0},{128,64},{192,128},{0,192},{65,1},{129,65},{193,129},{1,193... | collective-permute-start | bytes 294920 | tf_op jit(solution)/shard_map/gather/ppermute | solution.py:41
  12.4 5.3 %collective-permute-start.5 = (bf16[96,512]{1,0:T(8,128)(2,1)}, bf16[96,512]{1,0:T(8,128)(2,1)S(1)}, u32[]{:S(2)}, u32[]{:S(2)}) collective-permute-start(bf16[96,512]{1,0:T(8,128)(2,1)} %get-tuple-element.24.g0), channel_id=1, source_target_pairs={{128,0},{192,64},{0,128},{64,192},{129,1},{193,65},{1,129},{65,193... | collective-permute-start | bytes 294920 | tf_op jit(solution)/shard_map/gather/ppermute | solution.py:41
  12.7 7.7 %collective-permute-start.6 = (bf16[96,512]{1,0:T(8,128)(2,1)}, bf16[96,512]{1,0:T(8,128)(2,1)S(1)}, u32[]{:S(2)}, u32[]{:S(2)}) collective-permute-start(bf16[96,512]{1,0:T(8,128)(2,1)} %get-tuple-element.24.g0), channel_id=1, source_target_pairs={{192,0},{0,64},{64,128},{128,192},{193,1},{1,65},{65,129},{129,193... | collective-permute-start | bytes 294920 | tf_op jit(solution)/shard_map/gather/ppermute | solution.py:41
  24.0 9.6 %all-to-all-start = ((bf16[4,4,32,256]{3,2,1,0:T(8,128)(2,1)}), bf16[4,4,32,256]{3,2,1,0:T(8,128)(2,1)S(1)}, u32[]{:S(2)}, u32[]{:S(2)}) async-start(bf16[4,4,32,256]{3,2,1,0:T(8,128)(2,1)} %copy.49), calls=%async_computation | async-start | bytes 524288 | tf_op jit(solution)/shard_map/leaf_forward/all_to_all | solution.py:26
  37.4 7.7 %collective-permute-start = (bf16[4,16,2048]{2,1,0:T(8,128)(2,1)S(1)}, bf16[4,16,2048]{2,1,0:T(8,128)(2,1)S(1)}, u32[]{:S(2)}, u32[]{:S(2)}) collective-permute-start(bf16[4,16,2048]{2,1,0:T(8,128)(2,1)S(1)} %pad_maximum_fusion), channel_id=1, source_target_pairs={{0,4},{4,0},{1,5},{5,1},{2,6},{6,2},{3,7},{7,3},{8,12},{12,8},{9,1... | collective-permute-start | bytes 786440 | tf_op jit(solution)/shard_map/contrib_sum/ppermute | solution.py:35
  40.2 10.0 %collective-permute-start.2 = (bf16[4,32,256]{2,1,0:T(8,128)(2,1)S(1)}, bf16[4,32,256]{2,1,0:T(8,128)(2,1)S(1)}, u32[]{:S(2)}, u32[]{:S(2)}) collective-permute-start(bf16[4,32,256]{2,1,0:T(8,128)(2,1)S(1)} %select_convert_fusion.1), channel_id=1, source_target_pairs={{2,0},{3,1},{0,2},{1,3},{6,4},{7,5},{4,6},{5,7},{10,8},{11,9},{8,1... | collective-permute-start | bytes 196616 | tf_op jit(solution)/shard_map/contrib_sum/ppermute | solution.py:41
  42.5 7.7 %collective-permute-start.3 = (bf16[4,32,256]{2,1,0:T(8,128)(2,1)S(1)}, bf16[4,32,256]{2,1,0:T(8,128)(2,1)S(1)}, u32[]{:S(2)}, u32[]{:S(2)}) collective-permute-start(bf16[4,32,256]{2,1,0:T(8,128)(2,1)S(1)} %select_convert_fusion.1), channel_id=1, source_target_pairs={{3,0},{0,1},{1,2},{2,3},{7,4},{4,5},{5,6},{6,7},{11,8},{8,9},{9,10... | collective-permute-start | bytes 196616 | tf_op jit(solution)/shard_map/contrib_sum/ppermute | solution.py:41
  42.8 7.4 %collective-permute-start.1 = (bf16[4,32,256]{2,1,0:T(8,128)(2,1)S(1)}, bf16[4,32,256]{2,1,0:T(8,128)(2,1)S(1)}, u32[]{:S(2)}, u32[]{:S(2)}) collective-permute-start(bf16[4,32,256]{2,1,0:T(8,128)(2,1)S(1)} %select_convert_fusion.1), channel_id=1, source_target_pairs={{1,0},{2,1},{3,2},{0,3},{5,4},{6,5},{7,6},{4,7},{9,8},{10,9},{11,1... | collective-permute-start | bytes 196616 | tf_op jit(solution)/shard_map/contrib_sum/ppermute | solution.py:41
  46.5 11.4 %all-to-all-start.1 = ((bf16[16,16,512]{2,1,0:T(8,128)(2,1)}), bf16[16,16,512]{2,1,0:T(8,128)(2,1)S(1)}, u32[]{:S(2)}, u32[]{:S(2)}) async-start(bf16[16,16,512]{2,1,0:T(8,128)(2,1)} %reshape.168), calls=%async_computation.1 | async-start | bytes 524288 | tf_op jit(solution)/shard_map/contrib_sum/all_to_all | solution.py:26
  50.1 84.6 %all-gather.7.cloned.1.call-start = ((), (), s32[]{:S(2)}) async-start(), calls=%async_computation.7 | async-start | bytes 5242880 | tf_op jit(solution)/shard_map/contrib_sum/all_gather | solution.py:302
  74.9 11.9 %collective-permute-start.7 = (bf16[8,104,2048]{2,1,0:T(8,128)(2,1)}, bf16[8,104,2048]{2,1,0:T(8,128)(2,1)}, u32[]{:S(2)}, u32[]{:S(2)}) collective-permute-start(bf16[8,104,2048]{2,1,0:T(8,128)(2,1)} %bitcast.84), channel_id=1, source_target_pairs={{0,4},{4,0},{1,5},{5,1},{2,6},{6,2},{3,7},{7,3},{8,12},{12,8},{9,1... | collective-permute-start | bytes 10223624 | tf_op jit(solution)/shard_map/gather/ppermute | solution.py:35
  84.9 9.3 %collective-permute-start.8 = (bf16[2048,512]{1,0:T(8,128)(2,1)}, bf16[2048,512]{1,0:T(8,128)(2,1)}, u32[]{:S(2)}, u32[]{:S(2)}) collective-permute-start(bf16[2048,512]{1,0:T(8,128)(2,1)} %root_select.1.r0_ref), channel_id=1, source_target_pairs={{0,4},{4,0},{1,5},{5,1},{2,6},{6,2},{3,7},{7,3},{8,12},{12,8},{9,1... | collective-permute-start | bytes 6291464 | tf_op jit(solution)/shard_map/gather/ppermute | solution.py:35
  85.0 13.5 %collective-permute-start.10 = (bf16[32,512]{1,0:T(8,128)(2,1)}, bf16[32,512]{1,0:T(8,128)(2,1)}, u32[]{:S(2)}, u32[]{:S(2)}) collective-permute-start(bf16[32,512]{1,0:T(8,128)(2,1)} %get-tuple-element.30.w0_ref), channel_id=1, source_target_pairs={{0,4},{4,0},{1,5},{5,1},{2,6},{6,2},{3,7},{7,3},{8,12},{12,8},{9,1... | collective-permute-start | bytes 98312 | tf_op jit(solution)/shard_map/gather/ppermute | solution.py:35
  90.0 20.6 %copy-start.3 = (bf16[16,2048]{1,0:T(8,128)(2,1)}, bf16[16,2048]{1,0:T(8,128)(2,1)S(1)}, u32[]{:S(2)}) copy-start(bf16[16,2048]{1,0:T(8,128)(2,1)S(1)} %get-tuple-element.33.y0) | copy-start | bytes 196612
  90.1 15.7 %all-to-all-start.3 = ((bf16[16,16,512]{2,1,0:T(8,128)(2,1)}), bf16[16,16,512]{2,1,0:T(8,128)(2,1)}, u32[]{:S(2)}, u32[]{:S(2)}) async-start(bf16[16,16,512]{2,1,0:T(8,128)(2,1)} %copy-done.2), calls=%async_computation.3 | async-start | bytes 524288 | tf_op jit(solution)/shard_map/mid_forward/all_to_all | solution.py:26
  94.3 3.5 %collective-permute-start.9 = (bf16[16,512]{1,0:T(8,128)(2,1)S(1)}, bf16[16,512]{1,0:T(8,128)(2,1)S(1)}, u32[]{:S(2)}, u32[]{:S(2)}) collective-permute-start(bf16[16,512]{1,0:T(8,128)(2,1)S(1)} %select_convert_fusion.2), channel_id=1, source_target_pairs={{0,4},{4,0},{1,5},{5,1},{2,6},{6,2},{3,7},{7,3},{8,12},{12,8},{9,1... | collective-permute-start | bytes 49160 | tf_op jit(solution)/shard_map/mid_forward/ppermute | solution.py:35
  109.8 13.6 %collective-permute-start.11 = (bf16[16,2048]{1,0:T(8,128)(2,1)S(1)}, bf16[16,2048]{1,0:T(8,128)(2,1)S(1)}, u32[]{:S(2)}, u32[]{:S(2)}) collective-permute-start(bf16[16,2048]{1,0:T(8,128)(2,1)S(1)} %get-tuple-element.33.y0), channel_id=1, source_target_pairs={{64,0},{128,64},{192,128},{0,192},{65,1},{129,65},{193,129},{1,193... | collective-permute-start | bytes 196616 | tf_op jit(solution)/shard_map/root/ppermute | solution.py:41
  110.4 13.1 %collective-permute-start.12 = (bf16[16,2048]{1,0:T(8,128)(2,1)S(1)}, bf16[16,2048]{1,0:T(8,128)(2,1)S(1)}, u32[]{:S(2)}, u32[]{:S(2)}) collective-permute-start(bf16[16,2048]{1,0:T(8,128)(2,1)S(1)} %get-tuple-element.33.y0), channel_id=1, source_target_pairs={{128,0},{192,64},{0,128},{64,192},{129,1},{193,65},{1,129},{65,193... | collective-permute-start | bytes 196616 | tf_op jit(solution)/shard_map/root/ppermute | solution.py:41
  110.7 12.8 %collective-permute-start.13 = (bf16[16,2048]{1,0:T(8,128)(2,1)S(1)}, bf16[16,2048]{1,0:T(8,128)(2,1)S(1)}, u32[]{:S(2)}, u32[]{:S(2)}) collective-permute-start(bf16[16,2048]{1,0:T(8,128)(2,1)S(1)} %get-tuple-element.33.y0), channel_id=1, source_target_pairs={{192,0},{0,64},{64,128},{128,192},{193,1},{1,65},{65,129},{129,193... | collective-permute-start | bytes 196616 | tf_op jit(solution)/shard_map/root/ppermute | solution.py:41
  111.3 8.7 %all-to-all-start.4 = ((bf16[4,16,640]{2,1,0:T(8,128)(2,1)}), bf16[4,16,640]{2,1,0:T(8,128)(2,1)S(1)}, u32[]{:S(2)}, u32[]{:S(2)}) async-start(bf16[4,16,640]{2,1,0:T(8,128)(2,1)} %get-tuple-element.31), calls=%async_computation.4 | async-start | bytes 163840 | tf_op jit(solution)/shard_map/root/all_to_all | solution.py:26
  120.1 24.9 %collective-permute-start.15 = (f32[16,32]{1,0:T(8,128)S(1)}, f32[16,32]{1,0:T(8,128)S(1)}, u32[]{:S(2)}, u32[]{:S(2)}) collective-permute-start(f32[16,32]{1,0:T(8,128)S(1)} %slice.43), channel_id=1, source_target_pairs={{0,4},{4,0},{1,5},{5,1},{2,6},{6,2},{3,7},{7,3},{8,12},{12,8},{9,1... | collective-permute-start | bytes 6152 | tf_op jit(solution)/shard_map/outputs/ppermute | solution.py:35
  129.0 14.2 %all-to-all-start.5 = ((bf16[16,16,512]{2,1,0:T(8,128)(2,1)}), bf16[16,16,512]{2,1,0:T(8,128)(2,1)S(1)}, u32[]{:S(2)}, u32[]{:S(2)}) async-start(bf16[16,16,512]{2,1,0:T(8,128)(2,1)} %mid_backward.1), calls=%async_computation.5 | async-start | bytes 524288 | tf_op jit(solution)/shard_map/mid_backward/all_to_all | solution.py:26
  143.8 2.3 %collective-permute-start.14 = (bf16[4,16,2048]{2,1,0:T(8,128)(2,1)S(1)}, bf16[4,16,2048]{2,1,0:T(8,128)(2,1)S(1)}, u32[]{:S(2)}, u32[]{:S(2)}) collective-permute-start(bf16[4,16,2048]{2,1,0:T(8,128)(2,1)S(1)} %reshape.174.x0_ref), channel_id=1, source_target_pairs={{0,4},{4,0},{1,5},{5,1},{2,6},{6,2},{3,7},{7,3},{8,12},{12,8},{9,1... | collective-permute-start | bytes 786440 | tf_op jit(solution)/shard_map/mid_backward/ppermute | solution.py:35
  (24 other events, 171.7 us)
Sparse Core Ops, SparseCore 0:
  23.3 49.2 all-gather.4
  74.4 54.9 all-gather.6

commit v5 on v4

--- a/solution.py
+++ b/solution.py
@@ -369,7 +369,7 @@
             name="mid_backward",
         )(core, coupled, *ys, w0, w1, w0, w1)
         rx = jnp.sum(coupled[:, :, ncpl : ncpl + nc * rows].astype(F32), 0)
-        alive = lax.iota(jnp.int32, order)[None, :] < leaf_size[:, None]
+        alive = lax.iota(jnp.int32, order)[None, :] < after(leaf_size, root_y)[:, None]
         inv_m = jnp.where(alive[:, None, :], after(leaf_inv, root_y), 0)
         nmat = jnp.einsum(
             "lpxq,xlqc->lpc",
@@ -398,9 +398,9 @@
                 out_specs=pl.BlockSpec((1, nk, share), lambda i, *_: (i, 0, 0)),
             ),
             out_shape=jax.ShapeDtypeStruct((nl, nk, share), F32),
-            compiler_params=PARAMS,
+            compiler_params=pltpu.CompilerParams(vmem_limit_bytes=40 * 2**20),
             name="leaf_backward",
-        )(leaf_parent, core, mx, mo, target[:, None, :], nmat, base)
+        )(leaf_parent, core, mx, mo, after(target, root_y)[:, None, :], nmat, base)
 
     with jax.named_scope("outputs"):
 

time: 160 us -> 157 us (0.981)
  Pallas kernels: 26.8 us -> 25.1 us
  transfers between devices with their start and end apart: 23 -> 23, of which waited for: 7 -> 7; matrix products, arithmetic and copies ran while one was open for 17% -> 16% of each run, Pallas kernels for 11% -> 11%
where the time goes in v5:
time: 157 us; the launch traced here: 156 us
  starting transfers between devices  42.2 us (27%)
  waiting for transfers between devices  28.4 us (18%)
  Pallas kernels  25.1 us (16%)
  matrix products  17.6 us (11%)
  blocking collectives  16.8 us (11%)
  between operations  14.6 us (9%)
  local copies, waits for them, and re-layouts  6 us (4%)
  other arithmetic  4.99 us (3%)
    all_to_all x5, waiting for transfers between devices, a2a(): return lax.all_to_all(v, axes, 0, 0, tiled=True)  23 us
    all_to_all x5, starting transfers between devices, a2a(): return lax.all_to_all(v, axes, 0, 0, tiled=True)  20.6 us
    all_to_all x1, blocking collectives, a2a(): return lax.all_to_all(v, axes, 0, 0, tiled=True)  16.8 us
    ppermute x9, starting transfers between devices, ahead(): lax.ppermute(v, axis, [((i + k) % n, i) for i in range(n)])  11.1 us
    ppermute x7, starting transfers between devices, swap(): return lax.ppermute(v, 'c', [(0, 1), (1, 0)])  10.5 us
    pallas_call x1, Pallas kernels, body(): pl.pallas_call(select_kernel, grid=(nmid * ncpl // tile,), in_specs=[pl.B...  7.02 us
    dot_general x1, matrix products, body(): jnp.einsum('lcn,lpc->lnp', hot, leaf_cpl, preferred_element_type=F32)  5.08 us
    ppermute x9, waiting for transfers between devices, ahead(): lax.ppermute(v, axis, [((i + k) % n, i) for i in range(n)])  4.8 us
  transfers between devices with their start and end apart: 23, of which 7 were waited for; matrix products, arithmetic and copies ran while one was open for 16% of the time, Pallas kernels for 11%

profile of v5, /device:TPU:1, one launch (start us, length us, event | category | flops | bytes accessed | tf_op | source)
XLA Modules:
  0.0 155.8 jit_solution(7397721750900982399)
XLA Ops:
  8.8 3.6 %collective-permute-start.4 = (bf16[96,512]{1,0:T(8,128)(2,1)}, bf16[96,512]{1,0:T(8,128)(2,1)S(1)}, u32[]{:S(2)}, u32[]{:S(2)}) collective-permute-start(bf16[96,512]{1,0:T(8,128)(2,1)} %get-tuple-element.26.g0), channel_id=1, source_target_pairs={{64,0},{128,64},{192,128},{0,192},{65,1},{129,65},{193,129},{1,193... | collective-permute-start | bytes 294920 | tf_op jit(solution)/shard_map/gather/ppermute | solution.py:41
  17.6 2.7 %collective-permute-done.6.g3 = bf16[96,512]{1,0:T(8,128)(2,1)S(1)} collective-permute-done((bf16[96,512]{1,0:T(8,128)(2,1)}, bf16[96,512]{1,0:T(8,128)(2,1)S(1)}, u32[]{:S(2)}, u32[]{:S(2)}) %collective-permute-start.6) | collective-permute-done | bytes 98336 | tf_op jit(solution)/shard_map/gather/ppermute | solution.py:41
  23.9 4.0 %all-to-all-start = ((bf16[4,4,32,256]{3,2,1,0:T(8,128)(2,1)}), bf16[4,4,32,256]{3,2,1,0:T(8,128)(2,1)S(1)}, u32[]{:S(2)}, u32[]{:S(2)}) async-start(bf16[4,4,32,256]{3,2,1,0:T(8,128)(2,1)} %copy.49), calls=%async_computation | async-start | bytes 524288 | tf_op jit(solution)/shard_map/leaf_forward/all_to_all | solution.py:26
  28.4 5.1 %fusion = bf16[4,2048,256]{2,1,0:T(8,128)(2,1)} fusion(bf16[4,256,512]{2,1,0:T(8,128)(2,1)S(1)} %copy-done.7, s32[4,512]{1,0:T(4,128)S(1)} %fusion.46), kind=kOutput, calls=%fused_computation.1 | convolution fusion | flops 2151677952 | bytes 5251072 | tf_op jit(solution)/shard_map/leaf_spread/lcn,lpc->lnp/dot_general | solution.py:276
  33.6 3.7 %fusion.10 = f32[4,32,2048]{2,1,0:T(8,128)S(1)} fusion(bf16[4,2048,256]{2,1,0:T(8,128)(2,1)} %fusion, f32[32,2048]{1,0:T(8,128)S(1)} %convolution_bitcast_fusion, pred[4]{0:T(512)(128)(4,1)S(1)} %iota_compare_fusion.6, pred[4,4]{1,0:T(4,128)(4,1)S(1)} %iota_compare_fusion.5, bf16[32,4,256]{2,0,1:T(8,128)(2,1)S(1)} %fusion.71), kind=kOutput, calls=%fused_computation.9 | convolution fusion | flops 537526272 | bytes 5570580 | tf_op jit(solution)/shard_map/leaf_spread/mlp,lnp->mn/dot_general | solution.py:281
  37.4 2.5 %collective-permute-start = (bf16[4,16,2048]{2,1,0:T(8,128)(2,1)S(1)}, bf16[4,16,2048]{2,1,0:T(8,128)(2,1)S(1)}, u32[]{:S(2)}, u32[]{:S(2)}) collective-permute-start(bf16[4,16,2048]{2,1,0:T(8,128)(2,1)S(1)} %pad_maximum_fusion), channel_id=1, source_target_pairs={{0,4},{4,0},{1,5},{5,1},{2,6},{6,2},{3,7},{7,3},{8,12},{12,8},{9,1... | collective-permute-start | bytes 786440 | tf_op jit(solution)/shard_map/contrib_sum/ppermute | solution.py:35
  46.5 3.5 %all-to-all-start.1 = ((bf16[16,16,512]{2,1,0:T(8,128)(2,1)}), bf16[16,16,512]{2,1,0:T(8,128)(2,1)S(1)}, u32[]{:S(2)}, u32[]{:S(2)}) async-start(bf16[16,16,512]{2,1,0:T(8,128)(2,1)} %reshape.170), calls=%async_computation.1 | async-start | bytes 524288 | tf_op jit(solution)/shard_map/contrib_sum/all_to_all | solution.py:26
  51.0 6.9 %all-to-all-done.1 = bf16[16,16,512]{2,1,0:T(8,128)(2,1)S(1)} async-done(((bf16[16,16,512]{2,1,0:T(8,128)(2,1)}), bf16[16,16,512]{2,1,0:T(8,128)(2,1)S(1)}, u32[]{:S(2)}, u32[]{:S(2)}) %all-to-all-start.1) | async-done | bytes 262176 | tf_op jit(solution)/shard_map/contrib_sum/all_to_all | solution.py:26
  58.0 16.8 %all_to_all.30 = bf16[8,16,512]{2,1,0:T(8,128)(2,1)S(1)} all-to-all(bf16[8,16,512]{2,1,0:T(8,128)(2,1)S(1)} %broadcast_in_dim.98), channel_id=1, replica_groups=mesh['y'=4,'z'=8,'c'=2,'x'=4] {'z'}, dimensions={0} | all-to-all | bytes 262144 | tf_op jit(solution)/shard_map/contrib_sum/all_to_all | solution.py:26
  74.8 2.4 %collective-permute-start.7 = (bf16[8,104,2048]{2,1,0:T(8,128)(2,1)}, bf16[8,104,2048]{2,1,0:T(8,128)(2,1)}, u32[]{:S(2)}, u32[]{:S(2)}) collective-permute-start(bf16[8,104,2048]{2,1,0:T(8,128)(2,1)} %bitcast.84), channel_id=1, source_target_pairs={{0,4},{4,0},{1,5},{5,1},{2,6},{6,2},{3,7},{7,3},{8,12},{12,8},{9,1... | collective-permute-start | bytes 10223624 | tf_op jit(solution)/shard_map/gather/ppermute | solution.py:35
  77.9 7.0 %root_select.1.r0_ref = bf16[2048,512]{1,0:T(8,128)(2,1)} custom-call(s32[8,1,256]{2,1,0:T(1,128)} %copy.54.at_ref, bf16[8,104,2048]{2,1,0:T(8,128)(2,1)} %bitcast.85), custom_call_target="tpu_custom_call" | custom-call | tf_op jit(solution)/shard_map/gather/root_select/pallas_call | solution.py:312
  85.4 2.5 %mid_forward.1 = (bf16[16,2048]{1,0:T(8,128)(2,1)S(1)}, bf16[16,16,512]{2,1,0:T(8,128)(2,1)S(1)}) custom-call(s32[1]{0:T(128)} %bitcast.core, bf16[16,512]{1,0:T(8,128)(2,1)S(1)} %reduce_sum.53.h_ref, bf16[8,104,2048]{2,1,0:T(8,128)(2,1)S(1)} %bitcast.88, bf16[8,104,2048]{2,1,0:T(8,128)(2,1)} %collective-permute-done.7.m1_ref.c1_ref, ...), custom_call_target="tpu_custom_call" | custom-call | tf_op jit(solution)/shard_map/mid_forward/mid_forward/pallas_call | solution.py:328
  88.6 4.2 %all-to-all-start.3 = ((bf16[16,16,512]{2,1,0:T(8,128)(2,1)}), bf16[16,16,512]{2,1,0:T(8,128)(2,1)}, u32[]{:S(2)}, u32[]{:S(2)}) async-start(bf16[16,16,512]{2,1,0:T(8,128)(2,1)} %copy-done.2), calls=%async_computation.3 | async-start | bytes 524288 | tf_op jit(solution)/shard_map/mid_forward/all_to_all | solution.py:26
  93.3 2.4 %fusion.31.base_ref = f32[4,32,256]{2,1,0:T(8,128)S(1)} fusion(bf16[4,4,32,256]{3,2,0,1:T(8,128)(2,1)} %pad_maximum_fusion.1, bf16[4,32,4,8,256]{4,3,2,1,0:T(8,128)(2,1)} %bitcast.92), kind=kOutput, calls=%fused_computation.23 | convolution fusion | flops 67108864 | bytes 2490368 | tf_op jit(solution)/shard_map/mid_backward/xlkq,lpxq->lkp/dot_general | solution.py:380
  96.4 8.0 %all-to-all-done.3.u_ref = bf16[16,16,512]{2,1,0:T(8,128)(2,1)} async-done(((bf16[16,16,512]{2,1,0:T(8,128)(2,1)}), bf16[16,16,512]{2,1,0:T(8,128)(2,1)}, u32[]{:S(2)}, u32[]{:S(2)}) %all-to-all-start.3) | async-done | bytes 262176 | tf_op jit(solution)/shard_map/mid_forward/all_to_all | solution.py:26
  104.4 4.0 %root.1 = (bf16[16,512]{1,0:T(8,128)(2,1)}, bf16[4,16,640]{2,1,0:T(8,128)(2,1)}) custom-call(bf16[16,16,512]{2,1,0:T(8,128)(2,1)} %all-to-all-done.3.u_ref, bf16[2048,512]{1,0:T(8,128)(2,1)} %root_select.1.r0_ref, bf16[2048,512]{1,0:T(8,128)(2,1)} %collective-permute-done.8.r1_ref, f32[16,512]{1,0:T(8,128)} %convert_add_fusion.pre_ref, ...), custom_call_target="tpu_custom_call" | custom-call | tf_op jit(solution)/shard_map/root/root/pallas_call | solution.py:345
  109.9 3.3 %all-to-all-start.4 = ((bf16[4,16,640]{2,1,0:T(8,128)(2,1)}), bf16[4,16,640]{2,1,0:T(8,128)(2,1)S(1)}, u32[]{:S(2)}, u32[]{:S(2)}) async-start(bf16[4,16,640]{2,1,0:T(8,128)(2,1)} %get-tuple-element.33), calls=%async_computation.4 | async-start | bytes 163840 | tf_op jit(solution)/shard_map/root/all_to_all | solution.py:26
  114.9 3.7 %all-to-all-done.4.cp_ref = bf16[4,16,640]{2,1,0:T(8,128)(2,1)S(1)} async-done(((bf16[4,16,640]{2,1,0:T(8,128)(2,1)}), bf16[4,16,640]{2,1,0:T(8,128)(2,1)S(1)}, u32[]{:S(2)}, u32[]{:S(2)}) %all-to-all-start.4) | async-done | bytes 81952 | tf_op jit(solution)/shard_map/root/all_to_all | solution.py:26
  118.7 3.5 %collective-permute-start.15 = (f32[16,32]{1,0:T(8,128)S(1)}, f32[16,32]{1,0:T(8,128)S(1)}, u32[]{:S(2)}, u32[]{:S(2)}) collective-permute-start(f32[16,32]{1,0:T(8,128)S(1)} %slice.43), channel_id=1, source_target_pairs={{0,4},{4,0},{1,5},{5,1},{2,6},{6,2},{3,7},{7,3},{8,12},{12,8},{9,1... | collective-permute-start | bytes 6152 | tf_op jit(solution)/shard_map/outputs/ppermute | solution.py:35
  123.4 4.3 %mid_backward.1 = bf16[16,16,512]{2,1,0:T(8,128)(2,1)} custom-call(s32[1]{0:T(128)} %bitcast.core, bf16[4,16,640]{2,1,0:T(8,128)(2,1)} %copy-done.8, bf16[16,2048]{1,0:T(8,128)(2,1)} %copy-done.3, bf16[16,2048]{1,0:T(8,128)(2,1)} %copy-done.12, bf16[16,2048]{1,0:T(8,128)(2,1)} %copy-done.13, bf16[16,2048]{1,0:T(8,128)(2,1)} %copy-done.14, ...), custom_call_target="tpu_custom_call" | custom-call | tf_op jit(solution)/shard_map/mid_backward/mid_backward/pallas_call | solution.py:360
  127.7 5.5 %all-to-all-start.5 = ((bf16[16,16,512]{2,1,0:T(8,128)(2,1)}), bf16[16,16,512]{2,1,0:T(8,128)(2,1)S(1)}, u32[]{:S(2)}, u32[]{:S(2)}) async-start(bf16[16,16,512]{2,1,0:T(8,128)(2,1)} %mid_backward.1), calls=%async_computation.5 | async-start | bytes 524288 | tf_op jit(solution)/shard_map/mid_backward/all_to_all | solution.py:26
  133.3 4.1 %bitcast_convert_fusion.n_ref = bf16[4,256,512]{2,1,0:T(8,128)(2,1)S(1)} fusion(bf16[4,4,256,512]{3,2,1,0:T(8,128)(2,1)} %bitcast.99, bf16[4,32,4,8,256]{4,3,2,1,0:T(8,128)(2,1)} %bitcast.93), kind=kOutput, calls=%fused_computation.17 | convolution fusion | flops 1074266112 | bytes 7340032 | tf_op jit(solution)/shard_map/mid_backward/lpxq,xlqc->lpc/dot_general | solution.py:374
  137.3 4.4 %all-to-all-done.5 = bf16[16,16,512]{2,1,0:T(8,128)(2,1)S(1)} async-done(((bf16[16,16,512]{2,1,0:T(8,128)(2,1)}), bf16[16,16,512]{2,1,0:T(8,128)(2,1)S(1)}, u32[]{:S(2)}, u32[]{:S(2)}) %all-to-all-start.5) | async-done | bytes 262176 | tf_op jit(solution)/shard_map/mid_backward/all_to_all | solution.py:26
  145.4 3.6 %leaf_backward.1 = f32[4,32,256]{2,1,0:T(8,128)} custom-call(s32[4]{0:T(128)S(1)} %copy-done.5, s32[1]{0:T(128)} %bitcast.core, bf16[4,16,2048]{2,1,0:T(8,128)(2,1)S(1)} %reshape.176.x0_ref, bf16[4,16,2048]{2,1,0:T(8,128)(2,1)S(1)} %collective-permute-done.14.x1_ref, s32[4,1,512]{2,1,0:T(1,128)S(1)} %broadcast_in_dim.101.at_ref, ...), custom_call_target="tpu_custom_call" | custom-call | tf_op jit(solution)/shard_map/leaf_backward/leaf_backward/pallas_call | solution.py:386
  (123 shorter events, 29.5 us)
Async XLA Ops:
  7.2 67.7 %all-gather.5.cloned.1.call-start = ((), (), s32[]{:S(2)}) async-start(), calls=%async_computation.6 | async-start | bytes 3833856 | tf_op jit(solution)/shard_map/gather/all_gather | solution.py:271
  8.8 6.8 %collective-permute-start.4 = (bf16[96,512]{1,0:T(8,128)(2,1)}, bf16[96,512]{1,0:T(8,128)(2,1)S(1)}, u32[]{:S(2)}, u32[]{:S(2)}) collective-permute-start(bf16[96,512]{1,0:T(8,128)(2,1)} %get-tuple-element.26.g0), channel_id=1, source_target_pairs={{64,0},{128,64},{192,128},{0,192},{65,1},{129,65},{193,129},{1,193... | collective-permute-start | bytes 294920 | tf_op jit(solution)/shard_map/gather/ppermute | solution.py:41
  12.4 5.3 %collective-permute-start.5 = (bf16[96,512]{1,0:T(8,128)(2,1)}, bf16[96,512]{1,0:T(8,128)(2,1)S(1)}, u32[]{:S(2)}, u32[]{:S(2)}) collective-permute-start(bf16[96,512]{1,0:T(8,128)(2,1)} %get-tuple-element.26.g0), channel_id=1, source_target_pairs={{128,0},{192,64},{0,128},{64,192},{129,1},{193,65},{1,129},{65,193... | collective-permute-start | bytes 294920 | tf_op jit(solution)/shard_map/gather/ppermute | solution.py:41
  12.7 7.7 %collective-permute-start.6 = (bf16[96,512]{1,0:T(8,128)(2,1)}, bf16[96,512]{1,0:T(8,128)(2,1)S(1)}, u32[]{:S(2)}, u32[]{:S(2)}) collective-permute-start(bf16[96,512]{1,0:T(8,128)(2,1)} %get-tuple-element.26.g0), channel_id=1, source_target_pairs={{192,0},{0,64},{64,128},{128,192},{193,1},{1,65},{65,129},{129,193... | collective-permute-start | bytes 294920 | tf_op jit(solution)/shard_map/gather/ppermute | solution.py:41
  23.9 9.6 %all-to-all-start = ((bf16[4,4,32,256]{3,2,1,0:T(8,128)(2,1)}), bf16[4,4,32,256]{3,2,1,0:T(8,128)(2,1)S(1)}, u32[]{:S(2)}, u32[]{:S(2)}) async-start(bf16[4,4,32,256]{3,2,1,0:T(8,128)(2,1)} %copy.49), calls=%async_computation | async-start | bytes 524288 | tf_op jit(solution)/shard_map/leaf_forward/all_to_all | solution.py:26
  37.4 7.7 %collective-permute-start = (bf16[4,16,2048]{2,1,0:T(8,128)(2,1)S(1)}, bf16[4,16,2048]{2,1,0:T(8,128)(2,1)S(1)}, u32[]{:S(2)}, u32[]{:S(2)}) collective-permute-start(bf16[4,16,2048]{2,1,0:T(8,128)(2,1)S(1)} %pad_maximum_fusion), channel_id=1, source_target_pairs={{0,4},{4,0},{1,5},{5,1},{2,6},{6,2},{3,7},{7,3},{8,12},{12,8},{9,1... | collective-permute-start | bytes 786440 | tf_op jit(solution)/shard_map/contrib_sum/ppermute | solution.py:35
  40.1 10.0 %collective-permute-start.2 = (bf16[4,32,256]{2,1,0:T(8,128)(2,1)S(1)}, bf16[4,32,256]{2,1,0:T(8,128)(2,1)S(1)}, u32[]{:S(2)}, u32[]{:S(2)}) collective-permute-start(bf16[4,32,256]{2,1,0:T(8,128)(2,1)S(1)} %select_convert_fusion.1), channel_id=1, source_target_pairs={{2,0},{3,1},{0,2},{1,3},{6,4},{7,5},{4,6},{5,7},{10,8},{11,9},{8,1... | collective-permute-start | bytes 196616 | tf_op jit(solution)/shard_map/contrib_sum/ppermute | solution.py:41
  42.4 7.7 %collective-permute-start.3 = (bf16[4,32,256]{2,1,0:T(8,128)(2,1)S(1)}, bf16[4,32,256]{2,1,0:T(8,128)(2,1)S(1)}, u32[]{:S(2)}, u32[]{:S(2)}) collective-permute-start(bf16[4,32,256]{2,1,0:T(8,128)(2,1)S(1)} %select_convert_fusion.1), channel_id=1, source_target_pairs={{3,0},{0,1},{1,2},{2,3},{7,4},{4,5},{5,6},{6,7},{11,8},{8,9},{9,10... | collective-permute-start | bytes 196616 | tf_op jit(solution)/shard_map/contrib_sum/ppermute | solution.py:41
  42.7 7.4 %collective-permute-start.1 = (bf16[4,32,256]{2,1,0:T(8,128)(2,1)S(1)}, bf16[4,32,256]{2,1,0:T(8,128)(2,1)S(1)}, u32[]{:S(2)}, u32[]{:S(2)}) collective-permute-start(bf16[4,32,256]{2,1,0:T(8,128)(2,1)S(1)} %select_convert_fusion.1), channel_id=1, source_target_pairs={{1,0},{2,1},{3,2},{0,3},{5,4},{6,5},{7,6},{4,7},{9,8},{10,9},{11,1... | collective-permute-start | bytes 196616 | tf_op jit(solution)/shard_map/contrib_sum/ppermute | solution.py:41
  46.5 11.4 %all-to-all-start.1 = ((bf16[16,16,512]{2,1,0:T(8,128)(2,1)}), bf16[16,16,512]{2,1,0:T(8,128)(2,1)S(1)}, u32[]{:S(2)}, u32[]{:S(2)}) async-start(bf16[16,16,512]{2,1,0:T(8,128)(2,1)} %reshape.170), calls=%async_computation.1 | async-start | bytes 524288 | tf_op jit(solution)/shard_map/contrib_sum/all_to_all | solution.py:26
  50.0 83.2 %all-gather.7.cloned.1.call-start = ((), (), s32[]{:S(2)}) async-start(), calls=%async_computation.7 | async-start | bytes 5242880 | tf_op jit(solution)/shard_map/contrib_sum/all_gather | solution.py:302
  74.8 10.6 %collective-permute-start.7 = (bf16[8,104,2048]{2,1,0:T(8,128)(2,1)}, bf16[8,104,2048]{2,1,0:T(8,128)(2,1)}, u32[]{:S(2)}, u32[]{:S(2)}) collective-permute-start(bf16[8,104,2048]{2,1,0:T(8,128)(2,1)} %bitcast.84), channel_id=1, source_target_pairs={{0,4},{4,0},{1,5},{5,1},{2,6},{6,2},{3,7},{7,3},{8,12},{12,8},{9,1... | collective-permute-start | bytes 10223624 | tf_op jit(solution)/shard_map/gather/ppermute | solution.py:35
  84.9 8.0 %collective-permute-start.8 = (bf16[2048,512]{1,0:T(8,128)(2,1)}, bf16[2048,512]{1,0:T(8,128)(2,1)}, u32[]{:S(2)}, u32[]{:S(2)}) collective-permute-start(bf16[2048,512]{1,0:T(8,128)(2,1)} %root_select.1.r0_ref), channel_id=1, source_target_pairs={{0,4},{4,0},{1,5},{5,1},{2,6},{6,2},{3,7},{7,3},{8,12},{12,8},{9,1... | collective-permute-start | bytes 6291464 | tf_op jit(solution)/shard_map/gather/ppermute | solution.py:35
  84.9 11.5 %collective-permute-start.10 = (bf16[32,512]{1,0:T(8,128)(2,1)}, bf16[32,512]{1,0:T(8,128)(2,1)}, u32[]{:S(2)}, u32[]{:S(2)}) collective-permute-start(bf16[32,512]{1,0:T(8,128)(2,1)} %get-tuple-element.32.w0_ref), channel_id=1, source_target_pairs={{0,4},{4,0},{1,5},{5,1},{2,6},{6,2},{3,7},{7,3},{8,12},{12,8},{9,1... | collective-permute-start | bytes 98312 | tf_op jit(solution)/shard_map/gather/ppermute | solution.py:35
  88.6 20.6 %copy-start.3 = (bf16[16,2048]{1,0:T(8,128)(2,1)}, bf16[16,2048]{1,0:T(8,128)(2,1)S(1)}, u32[]{:S(2)}) copy-start(bf16[16,2048]{1,0:T(8,128)(2,1)S(1)} %get-tuple-element.35.y0) | copy-start | bytes 196612
  88.6 15.7 %all-to-all-start.3 = ((bf16[16,16,512]{2,1,0:T(8,128)(2,1)}), bf16[16,16,512]{2,1,0:T(8,128)(2,1)}, u32[]{:S(2)}, u32[]{:S(2)}) async-start(bf16[16,16,512]{2,1,0:T(8,128)(2,1)} %copy-done.2), calls=%async_computation.3 | async-start | bytes 524288 | tf_op jit(solution)/shard_map/mid_forward/all_to_all | solution.py:26
  93.0 2.8 %collective-permute-start.9 = (bf16[16,512]{1,0:T(8,128)(2,1)S(1)}, bf16[16,512]{1,0:T(8,128)(2,1)S(1)}, u32[]{:S(2)}, u32[]{:S(2)}) collective-permute-start(bf16[16,512]{1,0:T(8,128)(2,1)S(1)} %select_convert_fusion.2), channel_id=1, source_target_pairs={{0,4},{4,0},{1,5},{5,1},{2,6},{6,2},{3,7},{7,3},{8,12},{12,8},{9,1... | collective-permute-start | bytes 49160 | tf_op jit(solution)/shard_map/mid_forward/ppermute | solution.py:35
  108.4 13.7 %collective-permute-start.11 = (bf16[16,2048]{1,0:T(8,128)(2,1)S(1)}, bf16[16,2048]{1,0:T(8,128)(2,1)S(1)}, u32[]{:S(2)}, u32[]{:S(2)}) collective-permute-start(bf16[16,2048]{1,0:T(8,128)(2,1)S(1)} %get-tuple-element.35.y0), channel_id=1, source_target_pairs={{64,0},{128,64},{192,128},{0,192},{65,1},{129,65},{193,129},{1,193... | collective-permute-start | bytes 196616 | tf_op jit(solution)/shard_map/root/ppermute | solution.py:41
  109.0 13.1 %collective-permute-start.12 = (bf16[16,2048]{1,0:T(8,128)(2,1)S(1)}, bf16[16,2048]{1,0:T(8,128)(2,1)S(1)}, u32[]{:S(2)}, u32[]{:S(2)}) collective-permute-start(bf16[16,2048]{1,0:T(8,128)(2,1)S(1)} %get-tuple-element.35.y0), channel_id=1, source_target_pairs={{128,0},{192,64},{0,128},{64,192},{129,1},{193,65},{1,129},{65,193... | collective-permute-start | bytes 196616 | tf_op jit(solution)/shard_map/root/ppermute | solution.py:41
  109.3 12.9 %collective-permute-start.13 = (bf16[16,2048]{1,0:T(8,128)(2,1)S(1)}, bf16[16,2048]{1,0:T(8,128)(2,1)S(1)}, u32[]{:S(2)}, u32[]{:S(2)}) collective-permute-start(bf16[16,2048]{1,0:T(8,128)(2,1)S(1)} %get-tuple-element.35.y0), channel_id=1, source_target_pairs={{192,0},{0,64},{64,128},{128,192},{193,1},{1,65},{65,129},{129,193... | collective-permute-start | bytes 196616 | tf_op jit(solution)/shard_map/root/ppermute | solution.py:41
  109.9 8.7 %all-to-all-start.4 = ((bf16[4,16,640]{2,1,0:T(8,128)(2,1)}), bf16[4,16,640]{2,1,0:T(8,128)(2,1)S(1)}, u32[]{:S(2)}, u32[]{:S(2)}) async-start(bf16[4,16,640]{2,1,0:T(8,128)(2,1)} %get-tuple-element.33), calls=%async_computation.4 | async-start | bytes 163840 | tf_op jit(solution)/shard_map/root/all_to_all | solution.py:26
  118.7 24.9 %collective-permute-start.15 = (f32[16,32]{1,0:T(8,128)S(1)}, f32[16,32]{1,0:T(8,128)S(1)}, u32[]{:S(2)}, u32[]{:S(2)}) collective-permute-start(f32[16,32]{1,0:T(8,128)S(1)} %slice.43), channel_id=1, source_target_pairs={{0,4},{4,0},{1,5},{5,1},{2,6},{6,2},{3,7},{7,3},{8,12},{12,8},{9,1... | collective-permute-start | bytes 6152 | tf_op jit(solution)/shard_map/outputs/ppermute | solution.py:35
  127.7 14.1 %all-to-all-start.5 = ((bf16[16,16,512]{2,1,0:T(8,128)(2,1)}), bf16[16,16,512]{2,1,0:T(8,128)(2,1)S(1)}, u32[]{:S(2)}, u32[]{:S(2)}) async-start(bf16[16,16,512]{2,1,0:T(8,128)(2,1)} %mid_backward.1), calls=%async_computation.5 | async-start | bytes 524288 | tf_op jit(solution)/shard_map/mid_backward/all_to_all | solution.py:26
  142.3 2.4 %collective-permute-start.14 = (bf16[4,16,2048]{2,1,0:T(8,128)(2,1)S(1)}, bf16[4,16,2048]{2,1,0:T(8,128)(2,1)S(1)}, u32[]{:S(2)}, u32[]{:S(2)}) collective-permute-start(bf16[4,16,2048]{2,1,0:T(8,128)(2,1)S(1)} %reshape.176.x0_ref), channel_id=1, source_target_pairs={{0,4},{4,0},{1,5},{5,1},{2,6},{6,2},{3,7},{7,3},{8,12},{12,8},{9,1... | collective-permute-start | bytes 786440 | tf_op jit(solution)/shard_map/mid_backward/ppermute | solution.py:35
  (21 other events, 151.2 us)
Sparse Core Ops, SparseCore 0:
  23.3 49.2 all-gather.4
  74.4 54.9 all-gather.6
